TPU v7x, 32 devices: a whole 2x2x4 slice. The times are simulated.
32 devices in a mesh: fsdp: 8 (over z, y), seq: 4 (over x, core).
Axes of the slice: x: 2, y: 2, z: 4, core: 2. Of those that a mesh axis runs over, the one named last changes fastest.
Arguments:
- frames_in: bfloat16 [16, 1536, 1280], P('fsdp', 'seq'), may hold values from -6 to 6
- teacher: bfloat16 [16, 1536, 1280], P('fsdp', 'seq'), may hold values from -6 to 6
- lengths: int32 [16], replicated, may hold values from 384 to 1536, as said below
- norm1_gain: bfloat16 [1280], P('fsdp'), may hold values from 0.25 to 1.75
- norm1_bias: bfloat16 [1280], P('fsdp'), may hold values from -1.75 to 1.75
- w_qkv: bfloat16 [1280, 3840], P('fsdp'), may hold values from -0.15625 to 0.15625
- query_bias: bfloat16 [1280], P('fsdp'), may hold values from -1.75 to 1.75
- value_bias: bfloat16 [1280], P('fsdp'), may hold values from -1.75 to 1.75
- w_attn_out: bfloat16 [1280, 1280], P('fsdp'), may hold values from -0.875 to 0.875
- attn_out_bias: bfloat16 [1280], P('fsdp'), may hold values from -1.75 to 1.75
- norm2_gain: bfloat16 [1280], P('fsdp'), may hold values from 0.25 to 1.75
- norm2_bias: bfloat16 [1280], P('fsdp'), may hold values from -1.75 to 1.75
- w_up: bfloat16 [1280, 5120], P('fsdp'), may hold values from -0.15625 to 0.15625
- up_bias: bfloat16 [5120], P('fsdp'), may hold values from -1.75 to 1.75
- w_down: bfloat16 [5120, 1280], P('fsdp'), may hold values from -0.125 to 0.125
- down_bias: bfloat16 [1280], P('fsdp'), may hold values from -1.75 to 1.75
Outputs:
- frames_out: bfloat16 [16, 1536, 1280], P('fsdp', 'seq')
- clip_loss: float32 [16], P('fsdp')
- grad_in: float32 [16, 1536, 1280], P('fsdp', 'seq')
- grad_norm1_gain: float32 [1280], P('fsdp')
- grad_norm1_bias: float32 [1280], P('fsdp')
- grad_w_qkv: float32 [1280, 3840], P('fsdp')
- grad_query_bias: float32 [1280], P('fsdp')
- grad_value_bias: float32 [1280], P('fsdp')
- grad_w_attn_out: float32 [1280, 1280], P('fsdp')
- grad_attn_out_bias: float32 [1280], P('fsdp')
- grad_norm2_gain: float32 [1280], P('fsdp')
- grad_norm2_bias: float32 [1280], P('fsdp')
- grad_w_up: float32 [1280, 5120], P('fsdp')
- grad_up_bias: float32 [5120], P('fsdp')
- grad_w_down: float32 [5120, 1280], P('fsdp')
- grad_down_bias: float32 [1280], P('fsdp')
Inputs may be any that keep to these rules, and one draw needn't show every extreme that they name: `lengths`: a clip's valid frames are its first ones; in every draw some clip has all 1536 frames valid.
All inputs are finite; a program needn't handle non-finite values.
Results may differ from a plain program's by a relative error of at most 0.0095.
Values may be sent and summed in bfloat16 or wider, within the bound.
A program may use at most 256 MiB of HBM per device.

v0:
```python
import functools
import math

import jax
import jax.numpy as jnp
from jax import lax
from jax.sharding import PartitionSpec as P

HEADS = 16


def layer_norm(v, gain, bias):
    mean = jnp.mean(v, axis=-1, keepdims=True)
    cent = v - mean
    var = jnp.mean(cent * cent, axis=-1, keepdims=True)
    return cent * lax.rsqrt(var + 1e-05) * gain + bias


def local(
    frames_in,
    teacher,
    lengths,
    norm1_gain,
    norm1_bias,
    w_qkv,
    query_bias,
    value_bias,
    w_attn_out,
    attn_out_bias,
    norm2_gain,
    norm2_bias,
    w_up,
    up_bias,
    w_down,
    down_bias,
):
    single = jnp.float32
    half = jnp.bfloat16
    gain1, bias1, wqkv, qbias, vbias, wout, obias, gain2, bias2, wup, ubias, wdown, dbias = (
        lax.all_gather(norm1_gain, "fsdp", axis=0, tiled=True),
        lax.all_gather(norm1_bias, "fsdp", axis=0, tiled=True),
        lax.all_gather(w_qkv, "fsdp", axis=0, tiled=True),
        lax.all_gather(query_bias, "fsdp", axis=0, tiled=True),
        lax.all_gather(value_bias, "fsdp", axis=0, tiled=True),
        lax.all_gather(w_attn_out, "fsdp", axis=0, tiled=True),
        lax.all_gather(attn_out_bias, "fsdp", axis=0, tiled=True),
        lax.all_gather(norm2_gain, "fsdp", axis=0, tiled=True),
        lax.all_gather(norm2_bias, "fsdp", axis=0, tiled=True),
        lax.all_gather(w_up, "fsdp", axis=0, tiled=True),
        lax.all_gather(up_bias, "fsdp", axis=0, tiled=True),
        lax.all_gather(w_down, "fsdp", axis=0, tiled=True),
        lax.all_gather(down_bias, "fsdp", axis=0, tiled=True),
    )
    clips, frames, width = frames_in.shape
    groups = lax.axis_size("seq")
    seq_len = frames * groups
    head_dim = width // HEADS
    local_heads = HEADS // groups
    span = local_heads * head_dim
    rows = clips * frames
    block = min(512, seq_len)
    nblocks = seq_len // block
    scale = 1.0 / math.sqrt(head_dim)
    mine = lax.dynamic_slice_in_dim(lengths, lax.axis_index("fsdp") * clips, clips)
    place = lax.axis_index("seq") * frames + jnp.arange(frames, dtype=jnp.int32)
    row_valid = (place[None, :] < mine[:, None]).astype(single)
    key_valid = jnp.arange(seq_len, dtype=jnp.int32)[None, :] < mine[:, None]
    state = frames_in.astype(single).reshape(rows, width)
    hidden1, norm1_back = jax.vjp(layer_norm, state, gain1.astype(single), bias1.astype(single))
    hidden1 = hidden1.astype(half)
    qkv = jnp.dot(hidden1, wqkv, preferred_element_type=single)
    query = (qkv[:, :width] + qbias.astype(single)).astype(half)
    keyed = qkv[:, width : 2 * width].astype(half)
    valued = (qkv[:, 2 * width :] + vbias.astype(single)).astype(half)

    def to_groups(tensor):
        return tensor.reshape(clips, frames, groups, span)

    query_h, keyed_h, valued_h = (
        lax.all_to_all(to_groups(query), "seq", split_axis=2, concat_axis=1, tiled=True),
        lax.all_to_all(to_groups(keyed), "seq", split_axis=2, concat_axis=1, tiled=True),
        lax.all_to_all(to_groups(valued), "seq", split_axis=2, concat_axis=1, tiled=True),
    )
    query_h = query_h.reshape(clips, seq_len, local_heads, head_dim)
    keyed_h = keyed_h.reshape(clips, seq_len, local_heads, head_dim)
    valued_h = valued_h.reshape(clips, seq_len, local_heads, head_dim)

    def scores_of(query_block, keys, valid):
        scores = (
            jnp.einsum("qhd,khd->hqk", query_block, keys, preferred_element_type=single) * scale
        )
        return jnp.where(valid[None, None, :], scores, -1e30)

    def attend(item):
        queries, keys, values, valid = item
        blocks = queries.reshape(nblocks, block, local_heads, head_dim)

        def one_block(query_block):
            scores = scores_of(query_block, keys, valid)
            top = jnp.max(scores, axis=-1, keepdims=True)
            expo = jnp.exp(scores - top)
            total = jnp.sum(expo, axis=-1, keepdims=True)
            probs = (expo / total).astype(half)
            context = jnp.einsum("hqk,khd->qhd", probs, values, preferred_element_type=single)
            return (context.astype(half), (top + jnp.log(total))[..., 0])

        context, logsum = lax.map(one_block, blocks)
        return (context.reshape(seq_len, span), logsum)

    context_h, logsum = lax.map(attend, (query_h, keyed_h, valued_h, key_valid))
    context = lax.all_to_all(
        context_h.reshape(clips, seq_len, 1, span), "seq", split_axis=1, concat_axis=2, tiled=True
    ).reshape(rows, width)
    attn = jnp.dot(context, wout, preferred_element_type=single) + obias.astype(single)
    middle = state + attn
    hidden2, norm2_back = jax.vjp(layer_norm, middle, gain2.astype(single), bias2.astype(single))
    hidden2 = hidden2.astype(half)
    upper = jnp.dot(hidden2, wup, preferred_element_type=single) + ubias.astype(single)
    active, gelu_back = jax.vjp(functools.partial(jax.nn.gelu, approximate=False), upper)
    active = active.astype(half)
    result = middle + jnp.dot(active, wdown, preferred_element_type=single) + dbias.astype(single)
    frames_out = result.astype(half).reshape(clips, frames, width)
    count = jnp.sum(lengths).astype(single)
    diff = (result - teacher.astype(single).reshape(rows, width)).reshape(clips, frames, width)
    masked = diff * row_valid[:, :, None]
    part_loss = jnp.sum(masked * diff, axis=(1, 2)) / (2.0 * width * count)
    grad_out = (masked * (float(lengths.shape[0] * seq_len) / count)).reshape(rows, width)
    wqkv_b, wout_b, wup_b, wdown_b = (
        lax.all_gather(w_qkv, "fsdp", axis=0, tiled=True),
        lax.all_gather(w_attn_out, "fsdp", axis=0, tiled=True),
        lax.all_gather(w_up, "fsdp", axis=0, tiled=True),
        lax.all_gather(w_down, "fsdp", axis=0, tiled=True),
    )
    grad_branch2 = grad_out.astype(half)
    grad_wdown = jnp.dot(active.T, grad_branch2, preferred_element_type=single)
    grad_dbias = jnp.sum(grad_branch2.astype(single), axis=0)
    grad_active = jnp.dot(grad_branch2, wdown_b.T, preferred_element_type=single)
    (grad_upper,) = gelu_back(grad_active)
    grad_upper = grad_upper.astype(half)
    grad_wup = jnp.dot(hidden2.T, grad_upper, preferred_element_type=single)
    grad_ubias = jnp.sum(grad_upper.astype(single), axis=0)
    grad_hidden2 = jnp.dot(grad_upper, wup_b.T, preferred_element_type=single)
    grad_middle_norm, grad_gain2, grad_bias2 = norm2_back(grad_hidden2)
    grad_middle = grad_out + grad_middle_norm
    grad_branch1 = grad_middle.astype(half)
    grad_wout = jnp.dot(context.T, grad_branch1, preferred_element_type=single)
    grad_obias = jnp.sum(grad_branch1.astype(single), axis=0)
    grad_context = jnp.dot(grad_branch1, wout_b.T, preferred_element_type=single).astype(half)
    grad_context_h = lax.all_to_all(
        grad_context.reshape(clips, frames, groups, span),
        "seq",
        split_axis=2,
        concat_axis=1,
        tiled=True,
    )
    grad_context_h = grad_context_h.reshape(clips, seq_len, local_heads, head_dim)

    def attend_back(item):
        queries, keys, values, grads, sums, valid = item
        query_blocks = queries.reshape(nblocks, block, local_heads, head_dim)
        grad_blocks = grads.reshape(nblocks, block, local_heads, head_dim)

        def one_block(carry, piece):
            query_block, grad_block, sum_block = piece
            scores = scores_of(query_block, keys, valid)
            probs = jnp.exp(scores - sum_block[..., None])
            grad_probs = jnp.einsum(
                "qhd,khd->hqk", grad_block, values, preferred_element_type=single
            )
            inner = jnp.sum(probs * grad_probs, axis=-1, keepdims=True)
            grad_scores = (probs * (grad_probs - inner)).astype(half)
            grad_query = (
                jnp.einsum("hqk,khd->qhd", grad_scores, keys, preferred_element_type=single) * scale
            )
            grad_keys = (
                carry[0]
                + jnp.einsum(
                    "hqk,qhd->khd", grad_scores, query_block, preferred_element_type=single
                )
                * scale
            )
            grad_values = carry[1] + jnp.einsum(
                "hqk,qhd->khd", probs.astype(half), grad_block, preferred_element_type=single
            )
            return ((grad_keys, grad_values), grad_query.astype(half))

        empty = jnp.zeros((seq_len, local_heads, head_dim), single)
        (grad_keys, grad_values), grad_queries = lax.scan(
            one_block, (empty, empty), (query_blocks, grad_blocks, sums)
        )
        return (
            grad_queries.reshape(seq_len, 1, span),
            grad_keys.astype(half).reshape(seq_len, 1, span),
            grad_values.astype(half).reshape(seq_len, 1, span),
        )

    grad_query_h, grad_keyed_h, grad_valued_h = lax.map(
        attend_back, (query_h, keyed_h, valued_h, grad_context_h, logsum, key_valid)
    )
    grad_query, grad_keyed, grad_valued = (
        lax.all_to_all(grad_query_h, "seq", split_axis=1, concat_axis=2, tiled=True),
        lax.all_to_all(grad_keyed_h, "seq", split_axis=1, concat_axis=2, tiled=True),
        lax.all_to_all(grad_valued_h, "seq", split_axis=1, concat_axis=2, tiled=True),
    )
    grad_query = grad_query.reshape(rows, width)
    grad_keyed = grad_keyed.reshape(rows, width)
    grad_valued = grad_valued.reshape(rows, width)
    grad_qkv = jnp.concatenate([grad_query, grad_keyed, grad_valued], axis=1)
    grad_wqkv = jnp.dot(hidden1.T, grad_qkv, preferred_element_type=single)
    grad_qbias = jnp.sum(grad_query.astype(single), axis=0)
    grad_vbias = jnp.sum(grad_valued.astype(single), axis=0)
    grad_hidden1 = jnp.dot(grad_qkv, wqkv_b.T, preferred_element_type=single)
    grad_state_norm, grad_gain1, grad_bias1 = norm1_back(grad_hidden1)
    grad_in = (grad_middle + grad_state_norm).reshape(clips, frames, width)
    gradients = (
        grad_gain1,
        grad_bias1,
        grad_wqkv,
        grad_qbias,
        grad_vbias,
        grad_wout,
        grad_obias,
        grad_gain2,
        grad_bias2,
        grad_wup,
        grad_ubias,
        grad_wdown,
        grad_dbias,
    )
    owned = (
        lax.psum_scatter(
            gradients[0].astype(jnp.bfloat16), "fsdp", scatter_dimension=0, tiled=True
        ).astype(jnp.float32),
        lax.psum_scatter(
            gradients[1].astype(jnp.bfloat16), "fsdp", scatter_dimension=0, tiled=True
        ).astype(jnp.float32),
        lax.psum_scatter(
            gradients[2].astype(jnp.bfloat16), "fsdp", scatter_dimension=0, tiled=True
        ).astype(jnp.float32),
        lax.psum_scatter(
            gradients[3].astype(jnp.bfloat16), "fsdp", scatter_dimension=0, tiled=True
        ).astype(jnp.float32),
        lax.psum_scatter(
            gradients[4].astype(jnp.bfloat16), "fsdp", scatter_dimension=0, tiled=True
        ).astype(jnp.float32),
        lax.psum_scatter(
            gradients[5].astype(jnp.bfloat16), "fsdp", scatter_dimension=0, tiled=True
        ).astype(jnp.float32),
        lax.psum_scatter(
            gradients[6].astype(jnp.bfloat16), "fsdp", scatter_dimension=0, tiled=True
        ).astype(jnp.float32),
        lax.psum_scatter(
            gradients[7].astype(jnp.bfloat16), "fsdp", scatter_dimension=0, tiled=True
        ).astype(jnp.float32),
        lax.psum_scatter(
            gradients[8].astype(jnp.bfloat16), "fsdp", scatter_dimension=0, tiled=True
        ).astype(jnp.float32),
        lax.psum_scatter(
            gradients[9].astype(jnp.bfloat16), "fsdp", scatter_dimension=0, tiled=True
        ).astype(jnp.float32),
        lax.psum_scatter(
            gradients[10].astype(jnp.bfloat16), "fsdp", scatter_dimension=0, tiled=True
        ).astype(jnp.float32),
        lax.psum_scatter(
            gradients[11].astype(jnp.bfloat16), "fsdp", scatter_dimension=0, tiled=True
        ).astype(jnp.float32),
        lax.psum_scatter(
            gradients[12].astype(jnp.bfloat16), "fsdp", scatter_dimension=0, tiled=True
        ).astype(jnp.float32),
    )
    reduced = (
        lax.psum(owned[0].astype(jnp.bfloat16), "seq").astype(jnp.float32),
        lax.psum(owned[1].astype(jnp.bfloat16), "seq").astype(jnp.float32),
        lax.psum(owned[2].astype(jnp.bfloat16), "seq").astype(jnp.float32),
        lax.psum(owned[3].astype(jnp.bfloat16), "seq").astype(jnp.float32),
        lax.psum(owned[4].astype(jnp.bfloat16), "seq").astype(jnp.float32),
        lax.psum(owned[5].astype(jnp.bfloat16), "seq").astype(jnp.float32),
        lax.psum(owned[6].astype(jnp.bfloat16), "seq").astype(jnp.float32),
        lax.psum(owned[7].astype(jnp.bfloat16), "seq").astype(jnp.float32),
        lax.psum(owned[8].astype(jnp.bfloat16), "seq").astype(jnp.float32),
        lax.psum(owned[9].astype(jnp.bfloat16), "seq").astype(jnp.float32),
        lax.psum(owned[10].astype(jnp.bfloat16), "seq").astype(jnp.float32),
        lax.psum(owned[11].astype(jnp.bfloat16), "seq").astype(jnp.float32),
        lax.psum(owned[12].astype(jnp.bfloat16), "seq").astype(jnp.float32),
        lax.psum(part_loss.astype(jnp.bfloat16), "seq").astype(jnp.float32),
    )
    summed = tuple(reduced[:13])
    clip_loss = reduced[13]
    return (
        frames_out,
        clip_loss,
        grad_in,
        summed[0],
        summed[1],
        summed[2],
        summed[3],
        summed[4],
        summed[5],
        summed[6],
        summed[7],
        summed[8],
        summed[9],
        summed[10],
        summed[11],
        summed[12],
    )


def solution(mesh):
    placed = (
        P("fsdp", "seq", None),
        P("fsdp", "seq", None),
        P(),
        P("fsdp"),
        P("fsdp"),
        P("fsdp", None),
        P("fsdp"),
        P("fsdp"),
        P("fsdp", None),
        P("fsdp"),
        P("fsdp"),
        P("fsdp"),
        P("fsdp", None),
        P("fsdp"),
        P("fsdp", None),
        P("fsdp"),
    )
    return jax.shard_map(
        local,
        mesh=mesh,
        in_specs=placed,
        out_specs=(
            P("fsdp", "seq", None),
            P("fsdp"),
            P("fsdp", "seq", None),
            P("fsdp"),
            P("fsdp"),
            P("fsdp", None),
            P("fsdp"),
            P("fsdp"),
            P("fsdp", None),
            P("fsdp"),
            P("fsdp"),
            P("fsdp"),
            P("fsdp", None),
            P("fsdp"),
            P("fsdp", None),
            P("fsdp"),
        ),
        check_vma=False,
    )
```

profile of v0, /device:TPU:0, one launch (start us, length us, event | category | flops | bytes accessed | tf_op | source)
XLA Modules:
  0.0 1777.0 jit_solution(1138143871130389060)
XLA Ops:
  18.2 41.9 %all-reduce.18 = (bf16[1280]{0:T(1024)(128)(2,1)S(1)}, bf16[1280]{0:T(1024)(128)(2,1)S(1)}, bf16[1280]{0:T(1024)(128)(2,1)S(1)}, bf16[1280]{0:T(1024)(128)(2,1)S...) all-reduce(bf16[1280]{0:T(1024)(128)(2,1)S(1)} %dynamic-update-slic, ...), channel_id=1, replica_groups=mesh['fsdp'=8,'seq'=4] {'fsdp'}, use_global_device_ids=true, to_apply=%add.1 | all-reduce | flops 10240 | bytes 40960
  63.8 92.2 %all-gather.6.cloned.1.call-done = bf16[1280,3840]{1,0:T(8,128)(2,1)} async-done(((bf16[160,3840]{1,0:T(8,128)(2,1)}), bf16[1280,3840]{1,0:T(8,128)(2,1)}) %all-gather.6.cloned.1.call-update) | async-done | bytes 9830416 | tf_op jit(solution)/shard_map/all_gather | solution.py:42
  156.0 10.7 fusion.73
  194.7 15.3 all-to-all-done
  226.9 11.8 all-to-all-done.2
  260.4 6.1 all-to-all-done.1
  273.6 70.0 %while.54 = (s32[]{:T(128)}, bf16[2,1536,320]{1,2,0:T(8,128)(2,1)}, f32[2,3,4,512]{3,2,1,0:T(4,128)S(1)}, bf16[2,1536,4,80]{1,3,2,0:T(8,128)(2,1)}, bf16[2,1536,...) while((s32[]{:T(128)}, bf16[2,1536,320]{1,2,0:T(8,128)(2,1)}, ...), condition=%wide.region_7.8_spmd, body=%wide.region_2.7_spmd.sunk | while | flops 1044543488 | bytes 64087352 | solution.py:110
  277.6 27.9 %while.57 = (s32[]{:T(128)}, bf16[3,512,4,80]{1,3,2,0:T(8,128)(2,1)S(1)}, f32[3,4,512]{2,1,0:T(4,128)S(1)}, pred[1536]{0:T(1024)(128)(4,1)S(1)}, bf16[3,512,4,80...) while((s32[]{:T(128)}, ...), condition=%wide.region_6.6_spmd, body=%wide.region_3.5_spmd.sunk | while | flops 1044543488 | bytes 40441440 | solution.py:107
  312.5 27.8 %while.57 = (s32[]{:T(128)}, bf16[3,512,4,80]{1,3,2,0:T(8,128)(2,1)S(1)}, f32[3,4,512]{2,1,0:T(4,128)S(1)}, pred[1536]{0:T(1024)(128)(4,1)S(1)}, bf16[3,512,4,80...) while((s32[]{:T(128)}, ...), condition=%wide.region_6.6_spmd, body=%wide.region_3.5_spmd.sunk | while | flops 1044543488 | bytes 40441440 | solution.py:107
  343.7 6.8 copy.181
  354.8 31.4 %all-gather = bf16[8,1,640]{2,1,0:T(2,128)(2,1)S(1)} all-gather(bf16[1,1,640]{2,1,0:T(2,128)(2,1)S(1)} %reshape.315), channel_id=1, replica_groups=mesh['fsdp'=8,'seq'=4] {'fsdp'}, dimensions={0}, use_global_device_ids=true | all-gather | bytes 11520 | tf_op jit(solution)/shard_map/all_gather | solution.py:50
  388.5 8.7 copy.182
  408.8 51.7 %multiply_convert_fusion.1 = (bf16[768,5120]{1,0:T(8,128)(2,1)}, f32[768,5120]{1,0:T(8,128)}, f32[768,5120]{1,0:T(8,128)}) fusion(f32[5120]{0:T(1024)S(1)} %bitcast.260, bf16[1280,5120]{1,0:T(8,128)(2,1)} %all-gather.10.cloned.1.call-done, f32[768,1280]{1,0:T(8,128)} %copy-done.6, f32[1280]{0:T(1024)S(1)} %convert_element_type.214, ...), kind=kOutput, calls=%fused_computation.64 | convolution fusion | flops 10330767360 | bytes 56397824 | tf_op jit(solution)/shard_map/dot_general | solution.py:118
  460.5 123.9 %all-gather.12.cloned.1.call-done = bf16[5120,1280]{1,0:T(8,128)(2,1)} async-done(((bf16[640,1280]{1,0:T(8,128)(2,1)}), bf16[5120,1280]{1,0:T(8,128)(2,1)}) %all-gather.12.cloned.1.call-update) | async-done | bytes 13107216 | tf_op jit(solution)/shard_map/all_gather | solution.py:51
  584.3 18.9 %fusion.45 = (f32[768]{0:T(1024)}, bf16[768,1280]{1,0:T(8,128)(2,1)}, f32[768,1280]{1,0:T(8,128)S(1)}) fusion(f32[768]{0:T(1024)S(1)} %compare_convert_fusion, bf16[2,384,1280]{2,1,0:T(8,128)(2,1)S(1)} %copy-done.16, f32[1280]{0:T(1024)S(1)} %convert_element_type.218, f32[768,1280]{1,0:T(8,128)} %copy-done.6, bf16[768,5120]{1,0:T(8,128)(2,1)} %get-tuple-element.481, ...), kind=kOutput, calls=%fused_computation.86 | convolution fusion | flops 10074192896 | bytes 32779264 | tf_op jit(solution)/shard_map/dot_general | solution.py:121
  606.3 24.6 %fusion.68 = (bf16[5120]{0:T(1024)(128)(2,1)}, bf16[768,5120]{1,0:T(8,128)(2,1)}) fusion(f32[768,5120]{1,0:T(8,128)} %get-tuple-element.482, f32[768,5120]{1,0:T(8,128)} %get-tuple-element.501, f32[5120]{0:T(1024)S(1)} %bitcast.261, bf16[768,1280]{1,0:T(8,128)(2,1)} %get-tuple-element.474, bf16[5120,1280]{1,0:T(8,128)(2,1)} %all-gather.12.cloned.1.call-done), kind=kOutput, calls=%fused_computation.142 | convolution fusion | flops 10129239040 | bytes 54425600 | tf_op jit(solution)/shard_map/dot_general | solution.py:137
  630.9 19.5 %multiply_reduce_fusion.1 = (bf16[1280]{0:T(1024)(128)(2,1)}, f32[768]{0:T(1024)S(1)}, bf16[1280]{0:T(1024)(128)(2,1)}, f32[768,1280]{1,0:T(8,128)}) fusion(f32[768,1280]{1,0:T(8,128)} %copy-done.6, f32[768]{0:T(1024)S(1)} %fusion.60, f32[768]{0:T(1024)S(1)} %broadcast_multiply_fusion, f32[1280]{0:T(1024)S(1)} %convert_element_type.213, ...), kind=kOutput, calls=%fused_computation.108 | convolution fusion | flops 10074190848 | bytes 28855296 | tf_op jit(solution)/shard_map/dot_general | solution.py:142
  674.4 24.2 %all-to-all-done.4 = bf16[2,384,4,320]{1,0,3,2:T(2,128)(2,1)S(1)} async-done(((bf16[2,384,4,320]{1,0,3,2:T(2,128)(2,1)}), bf16[2,384,4,320]{1,0,3,2:T(2,128)(2,1)S(1)}, u32[]{:S(2)}, u32[]{:S(2)}) %all-to-all-start.4) | async-done | bytes 1966112 | tf_op jit(solution)/shard_map/all_to_all | solution.py:149
  705.6 227.1 %while.56 = (s32[]{:T(128)}, bf16[2,1536,1,320]{1,3,2,0:T(8,128)(2,1)}, bf16[2,1536,1,320]{1,3,2,0:T(8,128)(2,1)}, bf16[2,1536,1,320]{1,3,2,0:T(8,128)(2,1)}, bf...) while((s32[]{:T(128)}, ...), condition=%wide.region_20.21_spmd, body=%wide.region_16.20_spmd.sunk | while | flops 2548660224 | bytes 254784048 | solution.py:197
  714.5 93.9 %while.58 = (s32[]{:T(128)}, f32[1536,4,80]{0,2,1:T(8,128)S(1)}, f32[1536,4,80]{0,2,1:T(8,128)}, bf16[3,512,4,80]{1,3,2,0:T(8,128)(2,1)}, bf16[3,512,4,80]{1,3,2...) while((s32[]{:T(128)}, f32[1536,4,80]{0,2,1:T(8,128)S(1)}, ...), condition=%wide.region_19.19_spmd.clone, body=%wide.region_17.18_spmd.clone.sunk | while | flops 2547677184 | bytes 207532240 | solution.py:188
  735.3 6.5 fusion.131
  766.1 6.5 fusion.131
  797.6 6.5 fusion.131
  828.0 93.9 %while.58 = (s32[]{:T(128)}, f32[1536,4,80]{0,2,1:T(8,128)S(1)}, f32[1536,4,80]{0,2,1:T(8,128)}, bf16[3,512,4,80]{1,3,2,0:T(8,128)(2,1)}, bf16[3,512,4,80]{1,3,2...) while((s32[]{:T(128)}, f32[1536,4,80]{0,2,1:T(8,128)S(1)}, ...), condition=%wide.region_19.19_spmd.clone, body=%wide.region_17.18_spmd.clone.sunk | while | flops 2547677184 | bytes 207532240 | solution.py:188
  848.8 6.5 fusion.131
  879.7 6.5 fusion.131
  911.2 6.5 fusion.131
  932.7 6.7 copy.185
  943.1 7.1 convolution_convert_fusion.3
  950.3 6.7 copy.188
  957.0 14.5 all-to-all-done.5
  976.0 6.8 copy.191
  982.8 21.7 %all-to-all-done.6 = bf16[2,1536,1,320]{3,0,2,1:T(2,128)(2,1)} async-done(((bf16[2,1536,1,320]{3,0,2,1:T(2,128)(2,1)}), bf16[2,1536,1,320]{3,0,2,1:T(2,128)(2,1)}, u32[]{:S(2)}, u32[]{:S(2)}) %all-to-all-start.6) | async-done | bytes 1966112 | tf_op jit(solution)/shard_map/all_to_all | solution.py:202
  1009.6 6.6 copy.200
  1019.9 6.6 copy.201
  1030.2 7.5 all-to-all-done.7
  1037.6 6.6 copy.202
  1050.7 10.1 convolution_convert_fusion.2
  1061.5 17.3 convolution_convert_fusion.1
  1080.3 16.3 convolution_convert_fusion
  1098.6 15.0 fusion.65
  1113.5 114.4 %reduce-scatter.5.cloned.1.call-done = bf16[160,3840]{1,0:T(8,128)(2,1)} async-done(((bf16[1280,3840]{1,0:T(8,128)(2,1)}), bf16[160,3840]{1,0:T(8,128)(2,1)}) %reduce-scatter.5.cloned.1.call-update) | async-done | bytes 1228816 | tf_op jit(solution)/shard_map/reduce_scatter | solution.py:237
  1227.9 217.4 %reduce-scatter.9.cloned.1.call-done = bf16[160,5120]{1,0:T(8,128)(2,1)} async-done(((bf16[1280,5120]{1,0:T(8,128)(2,1)}), bf16[160,5120]{1,0:T(8,128)(2,1)}) %reduce-scatter.9.cloned.1.call-update) | async-done | bytes 1638416 | tf_op jit(solution)/shard_map/reduce_scatter | solution.py:258
  1445.3 217.5 %reduce-scatter.11.cloned.1.call-done = bf16[640,1280]{1,0:T(8,128)(2,1)} async-done(((bf16[5120,1280]{1,0:T(8,128)(2,1)}), bf16[640,1280]{1,0:T(8,128)(2,1)}) %reduce-scatter.11.cloned.1.call-update) | async-done | bytes 1638416 | tf_op jit(solution)/shard_map/reduce_scatter | solution.py:264
  1671.7 35.7 %all-reduce.17 = (bf16[1280]{0:T(1024)(128)(2,1)S(1)}, bf16[1280]{0:T(1024)(128)(2,1)S(1)}, bf16[1280]{0:T(1024)(128)(2,1)S(1)}, bf16[1280]{0:T(1024)(128)(2,1)S...) all-reduce(bf16[1280]{0:T(1024)(128)(2,1)S(1)} %get-tuple-element.3, ...), channel_id=2, replica_groups=mesh['fsdp'=8,'seq'=4] {'fsdp'}, use_global_device_ids=true, to_apply=%region_24.25.clone | all-reduce | flops 15360 | bytes 61440
  1708.1 5.7 all-reduce.19
  1719.5 6.2 add_add_fusion.2
  1725.6 36.5 %all-reduce.23.cloned.1.call-done = (bf16[160,3840]{1,0:T(8,128)(2,1)}, bf16[160,1280]{1,0:T(8,128)(2,1)}, bf16[160,5120]{1,0:T(8,128)(2,1)}, bf16[640,1280]{1,0:T(8,128)(2,1)}) async-done(((bf16[160,3840]{1,0:T(8,128)(2,1)}, bf16[160,1280]{1,0:T(8,128)(2,1)}, bf16[160,5120]{1,0:T(8,128)(2,1)}, bf16[640,1280]{1,0:T(8,128)(2,1)}), (bf16[160,3840]{1,0:T(8,128)(2,1)}, bf16[160,1280]{1,0:T(8,128)(2,1)}, ...) | async-done | bytes 4915216 | tf_op jit(solution)/shard_map/psum | solution.py:274
  (430 shorter events, 448.6 us)
Async XLA Ops:
  7.2 52.9 %copy-start.2 = (bf16[2,384,1280]{2,1,0:T(8,128)(2,1)S(1)}, bf16[2,384,1280]{2,1,0:T(8,128)(2,1)}, u32[]{:S(2)}) copy-start(bf16[2,384,1280]{2,1,0:T(8,128)(2,1)} %param.24) | copy-start | bytes 5898244
  7.2 148.8 %all-gather.6.cloned.1.call-start = ((), (), s32[]{:S(2)}) async-start(), calls=%async_computation.12 | async-start | bytes 11059200 | tf_op jit(solution)/shard_map/all_gather | solution.py:42
  7.9 392.6 %all-gather.8.cloned.1.call-start = ((), (), s32[]{:S(2)}) async-start(), calls=%async_computation.13 | async-start | bytes 3686400 | tf_op jit(solution)/shard_map/all_gather | solution.py:45
  8.7 400.1 %all-gather.10.cloned.1.call-start = ((), (), s32[]{:S(2)}) async-start(), calls=%async_computation.14 | async-start | bytes 14745600 | tf_op jit(solution)/shard_map/all_gather | solution.py:49
  60.5 106.3 %copy-start.35 = (f32[768]{0:T(1024)}, f32[768]{0:T(1024)S(1)}, u32[]{:S(2)}) copy-start(f32[768]{0:T(1024)S(1)} %div.56) | copy-start | bytes 9220
  61.1 105.6 %copy-start.41 = (f32[768]{0:T(1024)}, f32[768]{0:T(1024)S(1)}, u32[]{:S(2)}) copy-start(f32[768]{0:T(1024)S(1)} %add.192) | copy-start | bytes 9220
  181.2 28.7 %all-to-all-start = ((bf16[2,384,4,320]{1,0,3,2:T(2,128)(2,1)}), bf16[2,384,4,320]{1,0,3,2:T(2,128)(2,1)}, u32[]{:S(2)}, u32[]{:S(2)}) async-start(bf16[2,384,4,320]{1,0,3,2:T(2,128)(2,1)} %copy.196), calls=%async_computation | async-start | bytes 3932160 | tf_op jit(solution)/shard_map/all_to_all | solution.py:80
  209.9 28.7 %all-to-all-start.2 = ((bf16[2,384,4,320]{1,0,3,2:T(2,128)(2,1)}), bf16[2,384,4,320]{1,0,3,2:T(2,128)(2,1)}, u32[]{:S(2)}, u32[]{:S(2)}) async-start(bf16[2,384,4,320]{1,0,3,2:T(2,128)(2,1)} %copy.198), calls=%async_computation.2 | async-start | bytes 3932160 | tf_op jit(solution)/shard_map/all_to_all | solution.py:82
  222.0 20.9 %copy-start.64 = (s32[16]{0:T(128)S(1)}, s32[16]{0:T(128)}, u32[]{:S(2)}) copy-start(s32[16]{0:T(128)} %param.26) | copy-start | bytes 196
  238.7 27.8 %all-to-all-start.1 = ((bf16[2,384,4,320]{1,0,3,2:T(2,128)(2,1)}), bf16[2,384,4,320]{1,0,3,2:T(2,128)(2,1)S(1)}, u32[]{:S(2)}, u32[]{:S(2)}) async-start(bf16[2,384,4,320]{1,0,3,2:T(2,128)(2,1)} %copy.197), calls=%async_computation.1 | async-start | bytes 3932160 | tf_op jit(solution)/shard_map/all_to_all | solution.py:81
  242.3 342.0 %all-gather.12.cloned.1.call-start = ((), (), s32[]{:S(2)}) async-start(), calls=%async_computation.15 | async-start | bytes 14745600 | tf_op jit(solution)/shard_map/all_gather | solution.py:51
  243.0 8.7 copy-start.62
  343.6 6.8 copy-start.27
  343.6 6.8 copy-start.32
  343.6 10.5 copy-start.65
  343.6 11.1 copy-start.57
  343.6 11.1 copy-start.56
  343.6 11.1 copy-start.55
  343.6 11.1 copy-start.61
  343.7 42.6 %copy-start.54 = (bf16[1280]{0:T(1024)(128)(2,1)S(1)}, bf16[1280]{0:T(1024)(128)(2,1)}, u32[]{:S(2)}) copy-start(bf16[1280]{0:T(1024)(128)(2,1)} %get-tuple-element.458) | copy-start | bytes 7684
  343.7 42.6 %copy-start.63 = (s32[2]{0:T(128)S(1)}, s32[2]{0:T(128)}, u32[]{:S(2)}) copy-start(s32[2]{0:T(128)} %copy-done.62) | copy-start | bytes 28
  350.4 36.7 %all-to-all-start.3 = ((bf16[2,1536,1,320]{3,0,2,1:T(2,128)(2,1)}), bf16[2,1536,1,320]{3,0,2,1:T(2,128)(2,1)S(1)}, u32[]{:S(2)}, u32[]{:S(2)}) async-start(bf16[2,1536,1,320]{3,0,2,1:T(2,128)(2,1)} %bitcast.245), calls=%async_computation.3 | async-start | bytes 4718592 | tf_op jit(solution)/shard_map/all_to_all | solution.py:111
  354.7 295.7 %copy-start.45 = (f32[1280]{0:T(1024)}, f32[1280]{0:T(1024)S(1)}, u32[]{:S(2)}) copy-start(f32[1280]{0:T(1024)S(1)} %convert_element_type.213) | copy-start | bytes 15364
  354.8 54.0 %copy-start.52 = (f32[1280]{0:T(1024)}, f32[1280]{0:T(1024)S(1)}, u32[]{:S(2)}) copy-start(f32[1280]{0:T(1024)S(1)} %convert_element_type.214) | copy-start | bytes 15364
  388.5 12.0 copy-start.3
  406.2 244.2 %copy-start.39 = (f32[768]{0:T(1024)}, f32[768]{0:T(1024)S(1)}, u32[]{:S(2)}) copy-start(f32[768]{0:T(1024)S(1)} %broadcast_multiply_fusion) | copy-start | bytes 9220
  408.7 51.8 %copy-start.43 = (f32[768]{0:T(1024)}, f32[768]{0:T(1024)S(1)}, u32[]{:S(2)}) copy-start(f32[768]{0:T(1024)S(1)} %multiply_reduce_fusion.3) | copy-start | bytes 9220
  408.7 241.7 %copy-start.47 = (f32[768]{0:T(1024)}, f32[768]{0:T(1024)S(1)}, u32[]{:S(2)}) copy-start(f32[768]{0:T(1024)S(1)} %fusion.60) | copy-start | bytes 9220
  408.7 175.6 %copy-start.16 = (bf16[2,384,1280]{2,1,0:T(8,128)(2,1)S(1)}, bf16[2,384,1280]{2,1,0:T(8,128)(2,1)}, u32[]{:S(2)}) copy-start(bf16[2,384,1280]{2,1,0:T(8,128)(2,1)} %param.25) | copy-start | bytes 5898244
  630.9 19.5 %copy-start.44 = (f32[768]{0:T(1024)S(1)}, f32[768]{0:T(1024)}, u32[]{:S(2)}) copy-start(f32[768]{0:T(1024)} %copy-done.43) | copy-start | bytes 9220
  630.9 19.6 %copy-start.7 = (f32[768,1280]{1,0:T(8,128)S(1)}, f32[768,1280]{1,0:T(8,128)}, u32[]{:S(2)}) copy-start(f32[768,1280]{1,0:T(8,128)} %copy-done.6) | copy-start | bytes 11796484
  670.7 27.8 %all-to-all-start.4 = ((bf16[2,384,4,320]{1,0,3,2:T(2,128)(2,1)}), bf16[2,384,4,320]{1,0,3,2:T(2,128)(2,1)S(1)}, u32[]{:S(2)}, u32[]{:S(2)}) async-start(bf16[2,384,4,320]{1,0,3,2:T(2,128)(2,1)} %copy.199), calls=%async_computation.4 | async-start | bytes 3932160 | tf_op jit(solution)/shard_map/all_to_all | solution.py:149
  698.6 7.0 copy-start.28
  730.9 10.9 copy-start.1
  761.8 10.9 copy-start.1
  793.3 10.9 copy-start.1
  844.5 10.9 copy-start.1
  875.3 10.9 copy-start.1
  906.9 10.9 copy-start.1
  939.4 32.1 %all-to-all-start.5 = ((bf16[2,1536,1,320]{3,0,2,1:T(2,128)(2,1)}), bf16[2,1536,1,320]{3,0,2,1:T(2,128)(2,1)S(1)}, u32[]{:S(2)}, u32[]{:S(2)}) async-start(bf16[2,1536,1,320]{3,0,2,1:T(2,128)(2,1)} %copy.185), calls=%async_computation.5 | async-start | bytes 4718592 | tf_op jit(solution)/shard_map/all_to_all | solution.py:201
  943.1 170.4 %reduce-scatter.7.cloned.1.call-start = ((), (), s32[]{:S(2)}) async-start(), calls=%async_computation.17 | async-start | bytes 3686400 | tf_op jit(solution)/shard_map/reduce_scatter | solution.py:246
  971.5 11.3 copy-start.14
  971.5 33.0 %all-to-all-start.6 = ((bf16[2,1536,1,320]{3,0,2,1:T(2,128)(2,1)}), bf16[2,1536,1,320]{3,0,2,1:T(2,128)(2,1)}, u32[]{:S(2)}, u32[]{:S(2)}) async-start(bf16[2,1536,1,320]{3,0,2,1:T(2,128)(2,1)} %copy.188), calls=%async_computation.6 | async-start | bytes 4718592 | tf_op jit(solution)/shard_map/all_to_all | solution.py:202
  1004.6 33.1 %all-to-all-start.7 = ((bf16[2,1536,1,320]{3,0,2,1:T(2,128)(2,1)}), bf16[2,1536,1,320]{3,0,2,1:T(2,128)(2,1)}, u32[]{:S(2)}, u32[]{:S(2)}) async-start(bf16[2,1536,1,320]{3,0,2,1:T(2,128)(2,1)} %copy.191), calls=%async_computation.7 | async-start | bytes 4718592 | tf_op jit(solution)/shard_map/all_to_all | solution.py:203
  1009.1 218.8 %reduce-scatter.5.cloned.1.call-start = ((), (), s32[]{:S(2)}) async-start(), calls=%async_computation.16 | async-start | bytes 11059200 | tf_op jit(solution)/shard_map/reduce_scatter | solution.py:237
  1060.8 384.5 %reduce-scatter.9.cloned.1.call-start = ((), (), s32[]{:S(2)}) async-start(), calls=%async_computation.18 | async-start | bytes 14745600 | tf_op jit(solution)/shard_map/reduce_scatter | solution.py:258
  1078.8 584.0 %reduce-scatter.11.cloned.1.call-start = ((), (), s32[]{:S(2)}) async-start(), calls=%async_computation.19 | async-start | bytes 14745600 | tf_op jit(solution)/shard_map/reduce_scatter | solution.py:264
  1096.7 665.4 %all-reduce.23.cloned.1.call-start = ((), (), s32[]{:S(2)}) async-start(), calls=%async_computation.20 | async-start | bytes 9830400 | tf_op jit(solution)/shard_map/psum | solution.py:274
  (49 other events, 159.3 us)
Sparse Core Ops, SparseCore 0:
  10.2 145.8 all-gather.5
  158.2 59.6 all-gather.7
  220.1 181.2 all-gather.9
  403.4 180.8 all-gather.11
  950.4 74.5 reduce-scatter.6
  1060.9 166.9 reduce-scatter.4
  1231.5 213.7 reduce-scatter.8
  1449.0 213.8 reduce-scatter.10
  1665.4 96.6 all-reduce.22
where the time goes:
time: 1790 us; the launch traced here: 1780 us
  waiting for transfers between devices  905 us (51%)
  matrix products  379 us (21%)
  local copies, waits for them, and re-layouts  240 us (13%)
  blocking collectives  115 us (6%)
  other arithmetic  85 us (5%)
  starting transfers between devices  34 us (2%)
    reduce_scatter x1, waiting for transfers between devices, local(): lax.psum_scatter(gradients[11].astype(jnp.bfloat16), 'fsdp', scatter_dime...  217 us
    reduce_scatter x1, waiting for transfers between devices, local(): lax.psum_scatter(gradients[9].astype(jnp.bfloat16), 'fsdp', scatter_dimen...  217 us
    all_gather x1, waiting for transfers between devices, local(): lax.all_gather(w_down, 'fsdp', axis=0, tiled=True)  124 us
    reduce_scatter x1, waiting for transfers between devices, local(): lax.psum_scatter(gradients[2].astype(jnp.bfloat16), 'fsdp', scatter_dimen...  114 us
    all_gather x1, waiting for transfers between devices, local(): lax.all_gather(w_qkv, 'fsdp', axis=0, tiled=True)  92.2 us
    unnamed x2, blocking collectives  77.6 us
    dot_general x1, matrix products, local(): jnp.dot(hidden2, wup, preferred_element_type=single) + ubias.astype(single)  51.7 us
    dot_general x12, matrix products, scores_of(): jnp.einsum('qhd,khd->hqk', query_block, keys, preferred_element_type=single)  45.4 us
  transfers between devices with their start and end apart: 17, of which 13 were waited for; matrix products, arithmetic and copies ran while one was open for 20% of the time, Pallas kernels for 0%

commit v1 on v0

v1 whole, which is shorter than its diff:
```python
import functools
import math

import jax
import jax.numpy as jnp
from jax import lax
from jax.experimental import pallas as pl
from jax.experimental.pallas import tpu as pltpu
from jax.sharding import PartitionSpec as P

HEADS = 16
LANES = 128
LOG2E = 1.0 / math.log(2.0)
single = jnp.float32
half = jnp.bfloat16


def layer_norm(v, gain, bias):
    mean = jnp.mean(v, axis=-1, keepdims=True)
    cent = v - mean
    var = jnp.mean(cent * cent, axis=-1, keepdims=True)
    return cent * lax.rsqrt(var + 1e-05) * gain + bias


def flip(tensor, bits, axis="seq"):
    return lax.ppermute(
        tensor, axis, [(i, i ^ bits) for i in range(lax.axis_size(axis))]
    )


def gather_all(piece):
    groups = lax.axis_size("seq")
    blocks = {0: piece}
    bits = groups // 2
    while bits:
        for r in sorted(blocks):
            blocks[r | bits] = flip(blocks[r], bits)
        bits //= 2
    return [blocks[r] for r in range(groups)]


def scatter_sum(partial):
    groups = lax.axis_size("seq")
    n = partial.shape[0] // groups
    terms = {r: partial[r * n : (r + 1) * n] for r in range(groups)}
    bits = 1
    while bits < groups:
        for r in reversed(range(0, groups, 2 * bits)):
            terms[r] = terms[r].astype(single) + flip(terms[r | bits].astype(half), bits).astype(single)
        bits *= 2
    return terms[0]


def swap(parts):
    return [parts[0]] + [flip(parts[r], r) for r in range(1, len(parts))]


def pad_lanes(tensor, tail):
    return jnp.concatenate([tensor, tail], axis=1)


def unit_tail(rows, width):
    lane = lax.broadcasted_iota(jnp.int32, (rows, width), 1)
    return jnp.where(lane == 0, 1.0, 0.0).astype(half)


def attend_kernel(heads, dim, block, scale, qkv_ref, mask_ref, ctx_ref, lse_ref, keys, values):
    seq = qkv_ref.shape[0]
    span = heads * dim
    rest = LANES - dim
    rate = scale * LOG2E
    for j in range(heads):
        keys[j] = pad_lanes(
            qkv_ref[:, span + j * dim : span + (j + 1) * dim], mask_ref[...]
        )
        values[j] = pad_lanes(
            qkv_ref[:, 2 * span + j * dim : 2 * span + (j + 1) * dim], unit_tail(seq, rest)
        )

    def one_block(i, carry):
        rows = pl.ds(pl.multiple_of(i * block, block), block)
        ones = unit_tail(block, rest)
        contexts, sums = [], []
        for j in range(heads):
            query = pad_lanes(qkv_ref[rows, j * dim : (j + 1) * dim], ones)
            scores = lax.dot_general(
                query, keys[j], (((1,), (1,)), ((), ())), preferred_element_type=single
            )
            top = jnp.max(scores, axis=-1, keepdims=True) * rate
            probs = jnp.exp2(scores * rate - top).astype(half)
            mixed = jnp.dot(probs, values[j], preferred_element_type=single)
            total = mixed[:, dim : dim + 1]
            contexts.append((mixed[:, :dim] / total).astype(half))
            sums.append(top + jnp.log(total) * LOG2E)
        ctx_ref[rows, :] = jnp.concatenate(contexts, axis=1)
        lse_ref[rows, :] = jnp.concatenate(sums, axis=1)
        return carry

    lax.fori_loop(0, seq // block, one_block, 0)


def attend_back_kernel(
    heads, dim, block, scale,
    qkv_ref, mask_ref, grad_ref, lse_ref, out_ref, keys, values, gkeys, gvalues, gquery,
):
    seq = qkv_ref.shape[0]
    span = heads * dim
    rest = LANES - dim
    rate = scale * LOG2E
    for j in range(heads):
        keys[j] = pad_lanes(
            qkv_ref[:, span + j * dim : span + (j + 1) * dim], mask_ref[...]
        )
        values[j] = pad_lanes(
            qkv_ref[:, 2 * span + j * dim : 2 * span + (j + 1) * dim],
            jnp.zeros((seq, rest), half),
        )
    gkeys[...] = jnp.zeros_like(gkeys)
    gvalues[...] = jnp.zeros_like(gvalues)

    def one_block(i, carry):
        rows = pl.ds(pl.multiple_of(i * block, block), block)
        ones = unit_tail(block, rest)
        none = jnp.zeros((block, rest), half)
        pieces = []
        for j in range(heads):
            query = pad_lanes(qkv_ref[rows, j * dim : (j + 1) * dim], ones)
            grad = pad_lanes(grad_ref[rows, j * dim : (j + 1) * dim], none)
            scores = lax.dot_general(
                query, keys[j], (((1,), (1,)), ((), ())), preferred_element_type=single
            )
            probs = jnp.exp2(scores * rate - lse_ref[rows, j : j + 1])
            dprobs = lax.dot_general(
                grad, values[j], (((1,), (1,)), ((), ())), preferred_element_type=single
            )
            inner = jnp.sum(probs * dprobs, axis=-1, keepdims=True)
            dscores = (probs * (dprobs - inner)).astype(half)
            pieces.append(
                (jnp.dot(dscores, keys[j], preferred_element_type=single)[:, :dim] * scale).astype(half)
            )
            gkeys[j] += jnp.dot(query.T, dscores, preferred_element_type=single)
            gvalues[j] += jnp.dot(grad.T, probs.astype(half), preferred_element_type=single)
        gquery[rows, :] = jnp.concatenate(pieces, axis=1)
        return carry

    lax.fori_loop(0, seq // block, one_block, 0)

    def put(i, carry):
        rows = pl.ds(pl.multiple_of(i * block, block), block)
        pieces = [gquery[rows, :]]
        for j in range(heads):
            pieces.append((gkeys[j, :, rows].T[:, :dim] * scale).astype(half))
        for j in range(heads):
            pieces.append(gvalues[j, :, rows].T[:, :dim].astype(half))
        out_ref[rows, :] = jnp.concatenate(pieces, axis=1)
        return carry

    lax.fori_loop(0, seq // block, put, 0)


def attend(qkv, mask, heads, dim, scale):
    seq = qkv.shape[0]
    block = 256
    return pl.pallas_call(
        functools.partial(attend_kernel, heads, dim, block, scale),
        out_shape=(
            jax.ShapeDtypeStruct((seq, heads * dim), half),
            jax.ShapeDtypeStruct((seq, heads), single),
        ),
        scratch_shapes=[
            pltpu.VMEM((heads, seq, LANES), half),
            pltpu.VMEM((heads, seq, LANES), half),
        ],
        compiler_params=pltpu.CompilerParams(vmem_limit_bytes=48 << 20),
        cost_estimate=pl.CostEstimate(
            flops=4 * heads * seq * seq * 256, bytes_accessed=qkv.size * 3, transcendentals=heads * seq * seq
        ),
        name="attend",
    )(qkv, mask)


def attend_back(qkv, mask, grad, lse, heads, dim, scale):
    seq = qkv.shape[0]
    block = 256
    return pl.pallas_call(
        functools.partial(attend_back_kernel, heads, dim, block, scale),
        out_shape=jax.ShapeDtypeStruct(qkv.shape, half),
        scratch_shapes=[
            pltpu.VMEM((heads, seq, LANES), half),
            pltpu.VMEM((heads, seq, LANES), half),
            pltpu.VMEM((heads, LANES, seq), single),
            pltpu.VMEM((heads, LANES, seq), single),
            pltpu.VMEM((seq, heads * dim), half),
        ],
        compiler_params=pltpu.CompilerParams(vmem_limit_bytes=56 << 20),
        cost_estimate=pl.CostEstimate(
            flops=10 * heads * seq * seq * 256, bytes_accessed=qkv.size * 5, transcendentals=heads * seq * seq
        ),
        name="attend_back",
    )(qkv, mask, grad, lse)


def local(
    frames_in, teacher, lengths, norm1_gain, norm1_bias, w_qkv, query_bias, value_bias,
    w_attn_out, attn_out_bias, norm2_gain, norm2_bias, w_up, up_bias, w_down, down_bias,
):
    clips, frames, width = frames_in.shape
    groups = lax.axis_size("seq")
    owners = lax.axis_size("fsdp")
    me = lax.axis_index("seq")
    own = lax.axis_index("fsdp")
    seq_len = frames * groups
    dim = width // HEADS
    heads = HEADS // groups
    span = heads * dim
    depth = w_qkv.shape[0]
    units = w_down.shape[0]
    part = units // groups
    scale = 1.0 / math.sqrt(dim)

    def dot(a, b):
        return jnp.dot(a, b, preferred_element_type=single)

    def dot_t(a, b):
        return lax.dot_general(a, b, (((1,), (1,)), ((), ())), preferred_element_type=single)

    def t_dot(a, b):
        return lax.dot_general(a, b, (((0,), (0,)), ((), ())), preferred_element_type=single)

    def columns(array, start, size):
        return lax.dynamic_slice_in_dim(array, start, size, 1)

    states = [gather_all(frames_in[c]) for c in range(clips)]

    first = jnp.concatenate(
        [columns(w_qkv, k * width + me * span, span) for k in range(3)]
        + [columns(w_attn_out, me * span, span)],
        axis=1,
    )
    first = lax.all_gather(first, "fsdp", axis=0, tiled=True)
    ff = owners * part
    wup = jnp.concatenate([columns(w_up, f * units + me * part, part) for f in range(owners)], axis=1)
    wdown = lax.dynamic_slice_in_dim(w_down, me * part, part, 0)
    if part == depth:
        second = lax.all_gather(jnp.concatenate([wup, wdown], axis=1), "fsdp", axis=0, tiled=True)
        wup, wdown = second[:, :ff], second[:, ff:]
    else:
        wup = lax.all_gather(wup, "fsdp", axis=0, tiled=True)
        wdown = lax.all_gather(wdown, "fsdp", axis=0, tiled=True)
    wqkv = first[:, : 3 * span]

    packed = jnp.concatenate(
        [norm1_gain, norm1_bias, query_bias, value_bias, attn_out_bias, norm2_gain, norm2_bias,
         down_bias, up_bias]
    )[None]
    bits = 1
    while bits < owners:
        packed = jnp.concatenate([packed, flip(packed, bits, "fsdp")], axis=0)
        bits *= 2
    vectors = jnp.take(packed, own ^ jnp.arange(owners), axis=0).astype(single)

    def vector(k):
        return vectors[:, k * depth : (k + 1) * depth].reshape(1, width)

    gain1, bias1, qbias, vbias, obias, gain2, bias2, dbias = (vector(k) for k in range(8))
    ubias = lax.dynamic_slice_in_dim(vectors, 8 * depth + me * part, part, 1).reshape(1, ff)
    qkv_bias = jnp.concatenate(
        [columns(qbias, me * span, span), jnp.zeros((1, span), single), columns(vbias, me * span, span)],
        axis=1,
    )

    quarters = jnp.stack(gather_all(first[:, 3 * span :]))
    wout = jnp.concatenate(
        [lax.dynamic_index_in_dim(quarters, me ^ g, 0, keepdims=False) for g in range(groups)], axis=1
    )
    wout = jnp.concatenate(
        [lax.dynamic_slice_in_dim(wout, (me ^ r) * span, span, 0) for r in range(groups)], axis=0
    )

    mine = lax.dynamic_slice_in_dim(lengths, own * clips, clips)
    order = (me ^ jnp.arange(groups, dtype=jnp.int32))[:, None] * frames + jnp.arange(
        frames, dtype=jnp.int32
    )
    order = order.reshape(seq_len)
    count = jnp.sum(lengths).astype(single)
    lane0 = (jnp.arange(LANES - dim) == 0)[None, :]
    masks = [
        jnp.where((order >= mine[c])[:, None] & lane0, -1e30, 0.0).astype(half) for c in range(clips)
    ]
    row_valid = [(order[:frames] < mine[c]).astype(single)[:, None] for c in range(clips)]

    full1, qkvs, sums, contexts, middles, full2 = [], [], [], [], [], []
    for c in range(clips):
        state = jnp.concatenate(states[c], axis=0).astype(single)
        hidden = layer_norm(state, gain1, bias1).astype(half)
        qkv = (dot(hidden, wqkv) + qkv_bias).astype(half)
        context, lse = attend(qkv, masks[c], heads, dim, scale)
        full1.append(hidden)
        qkvs.append(qkv)
        sums.append(lse)
        context = swap([context[r * frames : (r + 1) * frames] for r in range(groups)])
        contexts.append(jnp.concatenate(context, axis=1))
    for c in range(clips):
        middle = frames_in[c].astype(single) + dot(contexts[c], wout) + obias
        hidden = layer_norm(middle, gain2, bias2).astype(half)
        middles.append(middle)
        full2.append(jnp.concatenate(gather_all(hidden), axis=0))
    actives, slopes, branches = [], [], []
    for c in range(clips):
        upper = dot(full2[c], wup) + ubias
        cdf = 0.5 * (1.0 + lax.erf(upper * math.sqrt(0.5)))
        actives.append((upper * cdf).astype(half))
        slopes.append(
            (cdf + upper * (jnp.exp(-0.5 * upper * upper) * (1.0 / math.sqrt(2.0 * math.pi)))).astype(half)
        )
        branches.append(scatter_sum(dot(actives[c], wdown).astype(half)))
    outs, losses, grad_outs, fulls = [], [], [], []
    for c in range(clips):
        result = middles[c] + branches[c] + dbias
        outs.append(result.astype(half))
        diff = result - teacher[c].astype(single)
        masked = diff * row_valid[c]
        losses.append(jnp.sum(masked * diff) / (2.0 * width * count))
        grad_out = masked * (float(lengths.shape[0] * seq_len) / count)
        grad_outs.append(grad_out)
        fulls.append(jnp.concatenate(gather_all(grad_out.astype(half)), axis=0))
    frames_out = jnp.stack(outs)

    def owned(grad):
        return lax.psum_scatter(grad.astype(half), "fsdp", scatter_dimension=0, tiled=True)

    grad_wdown = owned(sum(t_dot(actives[c], fulls[c]) for c in range(clips)))
    grad_dbias = sum(jnp.sum(g.astype(half).astype(single), axis=0) for g in grad_outs)
    grad_uppers = [
        (dot_t(fulls[c], wdown) * slopes[c].astype(single)).astype(half) for c in range(clips)
    ]
    grad_hidden2 = [scatter_sum(dot_t(grad_uppers[c], wup).astype(half)) for c in range(clips)]
    grad_wup = owned(sum(t_dot(full2[c], grad_uppers[c]) for c in range(clips)))
    grad_ubias = sum(jnp.sum(g.astype(single), axis=0) for g in grad_uppers)

    def norm_back(v, gain, bias, grad):
        _, back = jax.vjp(layer_norm, v, gain, bias)
        return back(grad)

    grad_gain2 = grad_bias2 = 0.0
    grad_middles, grad_branches, grad_heads = [], [], []
    for c in range(clips):
        gm, gg, gb = norm_back(middles[c], gain2, bias2, grad_hidden2[c])
        grad_gain2 += gg
        grad_bias2 += gb
        grad_middles.append(grad_outs[c] + gm)
        branch = grad_middles[c].astype(half)
        grad_branches.append(branch)
        grad_context = dot_t(branch, wout).astype(half)
        grad_context = swap([grad_context[:, r * span : (r + 1) * span] for r in range(groups)])
        grad_heads.append(jnp.concatenate(grad_context, axis=0))
    grad_obias = sum(jnp.sum(g.astype(single), axis=0) for g in grad_branches)

    grad_wout = sum(t_dot(contexts[c], grad_branches[c]) for c in range(clips)).astype(half)
    grad_wout = jnp.concatenate(
        [lax.dynamic_slice_in_dim(grad_wout, (me ^ g) * span, span, 0) for g in range(groups)], axis=0
    )
    quarter = jnp.concatenate([columns(grad_wout, (me ^ r) * span, span) for r in range(groups)], axis=0)
    grad_wout = owned(scatter_sum(quarter))

    grad_qkvs = [
        attend_back(qkvs[c], masks[c], grad_heads[c], sums[c], heads, dim, scale) for c in range(clips)
    ]
    grad_wqkv = owned(sum(t_dot(full1[c], grad_qkvs[c]) for c in range(clips)))
    grad_qkv_bias = sum(jnp.sum(g.astype(single), axis=0) for g in grad_qkvs)
    grad_hidden1 = [scatter_sum(dot_t(grad_qkvs[c], wqkv).astype(half)) for c in range(clips)]
    grad_gain1 = grad_bias1 = 0.0
    grads_in = []
    for c in range(clips):
        gs, gg, gb = norm_back(frames_in[c].astype(single), gain1, bias1, grad_hidden1[c])
        grad_gain1 += gg
        grad_bias1 += gb
        grads_in.append(grad_middles[c] + gs)
    grad_in = jnp.stack(grads_in)

    def rows8(v):
        return v.reshape(owners, depth)

    def spread(v):
        return lax.dynamic_update_slice(jnp.zeros((width,), single), v, (me * span,))

    slot = (jnp.arange(groups) == me).astype(single)[None, :, None]
    rows = jnp.concatenate(
        [rows8(grad_gain1), rows8(grad_bias1), rows8(spread(grad_qkv_bias[:span])),
         rows8(spread(grad_qkv_bias[2 * span :])), rows8(grad_obias), rows8(grad_gain2),
         rows8(grad_bias2), rows8(grad_dbias),
         (grad_ubias.reshape(owners, 1, part) * slot).reshape(owners, units)],
        axis=1,
    )
    rows = jnp.take(rows, own ^ jnp.arange(owners), axis=0)
    bits = owners // 2
    while bits:
        rows = rows[:bits] + flip(rows[bits:], bits, "fsdp")
        bits //= 2
    rows = jnp.concatenate([rows[0], jnp.stack(losses)])
    rows = rows + flip(rows, 1)
    rows = rows + flip(rows, 2)
    small = [rows[k * depth : (k + 1) * depth] for k in range(8)]
    small_up = rows[8 * depth : 8 * depth + units]
    clip_loss = rows[8 * depth + units :]

    def whole(piece):
        return jnp.take(jnp.stack(gather_all(piece)), me ^ jnp.arange(groups), axis=0).astype(single)

    grad_wqkv = whole(grad_wqkv).reshape(groups, depth, 3, span).transpose(1, 2, 0, 3).reshape(depth, 3 * width)
    grad_wout = whole(grad_wout).transpose(1, 0, 2).reshape(depth, width)
    grad_wup = whole(grad_wup).reshape(groups, depth, owners, part).transpose(1, 2, 0, 3).reshape(depth, owners * units)
    grad_wdown = whole(grad_wdown).reshape(units, width)
    return (
        frames_out, clip_loss, grad_in, small[0], small[1], grad_wqkv, small[2], small[3],
        grad_wout, small[4], small[5], small[6], grad_wup, small_up, grad_wdown, small[7],
    )


def solution(mesh):
    vec, mat, act = P("fsdp"), P("fsdp", None), P("fsdp", "seq", None)
    return jax.shard_map(
        local,
        mesh=mesh,
        in_specs=(act, act, P(), vec, vec, mat, vec, vec, mat, vec, vec, vec, mat, vec, mat, vec),
        out_specs=(act, vec, act, vec, vec, mat, vec, vec, mat, vec, vec, vec, mat, vec, mat, vec),
        check_vma=False,
    )
```

time: 1790 us -> 842 us (0.47)
  waiting for transfers between devices: 905 us -> 264 us
  matrix products: 379 us -> 176 us
  local copies, waits for them, and re-layouts: 240 us -> 113 us
  blocking collectives: 115 us -> 0 us
  Pallas kernels: 0 us -> 113 us
  other arithmetic: 85 us -> 103 us
    reduce_scatter x4 -> x3, waiting for transfers between devices: 549 us -> 0.02 us  [owned(): lax.psum_scatter(grad.astype(half), 'fsdp', scatter_dimension=0, tiled=True)]
    ppermute x0 -> x74, waiting for transfers between devices: none -> 259 us  [flip(): lax.ppermute(tensor, axis, [(i, i ^ bits) for i in range(lax.axis_size(ax...]
    all_gather x4 -> x2, waiting for transfers between devices: 216 us -> 4.76 us  [the longest x1 4.74 us: local(): first = lax.all_gather(first, 'fsdp', axis=0, tiled=True)]
    dot_general x54 -> x24, matrix products: 379 us -> 176 us  [the longest x8 64.4 us: dot_t(): lax.dot_general(a, b, (((1,), (1,)), ((), ())), preferred_element_type=si...]
    pallas_call x0 -> x4, Pallas kernels: none -> 113 us  [the longest x2 74.9 us: attend_back(): pl.pallas_call(functools.partial(attend_back_kernel, heads, dim, block, s...]
    all_to_all x8 -> x0, waiting for transfers between devices: 101 us -> none  [the longest x1 24.2 us: local(): lax.all_to_all(grad_context.reshape(clips, frames, groups, span), 'seq',...]
    unnamed x2 -> x0, blocking collectives: 77.6 us -> none
    while x54 -> x0, local copies, waits for them, and re-layouts: 67.7 us -> none
  transfers between devices with their start and end apart: 17 -> 80, of which waited for: 13 -> 25; matrix products, arithmetic and copies ran while one was open for 20% -> 43% of each run, Pallas kernels for 0% -> 14%
where the time goes in v1:
time: 842 us; the launch traced here: 831 us
  waiting for transfers between devices  264 us (31%)
  matrix products  176 us (21%)
  local copies, waits for them, and re-layouts  113 us (13%)
  Pallas kernels  113 us (13%)
  other arithmetic  103 us (12%)
  starting transfers between devices  44.8 us (5%)
  between operations  18.2 us (2%)
    ppermute x74, waiting for transfers between devices, flip(): lax.ppermute(tensor, axis, [(i, i ^ bits) for i in range(lax.axis_size(ax...  259 us
    pallas_call x2, Pallas kernels, attend_back(): pl.pallas_call(functools.partial(attend_back_kernel, heads, dim, block, s...  74.9 us
    dot_general x8, matrix products, dot_t(): lax.dot_general(a, b, (((1,), (1,)), ((), ())), preferred_element_type=si...  64.4 us
    dot_general x8, matrix products, t_dot(): lax.dot_general(a, b, (((0,), (0,)), ((), ())), preferred_element_type=si...  57 us
    dot_general x8, matrix products, dot(): return jnp.dot(a, b, preferred_element_type=single)  54.9 us
    ppermute x74, starting transfers between devices, flip(): lax.ppermute(tensor, axis, [(i, i ^ bits) for i in range(lax.axis_size(ax...  44.3 us
    pallas_call x2, Pallas kernels, attend(): pl.pallas_call(functools.partial(attend_kernel, heads, dim, block, scale)...  37.8 us
    reshape x3, local copies, waits for them, and re-layouts, local(): whole(grad_wup).reshape(groups, depth, owners, part).transpose(1, 2, 0, 3)  22.1 us
  transfers between devices with their start and end apart: 80, of which 25 were waited for; matrix products, arithmetic and copies ran while one was open for 43% of the time, Pallas kernels for 14%

profile of v1, /device:TPU:0, one launch (start us, length us, event | category | flops | bytes accessed | tf_op | source)
XLA Modules:
  0.0 831.2 jit_solution(4050826389366465431)
XLA Ops:
  38.8 19.6 %collective-permute-done.19 = bf16[384,1280]{1,0:T(8,128)(2,1)} collective-permute-done((bf16[384,1280]{1,0:T(8,128)(2,1)}, bf16[384,1280]{1,0:T(8,128)(2,1)}, u32[]{:S(2)}, u32[]{:S(2)}) %collective-permute-start.19) | collective-permute-done | bytes 983072 | tf_op jit(solution)/shard_map/ppermute | solution.py:26
  60.5 4.9 fusion.8
  70.9 4.7 all-gather.3.cloned.1.call-done
  82.3 9.1 %add_convert_fusion.1.qkv_ref = bf16[1536,960]{1,0:T(8,128)(2,1)S(1)} fusion(f32[960]{0:T(1024)S(1)} %bitcast.140, bf16[1280,1280]{1,0:T(8,128)(2,1)} %all-gather.3.cloned.1.call-done, f32[1280]{0:T(1024)S(1)} %add.529, f32[1280]{0:T(1024)S(1)} %mul.404, f32[1536]{0:T(1024)S(1)} %add_rsqrt_fusion.1, f32[1536]{0:T(1024)S(1)} %broadcast_multiply_fusion.2, ...), kind=kOutput, calls=%fused_computation.61 | convolution fusion | flops 3803381760 | bytes 9529088 | tf_op jit(solution)/shard_map/dot_general | solution.py:222
  91.4 19.1 %attend.2 = (bf16[1536,320]{1,0:T(8,128)(2,1)S(1)}, f32[1536,4]{1,0:T(8,128)S(1)}) custom-call(bf16[1536,960]{1,0:T(8,128)(2,1)S(1)} %add_convert_fusion.1.qkv_ref, bf16[1536,48]{1,0:T(8,128)(2,1)S(1)} %get-tuple-element.155.mask_ref), custom_call_target="tpu_custom_call" | custom-call | flops 9663676416 | bytes 4423680 | tf_op jit(solution)/shard_map/attend/pallas_call | solution.py:164
  112.8 8.5 %add_convert_fusion.qkv_ref = bf16[1536,960]{1,0:T(8,128)(2,1)S(1)} fusion(f32[960]{0:T(1024)S(1)} %bitcast.141, bf16[1280,1280]{1,0:T(8,128)(2,1)S(1)} %copy-done.57, f32[1536]{0:T(1024)S(1)} %add_rsqrt_fusion, f32[1536]{0:T(1024)S(1)} %broadcast_multiply_fusion.1, f32[1280]{0:T(1024)S(1)} %add.529, f32[1280]{0:T(1024)S(1)} %mul.404, ...), kind=kOutput, calls=%fused_computation.60 | convolution fusion | flops 3803381760 | bytes 9539584 | tf_op jit(solution)/shard_map/dot_general | solution.py:222
  122.1 18.7 %attend.3 = (bf16[1536,320]{1,0:T(8,128)(2,1)S(1)}, f32[1536,4]{1,0:T(8,128)S(1)}) custom-call(bf16[1536,960]{1,0:T(8,128)(2,1)S(1)} %add_convert_fusion.qkv_ref, bf16[1536,48]{1,0:T(8,128)(2,1)S(1)} %get-tuple-element.154.mask_ref), custom_call_target="tpu_custom_call" | custom-call | flops 9663676416 | bytes 4423680 | tf_op jit(solution)/shard_map/attend/pallas_call | solution.py:164
  151.6 5.2 collective-permute-done.23
  169.2 6.5 concatenate.76
  186.2 22.7 %collective-permute-done.25 = bf16[384,1280]{1,0:T(8,128)(2,1)} collective-permute-done((bf16[384,1280]{1,0:T(8,128)(2,1)}, bf16[384,1280]{1,0:T(8,128)(2,1)}, u32[]{:S(2)}, u32[]{:S(2)}) %collective-permute-start.25) | collective-permute-done | bytes 983072 | tf_op jit(solution)/shard_map/ppermute | solution.py:26
  209.5 20.3 %collective-permute-done.13 = bf16[384,1280]{1,0:T(8,128)(2,1)} collective-permute-done((bf16[384,1280]{1,0:T(8,128)(2,1)S(1)}, bf16[384,1280]{1,0:T(8,128)(2,1)}, u32[]{:S(2)}, u32[]{:S(2)}) %collective-permute-start.13) | collective-permute-done | bytes 983072 | tf_op jit(solution)/shard_map/ppermute | solution.py:26
  229.8 12.3 %multiply_convert_fusion = (bf16[1536,1280]{1,0:T(8,128)(2,1)S(1)}, f32[1536,1280]{1,0:T(8,128)}) fusion(f32[1280]{0:T(1024)S(1)} %add.572, bf16[1280,2560]{1,0:T(8,128)(2,1)} %all-gather.5.cloned.1.call-done, bf16[384,1280]{1,0:T(8,128)(2,1)} %collective-permute-done.26, bf16[384,1280]{1,0:T(8,128)(2,1)} %collective-permute-done.25, ...), kind=kOutput, calls=%fused_computation.43 | convolution fusion | flops 5060689920 | bytes 19010560 | tf_op jit(solution)/shard_map/dot_general | solution.py:222
  242.1 5.5 convolution_convert_fusion.4
  249.3 11.1 %multiply_convert_fusion.1 = (bf16[1536,1280]{1,0:T(8,128)(2,1)S(1)}, f32[1536,1280]{1,0:T(8,128)}) fusion(f32[1280]{0:T(1024)S(1)} %add.572, bf16[1280,2560]{1,0:T(8,128)(2,1)S(1)} %copy-done.97, bf16[384,1280]{1,0:T(8,128)(2,1)} %collective-permute-done.14, bf16[384,1280]{1,0:T(8,128)(2,1)} %collective-permute-done.13, ...), kind=kOutput, calls=%fused_computation.45 | convolution fusion | flops 5060689920 | bytes 19013632 | tf_op jit(solution)/shard_map/dot_general | solution.py:222
  260.4 5.4 convolution_convert_fusion.5
  274.9 18.9 %collective-permute-done.29 = bf16[384,1280]{1,0:T(8,128)(2,1)} collective-permute-done((bf16[384,1280]{1,0:T(8,128)(2,1)}, bf16[384,1280]{1,0:T(8,128)(2,1)}, u32[]{:S(2)}, u32[]{:S(2)}) %collective-permute-start.29) | collective-permute-done | bytes 983072 | tf_op jit(solution)/shard_map/ppermute | solution.py:26
  293.9 20.5 %collective-permute-done.17 = bf16[384,1280]{1,0:T(8,128)(2,1)} collective-permute-done((bf16[384,1280]{1,0:T(8,128)(2,1)}, bf16[384,1280]{1,0:T(8,128)(2,1)}, u32[]{:S(2)}, u32[]{:S(2)}) %collective-permute-start.17) | collective-permute-done | bytes 983072 | tf_op jit(solution)/shard_map/ppermute | solution.py:26
  314.3 5.7 fusion.46
  324.3 22.7 %collective-permute-done.31 = bf16[384,1280]{1,0:T(8,128)(2,1)} collective-permute-done((bf16[384,1280]{1,0:T(8,128)(2,1)S(1)}, bf16[384,1280]{1,0:T(8,128)(2,1)}, u32[]{:S(2)}, u32[]{:S(2)}) %collective-permute-start.31) | collective-permute-done | bytes 983072 | tf_op jit(solution)/shard_map/ppermute | solution.py:26
  349.4 17.2 %collective-permute-done.43 = bf16[384,1280]{1,0:T(8,128)(2,1)} collective-permute-done((bf16[384,1280]{1,0:T(8,128)(2,1)}, bf16[384,1280]{1,0:T(8,128)(2,1)}, u32[]{:S(2)}, u32[]{:S(2)}) %collective-permute-start.43) | collective-permute-done | bytes 983072 | tf_op jit(solution)/shard_map/ppermute | solution.py:26
  366.6 13.0 %convert_reduce_fusion.3 = (f32[1280]{0:T(1024)S(1)}, bf16[1536,1280]{1,0:T(8,128)(2,1)S(1)}) fusion(f32[1536,1280]{1,0:T(8,128)} %get-tuple-element.165, bf16[1280,2560]{1,0:T(8,128)(2,1)} %all-gather.5.cloned.1.call-done, bf16[384,1280]{1,0:T(8,128)(2,1)} %collective-permute-done.32, bf16[384,1280]{1,0:T(8,128)(2,1)} %collective-permute-done.31, ...), kind=kOutput, calls=%fused_computation.42 | convolution fusion | flops 5076417536 | bytes 19010560 | tf_op jit(solution)/shard_map/dot_general | solution.py:225
  379.7 8.9 %convolution_convert_fusion.3 = bf16[1536,1280]{1,0:T(8,128)(2,1)S(1)} fusion(bf16[1536,1280]{1,0:T(8,128)(2,1)S(1)} %get-tuple-element.169, bf16[1280,2560]{1,0:T(8,128)(2,1)} %all-gather.5.cloned.1.call-done), kind=kOutput, calls=%fused_computation.55 | convolution fusion | flops 5035130880 | bytes 11141120 | tf_op jit(solution)/shard_map/dot_general | solution.py:225
  390.2 14.9 %convert_reduce_fusion.2 = (f32[1280]{0:T(1024)S(1)}, bf16[1536,1280]{1,0:T(8,128)(2,1)S(1)}) fusion(f32[1536,1280]{1,0:T(8,128)} %get-tuple-element.167, bf16[1280,2560]{1,0:T(8,128)(2,1)} %all-gather.5.cloned.1.call-done, bf16[384,1280]{1,0:T(8,128)(2,1)S(1)} %collective-permute-done.44, bf16[384,1280]{1,0:T(8,128)(2,1)} %collective-permute-done.43, ...), kind=kOutput, calls=%fused_computation.41 | convolution fusion | flops 5076417536 | bytes 19010560 | tf_op jit(solution)/shard_map/dot_general | solution.py:225
  405.1 5.7 convolution_convert_fusion.2
  412.5 7.1 fusion.62
  424.1 8.1 fusion.22
  432.3 13.5 %collective-permute-done.35 = bf16[384,1280]{1,0:T(8,128)(2,1)} collective-permute-done((bf16[384,1280]{1,0:T(8,128)(2,1)}, bf16[384,1280]{1,0:T(8,128)(2,1)}, u32[]{:S(2)}, u32[]{:S(2)}) %collective-permute-start.35) | collective-permute-done | bytes 983072 | tf_op jit(solution)/shard_map/ppermute | solution.py:26
  445.8 20.6 %collective-permute-done.47 = bf16[384,1280]{1,0:T(8,128)(2,1)} collective-permute-done((bf16[384,1280]{1,0:T(8,128)(2,1)}, bf16[384,1280]{1,0:T(8,128)(2,1)}, u32[]{:S(2)}, u32[]{:S(2)}) %collective-permute-start.47) | collective-permute-done | bytes 983072 | tf_op jit(solution)/shard_map/ppermute | solution.py:26
  466.4 6.2 multiply_reduce_fusion
  487.3 6.5 concatenate.89
  501.3 11.3 %fusion.61 = f32[1280,1280]{1,0:T(8,128)} fusion(bf16[1536,1280]{1,0:T(8,128)(2,1)} %copy-done.102, bf16[384,1280]{1,0:T(8,128)(2,1)} %copy-done.99, bf16[384,1280]{1,0:T(8,128)(2,1)} %collective-permute-done.43, bf16[384,1280]{1,0:T(8,128)(2,1)} %copy-done.98, bf16[384,1280]{1,0:T(8,128)(2,1)} %get-tuple-element.51), kind=kOutput, calls=%fused_computation.174 | convolution fusion | flops 5048893440 | bytes 14417920 | tf_op jit(solution)/shard_map/dot_general | solution.py:228
  512.7 8.7 %collective-permute-done.64 = bf16[1280,320]{0,1:T(8,128)(2,1)S(1)} collective-permute-done((bf16[1280,320]{0,1:T(8,128)(2,1)S(1)}, bf16[1280,320]{0,1:T(8,128)(2,1)S(1)}, u32[]{:S(2)}, u32[]{:S(2)}) %collective-permute-start.64) | collective-permute-done | bytes 819232 | tf_op jit(solution)/shard_map/ppermute | solution.py:26
  524.2 12.0 %fusion.23 = bf16[1280,1280]{1,0:T(8,128)(2,1)} fusion(f32[1280,1280]{1,0:T(8,128)} %fusion.61, bf16[1536,1280]{1,0:T(8,128)(2,1)} %copy-done.101, bf16[384,1280]{1,0:T(8,128)(2,1)} %collective-permute-done.32, bf16[384,1280]{1,0:T(8,128)(2,1)} %collective-permute-done.31, bf16[384,1280]{1,0:T(8,128)(2,1)} %collective-permute-done.30, ...), kind=kOutput, calls=%fused_computation.48 | convolution fusion | flops 5052170240 | bytes 17694720 | tf_op jit(solution)/shard_map/dot_general | solution.py:228
  538.1 5.5 convolution_convert_fusion.6
  559.0 5.4 collective-permute-done.50
  566.7 37.4 %attend_back.3 = bf16[1536,960]{1,0:T(8,128)(2,1)} custom-call(bf16[1536,960]{1,0:T(8,128)(2,1)} %copy-done.5, bf16[1536,48]{1,0:T(8,128)(2,1)} %copy-done.3, bf16[1536,320]{1,0:T(8,128)(2,1)} %pad_maximum_fusion.14.grad_ref, f32[1536,4]{1,0:T(8,128)} %copy-done.7), custom_call_target="tpu_custom_call" | custom-call | flops 24159191040 | bytes 7372800 | tf_op jit(solution)/shard_map/attend_back/pallas_call | solution.py:185
  604.2 6.2 convolution_convert_fusion
  616.6 37.5 %attend_back.2 = bf16[1536,960]{1,0:T(8,128)(2,1)} custom-call(bf16[1536,960]{1,0:T(8,128)(2,1)} %copy-done.4, bf16[1536,48]{1,0:T(8,128)(2,1)} %copy-done.2, bf16[1536,320]{1,0:T(8,128)(2,1)} %pad_maximum_fusion.13.grad_ref, f32[1536,4]{1,0:T(8,128)} %copy-done.6), custom_call_target="tpu_custom_call" | custom-call | flops 24159191040 | bytes 7372800 | tf_op jit(solution)/shard_map/attend_back/pallas_call | solution.py:185
  654.1 6.3 convolution_convert_fusion.1
  662.7 6.9 fusion.94
  669.6 7.6 add_convert_fusion.2
  688.5 19.5 %collective-permute-done.41 = bf16[384,1280]{1,0:T(8,128)(2,1)} collective-permute-done((bf16[384,1280]{1,0:T(8,128)(2,1)}, bf16[384,1280]{1,0:T(8,128)(2,1)}, u32[]{:S(2)}, u32[]{:S(2)}) %collective-permute-start.41) | collective-permute-done | bytes 983072 | tf_op jit(solution)/shard_map/ppermute | solution.py:26
  711.8 17.1 %collective-permute-done.53 = bf16[384,1280]{1,0:T(8,128)(2,1)S(1)} collective-permute-done((bf16[384,1280]{1,0:T(8,128)(2,1)}, bf16[384,1280]{1,0:T(8,128)(2,1)S(1)}, u32[]{:S(2)}, u32[]{:S(2)}) %collective-permute-start.53) | collective-permute-done | bytes 983072 | tf_op jit(solution)/shard_map/ppermute | solution.py:26
  728.9 4.6 fusion.97
  768.5 4.6 collective-permute-done.72
  787.0 6.3 reshape.405
  793.3 8.2 copy.99
  801.4 7.7 reshape.398
  (545 shorter events, 237.3 us)
Async XLA Ops:
  7.3 68.4 %all-gather.3.cloned.1.call-start = ((), (), s32[]{:S(2)}) async-start(), calls=%async_computation.4 | async-start | bytes 3686400 | tf_op jit(solution)/shard_map/all_gather | solution.py:240
  9.9 219.9 %all-gather.5.cloned.1.call-start = ((), (), s32[]{:S(2)}) async-start(), calls=%async_computation.5 | async-start | bytes 7372800 | tf_op jit(solution)/shard_map/all_gather | solution.py:245
  12.5 25.7 %collective-permute-start.1 = (bf16[384,1280]{1,0:T(8,128)(2,1)S(1)}, bf16[384,1280]{1,0:T(8,128)(2,1)}, u32[]{:S(2)}, u32[]{:S(2)}) collective-permute-start(bf16[384,1280]{1,0:T(8,128)(2,1)S(1)} %get-tuple-element.100), channel_id=1, source_target_pairs={{0,2},{1,3},{2,0},{3,1},{4,6},{5,7},{6,4},{7,5},{8,10},{9,11},{10,... | collective-permute-start | bytes 2949128 | tf_op jit(solution)/shard_map/ppermute | solution.py:26
  15.5 42.9 %collective-permute-start = (bf16[384,1280]{1,0:T(8,128)(2,1)S(1)}, bf16[384,1280]{1,0:T(8,128)(2,1)}, u32[]{:S(2)}, u32[]{:S(2)}) collective-permute-start(bf16[384,1280]{1,0:T(8,128)(2,1)S(1)} %get-tuple-element.100), channel_id=1, source_target_pairs={{0,1},{1,0},{2,3},{3,2},{4,5},{5,4},{6,7},{7,6},{8,9},{9,8},{10,11... | collective-permute-start | bytes 2949128 | tf_op jit(solution)/shard_map/ppermute | solution.py:26
  15.5 42.9 %collective-permute-start.19 = (bf16[384,1280]{1,0:T(8,128)(2,1)}, bf16[384,1280]{1,0:T(8,128)(2,1)}, u32[]{:S(2)}, u32[]{:S(2)}) collective-permute-start(bf16[384,1280]{1,0:T(8,128)(2,1)} %get-tuple-element.99), channel_id=1, source_target_pairs={{0,2},{1,3},{2,0},{3,1},{4,6},{5,7},{6,4},{7,5},{8,10},{9,11},{10,... | collective-permute-start | bytes 2949128 | tf_op jit(solution)/shard_map/ppermute | solution.py:26
  15.6 49.9 %collective-permute-start.18 = (bf16[384,1280]{1,0:T(8,128)(2,1)}, bf16[384,1280]{1,0:T(8,128)(2,1)}, u32[]{:S(2)}, u32[]{:S(2)}) collective-permute-start(bf16[384,1280]{1,0:T(8,128)(2,1)} %get-tuple-element.99), channel_id=1, source_target_pairs={{0,1},{1,0},{2,3},{3,2},{4,5},{5,4},{6,7},{7,6},{8,9},{9,8},{10,11... | collective-permute-start | bytes 2949128 | tf_op jit(solution)/shard_map/ppermute | solution.py:26
  22.2 726.2 %reduce-scatter.9.cloned.1.call-start = ((), (), s32[]{:S(2)}) async-start(), calls=%async_computation.7 | async-start | bytes 3686400 | tf_op jit(solution)/shard_map/reduce_scatter | solution.py:330
  38.2 20.2 %collective-permute-start.2 = (bf16[384,1280]{1,0:T(8,128)(2,1)}, bf16[384,1280]{1,0:T(8,128)(2,1)}, u32[]{:S(2)}, u32[]{:S(2)}) collective-permute-start(bf16[384,1280]{1,0:T(8,128)(2,1)} %collective-permute-done.1), channel_id=1, source_target_pairs={{0,1},{1,0},{2,3},{3,2},{4,5},{5,4},{6,7},{7,6},{8,9},{9,8},{10,11... | collective-permute-start | bytes 2949128 | tf_op jit(solution)/shard_map/ppermute | solution.py:26
  80.8 40.5 %collective-permute-start.10 = (bf16[1280,320]{0,1:T(8,128)(2,1)}, bf16[1280,320]{0,1:T(8,128)(2,1)S(1)}, u32[]{:S(2)}, u32[]{:S(2)}) collective-permute-start(bf16[1280,320]{0,1:T(8,128)(2,1)} %copy.89), channel_id=1, source_target_pairs={{0,2},{1,3},{2,0},{3,1},{4,6},{5,7},{6,4},{7,5},{8,10},{9,11},{10,... | collective-permute-start | bytes 2457608 | tf_op jit(solution)/shard_map/ppermute | solution.py:26
  82.2 78.5 %collective-permute-start.9 = (bf16[1280,320]{0,1:T(8,128)(2,1)}, bf16[1280,320]{0,1:T(8,128)(2,1)}, u32[]{:S(2)}, u32[]{:S(2)}) collective-permute-start(bf16[1280,320]{0,1:T(8,128)(2,1)} %copy.89), channel_id=1, source_target_pairs={{0,1},{1,0},{2,3},{3,2},{4,5},{5,4},{6,7},{7,6},{8,9},{9,8},{10,11... | collective-permute-start | bytes 2457608 | tf_op jit(solution)/shard_map/ppermute | solution.py:26
  110.7 30.9 %collective-permute-start.6 = (bf16[384,320]{1,0:T(8,128)(2,1)S(1)}, bf16[384,320]{1,0:T(8,128)(2,1)S(1)}, u32[]{:S(2)}, u32[]{:S(2)}) collective-permute-start(bf16[384,320]{1,0:T(8,128)(2,1)S(1)} %get-tuple-element.118), channel_id=1, source_target_pairs={{0,1},{1,0},{2,3},{3,2},{4,5},{5,4},{6,7},{7,6},{8,9},{9,8},{10,11... | collective-permute-start | bytes 737288 | tf_op jit(solution)/shard_map/ppermute | solution.py:26
  111.3 30.3 %collective-permute-start.7 = (bf16[384,320]{1,0:T(8,128)(2,1)S(1)}, bf16[384,320]{1,0:T(8,128)(2,1)S(1)}, u32[]{:S(2)}, u32[]{:S(2)}) collective-permute-start(bf16[384,320]{1,0:T(8,128)(2,1)S(1)} %get-tuple-element.117), channel_id=1, source_target_pairs={{0,2},{1,3},{2,0},{3,1},{4,6},{5,7},{6,4},{7,5},{8,10},{9,11},{10,... | collective-permute-start | bytes 737288 | tf_op jit(solution)/shard_map/ppermute | solution.py:26
  111.8 30.4 %collective-permute-start.8 = (bf16[384,320]{1,0:T(8,128)(2,1)S(1)}, bf16[384,320]{1,0:T(8,128)(2,1)S(1)}, u32[]{:S(2)}, u32[]{:S(2)}) collective-permute-start(bf16[384,320]{1,0:T(8,128)(2,1)S(1)} %get-tuple-element.116), channel_id=1, source_target_pairs={{0,3},{1,2},{2,1},{3,0},{4,7},{5,6},{6,5},{7,4},{8,11},{9,10},{10,... | collective-permute-start | bytes 737288 | tf_op jit(solution)/shard_map/ppermute | solution.py:26
  121.3 41.7 %collective-permute-start.11 = (bf16[1280,320]{0,1:T(8,128)(2,1)S(1)}, bf16[1280,320]{0,1:T(8,128)(2,1)}, u32[]{:S(2)}, u32[]{:S(2)}) collective-permute-start(bf16[1280,320]{0,1:T(8,128)(2,1)S(1)} %collective-permute-done.10), channel_id=1, source_target_pairs={{0,1},{1,0},{2,3},{3,2},{4,5},{5,4},{6,7},{7,6},{8,9},{9,8},{10,11... | collective-permute-start | bytes 2457608 | tf_op jit(solution)/shard_map/ppermute | solution.py:26
  184.0 24.9 %collective-permute-start.25 = (bf16[384,1280]{1,0:T(8,128)(2,1)}, bf16[384,1280]{1,0:T(8,128)(2,1)}, u32[]{:S(2)}, u32[]{:S(2)}) collective-permute-start(bf16[384,1280]{1,0:T(8,128)(2,1)} %get-tuple-element.137), channel_id=1, source_target_pairs={{0,2},{1,3},{2,0},{3,1},{4,6},{5,7},{6,4},{7,5},{8,10},{9,11},{10,... | collective-permute-start | bytes 2949128 | tf_op jit(solution)/shard_map/ppermute | solution.py:26
  184.3 45.4 %collective-permute-start.13 = (bf16[384,1280]{1,0:T(8,128)(2,1)S(1)}, bf16[384,1280]{1,0:T(8,128)(2,1)}, u32[]{:S(2)}, u32[]{:S(2)}) collective-permute-start(bf16[384,1280]{1,0:T(8,128)(2,1)S(1)} %get-tuple-element.138), channel_id=1, source_target_pairs={{0,2},{1,3},{2,0},{3,1},{4,6},{5,7},{6,4},{7,5},{8,10},{9,11},{10,... | collective-permute-start | bytes 2949128 | tf_op jit(solution)/shard_map/ppermute | solution.py:26
  186.0 43.8 %collective-permute-start.24 = (bf16[384,1280]{1,0:T(8,128)(2,1)}, bf16[384,1280]{1,0:T(8,128)(2,1)}, u32[]{:S(2)}, u32[]{:S(2)}) collective-permute-start(bf16[384,1280]{1,0:T(8,128)(2,1)} %get-tuple-element.137), channel_id=1, source_target_pairs={{0,1},{1,0},{2,3},{3,2},{4,5},{5,4},{6,7},{7,6},{8,9},{9,8},{10,11... | collective-permute-start | bytes 2949128 | tf_op jit(solution)/shard_map/ppermute | solution.py:26
  208.9 20.9 %collective-permute-start.26 = (bf16[384,1280]{1,0:T(8,128)(2,1)}, bf16[384,1280]{1,0:T(8,128)(2,1)}, u32[]{:S(2)}, u32[]{:S(2)}) collective-permute-start(bf16[384,1280]{1,0:T(8,128)(2,1)} %collective-permute-done.25), channel_id=1, source_target_pairs={{0,1},{1,0},{2,3},{3,2},{4,5},{5,4},{6,7},{7,6},{8,9},{9,8},{10,11... | collective-permute-start | bytes 2949128 | tf_op jit(solution)/shard_map/ppermute | solution.py:26
  209.0 40.3 %collective-permute-start.12 = (bf16[384,1280]{1,0:T(8,128)(2,1)S(1)}, bf16[384,1280]{1,0:T(8,128)(2,1)}, u32[]{:S(2)}, u32[]{:S(2)}) collective-permute-start(bf16[384,1280]{1,0:T(8,128)(2,1)S(1)} %get-tuple-element.138), channel_id=1, source_target_pairs={{0,1},{1,0},{2,3},{3,2},{4,5},{5,4},{6,7},{7,6},{8,9},{9,8},{10,11... | collective-permute-start | bytes 2949128 | tf_op jit(solution)/shard_map/ppermute | solution.py:26
  229.8 19.5 %collective-permute-start.14 = (bf16[384,1280]{1,0:T(8,128)(2,1)}, bf16[384,1280]{1,0:T(8,128)(2,1)}, u32[]{:S(2)}, u32[]{:S(2)}) collective-permute-start(bf16[384,1280]{1,0:T(8,128)(2,1)} %collective-permute-done.13), channel_id=1, source_target_pairs={{0,1},{1,0},{2,3},{3,2},{4,5},{5,4},{6,7},{7,6},{8,9},{9,8},{10,11... | collective-permute-start | bytes 2949128 | tf_op jit(solution)/shard_map/ppermute | solution.py:26
  248.8 18.9 %collective-permute-start.28 = (bf16[384,1280]{1,0:T(8,128)(2,1)S(1)}, bf16[384,1280]{1,0:T(8,128)(2,1)S(1)}, u32[]{:S(2)}, u32[]{:S(2)}) collective-permute-start(bf16[384,1280]{1,0:T(8,128)(2,1)S(1)} %get-tuple-element.71), channel_id=1, source_target_pairs={{0,1},{1,0},{2,3},{3,2},{4,5},{5,4},{6,7},{7,6},{8,9},{9,8},{10,11... | collective-permute-start | bytes 2949128 | tf_op jit(solution)/shard_map/ppermute | solution.py:26
  268.9 24.9 %collective-permute-start.29 = (bf16[384,1280]{1,0:T(8,128)(2,1)}, bf16[384,1280]{1,0:T(8,128)(2,1)}, u32[]{:S(2)}, u32[]{:S(2)}) collective-permute-start(bf16[384,1280]{1,0:T(8,128)(2,1)} %add_convert_fusion.7), channel_id=1, source_target_pairs={{0,2},{1,3},{2,0},{3,1},{4,6},{5,7},{6,4},{7,5},{8,10},{9,11},{10,... | collective-permute-start | bytes 2949128 | tf_op jit(solution)/shard_map/ppermute | solution.py:26
  270.8 43.5 %collective-permute-start.17 = (bf16[384,1280]{1,0:T(8,128)(2,1)}, bf16[384,1280]{1,0:T(8,128)(2,1)}, u32[]{:S(2)}, u32[]{:S(2)}) collective-permute-start(bf16[384,1280]{1,0:T(8,128)(2,1)} %add_convert_fusion.9), channel_id=1, source_target_pairs={{0,2},{1,3},{2,0},{3,1},{4,6},{5,7},{6,4},{7,5},{8,10},{9,11},{10,... | collective-permute-start | bytes 2949128 | tf_op jit(solution)/shard_map/ppermute | solution.py:26
  322.3 24.7 %collective-permute-start.31 = (bf16[384,1280]{1,0:T(8,128)(2,1)S(1)}, bf16[384,1280]{1,0:T(8,128)(2,1)}, u32[]{:S(2)}, u32[]{:S(2)}) collective-permute-start(bf16[384,1280]{1,0:T(8,128)(2,1)S(1)} %get-tuple-element.98), channel_id=1, source_target_pairs={{0,2},{1,3},{2,0},{3,1},{4,6},{5,7},{6,4},{7,5},{8,10},{9,11},{10,... | collective-permute-start | bytes 2949128 | tf_op jit(solution)/shard_map/ppermute | solution.py:26
  322.7 43.9 %collective-permute-start.43 = (bf16[384,1280]{1,0:T(8,128)(2,1)}, bf16[384,1280]{1,0:T(8,128)(2,1)}, u32[]{:S(2)}, u32[]{:S(2)}) collective-permute-start(bf16[384,1280]{1,0:T(8,128)(2,1)} %get-tuple-element.51), channel_id=1, source_target_pairs={{0,2},{1,3},{2,0},{3,1},{4,6},{5,7},{6,4},{7,5},{8,10},{9,11},{10,... | collective-permute-start | bytes 2949128 | tf_op jit(solution)/shard_map/ppermute | solution.py:26
  324.3 42.3 %collective-permute-start.30 = (bf16[384,1280]{1,0:T(8,128)(2,1)S(1)}, bf16[384,1280]{1,0:T(8,128)(2,1)}, u32[]{:S(2)}, u32[]{:S(2)}) collective-permute-start(bf16[384,1280]{1,0:T(8,128)(2,1)S(1)} %get-tuple-element.98), channel_id=1, source_target_pairs={{0,1},{1,0},{2,3},{3,2},{4,5},{5,4},{6,7},{7,6},{8,9},{9,8},{10,11... | collective-permute-start | bytes 2949128 | tf_op jit(solution)/shard_map/ppermute | solution.py:26
  347.0 19.6 %collective-permute-start.32 = (bf16[384,1280]{1,0:T(8,128)(2,1)}, bf16[384,1280]{1,0:T(8,128)(2,1)}, u32[]{:S(2)}, u32[]{:S(2)}) collective-permute-start(bf16[384,1280]{1,0:T(8,128)(2,1)} %collective-permute-done.31), channel_id=1, source_target_pairs={{0,1},{1,0},{2,3},{3,2},{4,5},{5,4},{6,7},{7,6},{8,9},{9,8},{10,11... | collective-permute-start | bytes 2949128 | tf_op jit(solution)/shard_map/ppermute | solution.py:26
  348.9 41.3 %collective-permute-start.42 = (bf16[384,1280]{1,0:T(8,128)(2,1)}, bf16[384,1280]{1,0:T(8,128)(2,1)S(1)}, u32[]{:S(2)}, u32[]{:S(2)}) collective-permute-start(bf16[384,1280]{1,0:T(8,128)(2,1)} %get-tuple-element.51), channel_id=1, source_target_pairs={{0,1},{1,0},{2,3},{3,2},{4,5},{5,4},{6,7},{7,6},{8,9},{9,8},{10,11... | collective-permute-start | bytes 2949128 | tf_op jit(solution)/shard_map/ppermute | solution.py:26
  366.6 23.5 %collective-permute-start.44 = (bf16[384,1280]{1,0:T(8,128)(2,1)}, bf16[384,1280]{1,0:T(8,128)(2,1)S(1)}, u32[]{:S(2)}, u32[]{:S(2)}) collective-permute-start(bf16[384,1280]{1,0:T(8,128)(2,1)} %collective-permute-done.43), channel_id=1, source_target_pairs={{0,1},{1,0},{2,3},{3,2},{4,5},{5,4},{6,7},{7,6},{8,9},{9,8},{10,11... | collective-permute-start | bytes 2949128 | tf_op jit(solution)/shard_map/ppermute | solution.py:26
  389.6 30.0 %collective-permute-start.34 = (bf16[384,1280]{1,0:T(8,128)(2,1)S(1)}, bf16[384,1280]{1,0:T(8,128)(2,1)S(1)}, u32[]{:S(2)}, u32[]{:S(2)}) collective-permute-start(bf16[384,1280]{1,0:T(8,128)(2,1)S(1)} %get-tuple-element.69), channel_id=1, source_target_pairs={{0,1},{1,0},{2,3},{3,2},{4,5},{5,4},{6,7},{7,6},{8,9},{9,8},{10,11... | collective-permute-start | bytes 2949128 | tf_op jit(solution)/shard_map/ppermute | solution.py:26
  390.1 42.1 %collective-permute-start.33 = (bf16[384,1280]{1,0:T(8,128)(2,1)}, bf16[384,1280]{1,0:T(8,128)(2,1)S(1)}, u32[]{:S(2)}, u32[]{:S(2)}) collective-permute-start(bf16[384,1280]{1,0:T(8,128)(2,1)} %get-tuple-element.68), channel_id=1, source_target_pairs={{0,1},{1,0},{2,3},{3,2},{4,5},{5,4},{6,7},{7,6},{8,9},{9,8},{10,11... | collective-permute-start | bytes 2949128 | tf_op jit(solution)/shard_map/ppermute | solution.py:26
  412.5 19.8 %collective-permute-start.45 = (bf16[384,1280]{1,0:T(8,128)(2,1)}, bf16[384,1280]{1,0:T(8,128)(2,1)}, u32[]{:S(2)}, u32[]{:S(2)}) collective-permute-start(bf16[384,1280]{1,0:T(8,128)(2,1)} %get-tuple-element.64), channel_id=1, source_target_pairs={{0,1},{1,0},{2,3},{3,2},{4,5},{5,4},{6,7},{7,6},{8,9},{9,8},{10,11... | collective-permute-start | bytes 2949128 | tf_op jit(solution)/shard_map/ppermute | solution.py:26
  420.8 24.9 %collective-permute-start.35 = (bf16[384,1280]{1,0:T(8,128)(2,1)}, bf16[384,1280]{1,0:T(8,128)(2,1)}, u32[]{:S(2)}, u32[]{:S(2)}) collective-permute-start(bf16[384,1280]{1,0:T(8,128)(2,1)} %add_convert_fusion.6), channel_id=1, source_target_pairs={{0,2},{1,3},{2,0},{3,1},{4,6},{5,7},{6,4},{7,5},{8,10},{9,11},{10,... | collective-permute-start | bytes 2949128 | tf_op jit(solution)/shard_map/ppermute | solution.py:26
  422.5 43.9 %collective-permute-start.47 = (bf16[384,1280]{1,0:T(8,128)(2,1)}, bf16[384,1280]{1,0:T(8,128)(2,1)}, u32[]{:S(2)}, u32[]{:S(2)}) collective-permute-start(bf16[384,1280]{1,0:T(8,128)(2,1)} %add_convert_fusion.4), channel_id=1, source_target_pairs={{0,2},{1,3},{2,0},{3,1},{4,6},{5,7},{6,4},{7,5},{8,10},{9,11},{10,... | collective-permute-start | bytes 2949128 | tf_op jit(solution)/shard_map/ppermute | solution.py:26
  432.2 322.0 %reduce-scatter.13.cloned.1.call-start = ((), (), s32[]{:S(2)}) async-start(), calls=%async_computation.9 | async-start | bytes 1105920
  500.8 20.5 %collective-permute-start.64 = (bf16[1280,320]{0,1:T(8,128)(2,1)S(1)}, bf16[1280,320]{0,1:T(8,128)(2,1)S(1)}, u32[]{:S(2)}, u32[]{:S(2)}) collective-permute-start(bf16[1280,320]{0,1:T(8,128)(2,1)S(1)} %add_convert_fusion.12), channel_id=1, source_target_pairs={{0,2},{1,3},{2,0},{3,1},{4,6},{5,7},{6,4},{7,5},{8,10},{9,11},{10,... | collective-permute-start | bytes 2457608 | tf_op jit(solution)/shard_map/ppermute | solution.py:26
  524.2 231.9 %reduce-scatter.11.cloned.1.call-start = ((), (), s32[]{:S(2)}) async-start(), calls=%async_computation.8 | async-start | bytes 3686400 | tf_op jit(solution)/shard_map/reduce_scatter | solution.py:330
  536.2 238.3 %reduce-scatter.7.cloned.1.call-start = ((), (), s32[]{:S(2)}) async-start(), calls=%async_computation.6 | async-start | bytes 2949120 | tf_op jit(solution)/shard_map/reduce_scatter | solution.py:330
  551.7 62.8 %collective-permute-start.36 = (bf16[384,320]{1,0:T(8,128)(2,1)}, bf16[384,320]{1,0:T(8,128)(2,1)S(1)}, u32[]{:S(2)}, u32[]{:S(2)}) collective-permute-start(bf16[384,320]{1,0:T(8,128)(2,1)} %get-tuple-element.127), channel_id=1, source_target_pairs={{0,1},{1,0},{2,3},{3,2},{4,5},{5,4},{6,7},{7,6},{8,9},{9,8},{10,11... | collective-permute-start | bytes 737288 | tf_op jit(solution)/shard_map/ppermute | solution.py:26
  551.9 62.6 %collective-permute-start.37 = (bf16[384,320]{1,0:T(8,128)(2,1)S(1)}, bf16[384,320]{1,0:T(8,128)(2,1)}, u32[]{:S(2)}, u32[]{:S(2)}) collective-permute-start(bf16[384,320]{1,0:T(8,128)(2,1)S(1)} %get-tuple-element.126), channel_id=1, source_target_pairs={{0,2},{1,3},{2,0},{3,1},{4,6},{5,7},{6,4},{7,5},{8,10},{9,11},{10,... | collective-permute-start | bytes 737288 | tf_op jit(solution)/shard_map/ppermute | solution.py:26
  554.1 60.4 %collective-permute-start.38 = (bf16[384,320]{1,0:T(8,128)(2,1)S(1)}, bf16[384,320]{1,0:T(8,128)(2,1)S(1)}, u32[]{:S(2)}, u32[]{:S(2)}) collective-permute-start(bf16[384,320]{1,0:T(8,128)(2,1)S(1)} %get-tuple-element.125), channel_id=1, source_target_pairs={{0,3},{1,2},{2,1},{3,0},{4,7},{5,6},{6,5},{7,4},{8,11},{9,10},{10,... | collective-permute-start | bytes 737288 | tf_op jit(solution)/shard_map/ppermute | solution.py:26
  613.7 70.2 %collective-permute-start.52 = (bf16[384,1280]{1,0:T(8,128)(2,1)}, bf16[384,1280]{1,0:T(8,128)(2,1)}, u32[]{:S(2)}, u32[]{:S(2)}) collective-permute-start(bf16[384,1280]{1,0:T(8,128)(2,1)} %get-tuple-element.63), channel_id=1, source_target_pairs={{0,1},{1,0},{2,3},{3,2},{4,5},{5,4},{6,7},{7,6},{8,9},{9,8},{10,11... | collective-permute-start | bytes 2949128 | tf_op jit(solution)/shard_map/ppermute | solution.py:26
  614.5 97.3 %collective-permute-start.51 = (bf16[384,1280]{1,0:T(8,128)(2,1)}, bf16[384,1280]{1,0:T(8,128)(2,1)S(1)}, u32[]{:S(2)}, u32[]{:S(2)}) collective-permute-start(bf16[384,1280]{1,0:T(8,128)(2,1)} %get-tuple-element.62), channel_id=1, source_target_pairs={{0,1},{1,0},{2,3},{3,2},{4,5},{5,4},{6,7},{7,6},{8,9},{9,8},{10,11... | collective-permute-start | bytes 2949128 | tf_op jit(solution)/shard_map/ppermute | solution.py:26
  662.5 26.0 %collective-permute-start.39 = (bf16[384,1280]{1,0:T(8,128)(2,1)}, bf16[384,1280]{1,0:T(8,128)(2,1)}, u32[]{:S(2)}, u32[]{:S(2)}) collective-permute-start(bf16[384,1280]{1,0:T(8,128)(2,1)} %get-tuple-element.66), channel_id=1, source_target_pairs={{0,1},{1,0},{2,3},{3,2},{4,5},{5,4},{6,7},{7,6},{8,9},{9,8},{10,11... | collective-permute-start | bytes 2949128 | tf_op jit(solution)/shard_map/ppermute | solution.py:26
  683.3 24.6 %collective-permute-start.41 = (bf16[384,1280]{1,0:T(8,128)(2,1)}, bf16[384,1280]{1,0:T(8,128)(2,1)}, u32[]{:S(2)}, u32[]{:S(2)}) collective-permute-start(bf16[384,1280]{1,0:T(8,128)(2,1)} %add_convert_fusion.5), channel_id=1, source_target_pairs={{0,2},{1,3},{2,0},{3,1},{4,6},{5,7},{6,4},{7,5},{8,10},{9,11},{10,... | collective-permute-start | bytes 2949128 | tf_op jit(solution)/shard_map/ppermute | solution.py:26
  686.7 42.3 %collective-permute-start.53 = (bf16[384,1280]{1,0:T(8,128)(2,1)}, bf16[384,1280]{1,0:T(8,128)(2,1)S(1)}, u32[]{:S(2)}, u32[]{:S(2)}) collective-permute-start(bf16[384,1280]{1,0:T(8,128)(2,1)} %add_convert_fusion.3), channel_id=1, source_target_pairs={{0,2},{1,3},{2,0},{3,1},{4,6},{5,7},{6,4},{7,5},{8,10},{9,11},{10,... | collective-permute-start | bytes 2949128 | tf_op jit(solution)/shard_map/ppermute | solution.py:26
  775.2 33.9 %collective-permute-start.59 = (bf16[160,960]{1,0:T(8,128)(2,1)}, bf16[160,960]{1,0:T(8,128)(2,1)}, u32[]{:S(2)}, u32[]{:S(2)}) collective-permute-start(bf16[160,960]{1,0:T(8,128)(2,1)} %reduce-scatter.7.cloned.1.call-done), channel_id=1, source_target_pairs={{0,1},{1,0},{2,3},{3,2},{4,5},{5,4},{6,7},{7,6},{8,9},{9,8},{10,11... | collective-permute-start | bytes 921608 | tf_op jit(solution)/shard_map/ppermute | solution.py:26
  785.0 24.2 %collective-permute-start.61 = (bf16[160,960]{1,0:T(8,128)(2,1)}, bf16[160,960]{1,0:T(8,128)(2,1)S(1)}, u32[]{:S(2)}, u32[]{:S(2)}) collective-permute-start(bf16[160,960]{1,0:T(8,128)(2,1)} %collective-permute-done.60), channel_id=1, source_target_pairs={{0,1},{1,0},{2,3},{3,2},{4,5},{5,4},{6,7},{7,6},{8,9},{9,8},{10,11... | collective-permute-start | bytes 921608 | tf_op jit(solution)/shard_map/ppermute | solution.py:26
  (139 other events, 1744.5 us)
Sparse Core Ops, SparseCore 0:
  10.9 64.7 all-gather.2
  78.4 100.5 all-gather.4
  432.3 73.8 reduce-scatter.8
  524.3 61.9 reduce-scatter.12
  590.3 75.1 reduce-scatter.10
  688.6 69.4 reduce-scatter.6

commit v2 on v1

--- a/solution.py
+++ b/solution.py
@@ -28,27 +28,55 @@
     )
 
 
-def gather_all(piece):
-    groups = lax.axis_size("seq")
+def gather_low(piece, size):
     blocks = {0: piece}
-    bits = groups // 2
+    bits = size // 2
     while bits:
         for r in sorted(blocks):
             blocks[r | bits] = flip(blocks[r], bits)
         bits //= 2
-    return [blocks[r] for r in range(groups)]
-
-
-def scatter_sum(partial):
+    return [blocks[r] for r in range(size)]
+
+
+def gather_begin(piece):
+    size = lax.axis_size("seq") // 2
+    far = flip(piece, size)
+    return gather_low(piece, size), far
+
+
+def gather_end(far):
+    return gather_low(far, lax.axis_size("seq") // 2)
+
+
+def gather_all(piece):
+    near, far = gather_begin(piece)
+    return near + gather_end(far)
+
+
+def scatter_terms(make, step):
     groups = lax.axis_size("seq")
-    n = partial.shape[0] // groups
-    terms = {r: partial[r * n : (r + 1) * n] for r in range(groups)}
-    bits = 1
-    while bits < groups:
-        for r in reversed(range(0, groups, 2 * bits)):
-            terms[r] = terms[r].astype(single) + flip(terms[r | bits].astype(half), bits).astype(single)
-        bits *= 2
-    return terms[0]
+
+    def terms(base, size):
+        if size == 1:
+            out = make(base)
+            step.mark(out)
+            return [out]
+        near = size // 2
+        high = terms(base + near, near)
+        if len(high) > 1:
+            high = step.after(high[0]).astype(single) + sum(h.astype(single) for h in high[1:])
+            high = high.astype(half)
+            step.mark(high)
+        else:
+            high = high[0]
+        moved = flip(high, near)
+        return terms(base, near) + [moved]
+
+    return terms(0, groups)
+
+
+def add_terms(parts):
+    return sum(p.astype(single) for p in parts)
 
 
 def swap(parts):
@@ -200,6 +228,181 @@
     )(qkv, mask, grad, lse)
 
 
+def norm_kernel(groups, chunk, *refs):
+    blocks, gain_ref, bias_ref, out = refs[:groups], refs[groups], refs[groups + 1], refs[groups + 2]
+    rows = blocks[0].shape[0]
+    for r in range(groups):
+
+        def some(i, carry, r=r):
+            start = pl.multiple_of(i * chunk, chunk)
+            v = blocks[r][pl.ds(start, chunk), :].astype(single)
+            out[pl.ds(r * rows + start, chunk), :] = layer_norm(v, gain_ref[...], bias_ref[...]).astype(half)
+            return carry
+
+        lax.fori_loop(0, rows // chunk, some, 0)
+
+
+def norm_blocks(blocks, gain, bias):
+    groups = len(blocks)
+    rows, width = blocks[0].shape
+    return pl.pallas_call(
+        functools.partial(norm_kernel, groups, 64 if rows % 128 else 128),
+        out_shape=jax.ShapeDtypeStruct((groups * rows, width), half),
+        cost_estimate=pl.CostEstimate(
+            flops=groups * rows * width * 10, bytes_accessed=groups * rows * width * 4, transcendentals=0
+        ),
+        name="norm_blocks",
+    )(*blocks, gain, bias)
+
+
+def products_kernel(pairs, before, beside, *refs):
+    lefts, rights = refs[:pairs], refs[pairs : 2 * pairs]
+    more, out = refs[2 * pairs : -1], refs[-1]
+    total = more[0][...] if before else None
+    for a, b in zip(lefts, rights):
+        term = lax.dot_general(
+            a[...], b[...], (((0,), (0,)), ((), ())), preferred_element_type=single
+        )
+        total = term if total is None else total + term
+    total = total.astype(out.dtype)
+    if beside:
+        total = jnp.concatenate([total, more[-1][...]], axis=1)
+    out[...] = total
+
+
+def products(lefts, rights, kind, before=None, beside=None, into=None, slot=0, slots=1):
+    pairs = len(lefts)
+    rows, cols = lefts[0].shape[1], rights[0].shape[1]
+    tile = next(t for t in (256, 128, rows) if rows % t == 0)
+    depth = sum(a.shape[0] for a in lefts)
+    in_specs = [pl.BlockSpec((a.shape[0], tile), lambda i: (0, i)) for a in lefts]
+    in_specs += [pl.BlockSpec(b.shape, lambda i: (0, 0)) for b in rights]
+    more = []
+    if before is not None:
+        more.append(before)
+        in_specs.append(pl.BlockSpec((tile, cols), lambda i: (i, 0)))
+    if beside is not None:
+        more.append(beside)
+        in_specs.append(pl.BlockSpec((tile, beside.shape[1]), lambda i: (i, 0)))
+        cols += beside.shape[1]
+    body = functools.partial(products_kernel, pairs, before is not None, beside is not None)
+    aliases = {}
+    if into is not None:
+        aliases = {2 * pairs + len(more): 0}
+        more.append(into)
+        in_specs.append(pl.BlockSpec(memory_space=pl.ANY))
+        inner = body
+
+        def body(*refs):
+            inner(*refs[:-2], refs[-1])
+
+    return pl.pallas_call(
+        body,
+        grid=(rows // tile,),
+        in_specs=in_specs,
+        out_specs=pl.BlockSpec((tile, cols), lambda i: (i, slot)),
+        out_shape=jax.ShapeDtypeStruct((rows, cols * slots), kind),
+        input_output_aliases=aliases,
+        compiler_params=pltpu.CompilerParams(vmem_limit_bytes=56 << 20),
+        cost_estimate=pl.CostEstimate(
+            flops=2 * depth * rows * cols, bytes_accessed=2 * depth * (rows + cols), transcendentals=0
+        ),
+        name="products",
+    )(*lefts, *rights, *more)
+
+
+def assemble_kernel(groups, counts, width, me_ref, *refs):
+    pieces, out = refs[:groups], refs[groups]
+    rows = pieces[0].shape[0]
+    for v in range(groups):
+
+        @pl.when(me_ref[0] == v)
+        def _():
+            for g in range(groups):
+                piece = pieces[v ^ g]
+                if counts == 0:
+                    out[g * rows : (g + 1) * rows, :] = piece[...].astype(single)
+            if counts:
+                blocks = [
+                    pieces[v ^ g][:, k * width : (k + 1) * width]
+                    for k in range(counts)
+                    for g in range(groups)
+                ]
+                out[...] = jnp.concatenate(blocks, axis=1).astype(single)
+
+
+def assemble(pieces, counts, me):
+    groups = len(pieces)
+    rows, cols = pieces[0].shape
+    shape = (rows, cols * groups) if counts else (rows * groups, cols)
+    return pl.pallas_call(
+        functools.partial(assemble_kernel, groups, counts, cols // max(counts, 1)),
+        out_shape=jax.ShapeDtypeStruct(shape, single),
+        in_specs=[pl.BlockSpec(memory_space=pltpu.SMEM)]
+        + [pl.BlockSpec(memory_space=pltpu.VMEM)] * groups,
+        cost_estimate=pl.CostEstimate(
+            flops=0, bytes_accessed=rows * cols * groups * 6, transcendentals=0
+        ),
+        name="assemble",
+    )(me.astype(jnp.int32).reshape(1), *pieces)
+
+
+def gather_blocks_kernel(groups, me_ref, *refs):
+    pieces, out = refs[:groups], refs[groups]
+    span = pieces[0].shape[1]
+    for v in range(groups):
+
+        @pl.when(me_ref[0] == v)
+        def _():
+            for r in range(groups):
+                rows = [
+                    pieces[v ^ g][(v ^ r) * span : ((v ^ r) + 1) * span, :] for g in range(groups)
+                ]
+                out[r * span : (r + 1) * span, :] = jnp.concatenate(rows, axis=1)
+
+
+def scatter_blocks_kernel(groups, me_ref, full, *outs):
+    span = outs[0].shape[1]
+    for v in range(groups):
+
+        @pl.when(me_ref[0] == v)
+        def _():
+            for r in range(groups):
+                for g in range(groups):
+                    outs[r][g * span : (g + 1) * span, :] = full[
+                        (v ^ g) * span : ((v ^ g) + 1) * span, (v ^ r) * span : ((v ^ r) + 1) * span
+                    ]
+
+
+def arrange(kernel, arrays, shapes, groups, me, name):
+    return pl.pallas_call(
+        functools.partial(kernel, groups),
+        out_shape=shapes,
+        in_specs=[pl.BlockSpec(memory_space=pltpu.SMEM)]
+        + [pl.BlockSpec(memory_space=pltpu.VMEM)] * len(arrays),
+        cost_estimate=pl.CostEstimate(
+            flops=0, bytes_accessed=sum(x.size for x in arrays) * 4, transcendentals=0
+        ),
+        name=name,
+    )(me.astype(jnp.int32).reshape(1), *arrays)
+
+
+class Order:
+    def __init__(self):
+        self.tokens = []
+
+    def after(self, tensor):
+        if not self.tokens:
+            return tensor
+        return lax.optimization_barrier((tensor, *self.tokens))[0]
+
+    def mark(self, *tensors):
+        self.tokens = list(tensors)
+
+    def also(self, *tensors):
+        self.tokens += tensors
+
+
 def local(
     frames_in, teacher, lengths, norm1_gain, norm1_bias, w_qkv, query_bias, value_bias,
     w_attn_out, attn_out_bias, norm2_gain, norm2_bias, w_up, up_bias, w_down, down_bias,
@@ -230,15 +433,23 @@
     def columns(array, start, size):
         return lax.dynamic_slice_in_dim(array, start, size, 1)
 
-    states = [gather_all(frames_in[c]) for c in range(clips)]
-
+    def butterfly(array):
+        bits = 1
+        while bits < owners:
+            array = jnp.concatenate([array, flip(array, bits, "fsdp")], axis=0)
+            bits *= 2
+        return [
+            lax.dynamic_index_in_dim(array, own ^ f, 0, keepdims=False) for f in range(owners)
+        ]
+
+    ff = owners * part
     first = jnp.concatenate(
         [columns(w_qkv, k * width + me * span, span) for k in range(3)]
         + [columns(w_attn_out, me * span, span)],
         axis=1,
     )
     first = lax.all_gather(first, "fsdp", axis=0, tiled=True)
-    ff = owners * part
+    wqkv = first[:, : 3 * span]
     wup = jnp.concatenate([columns(w_up, f * units + me * part, part) for f in range(owners)], axis=1)
     wdown = lax.dynamic_slice_in_dim(w_down, me * part, part, 0)
     if part == depth:
@@ -247,17 +458,19 @@
     else:
         wup = lax.all_gather(wup, "fsdp", axis=0, tiled=True)
         wdown = lax.all_gather(wdown, "fsdp", axis=0, tiled=True)
-    wqkv = first[:, : 3 * span]
+
+    states = []
+    for c in range(clips):
+        piece = frames_in[c]
+        if states:
+            piece = lax.optimization_barrier((piece, states[-1][0][-1]))[0]
+        states.append(gather_begin(piece))
 
     packed = jnp.concatenate(
         [norm1_gain, norm1_bias, query_bias, value_bias, attn_out_bias, norm2_gain, norm2_bias,
          down_bias, up_bias]
     )[None]
-    bits = 1
-    while bits < owners:
-        packed = jnp.concatenate([packed, flip(packed, bits, "fsdp")], axis=0)
-        bits *= 2
-    vectors = jnp.take(packed, own ^ jnp.arange(owners), axis=0).astype(single)
+    vectors = jnp.stack(butterfly(packed)).astype(single)
 
     def vector(k):
         return vectors[:, k * depth : (k + 1) * depth].reshape(1, width)
@@ -269,13 +482,7 @@
         axis=1,
     )
 
-    quarters = jnp.stack(gather_all(first[:, 3 * span :]))
-    wout = jnp.concatenate(
-        [lax.dynamic_index_in_dim(quarters, me ^ g, 0, keepdims=False) for g in range(groups)], axis=1
-    )
-    wout = jnp.concatenate(
-        [lax.dynamic_slice_in_dim(wout, (me ^ r) * span, span, 0) for r in range(groups)], axis=0
-    )
+    quarters = gather_all(first[:, 3 * span :])
 
     mine = lax.dynamic_slice_in_dim(lengths, own * clips, clips)
     order = (me ^ jnp.arange(groups, dtype=jnp.int32))[:, None] * frames + jnp.arange(
@@ -289,94 +496,196 @@
     ]
     row_valid = [(order[:frames] < mine[c]).astype(single)[:, None] for c in range(clips)]
 
-    full1, qkvs, sums, contexts, middles, full2 = [], [], [], [], [], []
-    for c in range(clips):
-        state = jnp.concatenate(states[c], axis=0).astype(single)
-        hidden = layer_norm(state, gain1, bias1).astype(half)
-        qkv = (dot(hidden, wqkv) + qkv_bias).astype(half)
-        context, lse = attend(qkv, masks[c], heads, dim, scale)
-        full1.append(hidden)
-        qkvs.append(qkv)
-        sums.append(lse)
-        context = swap([context[r * frames : (r + 1) * frames] for r in range(groups)])
-        contexts.append(jnp.concatenate(context, axis=1))
-    for c in range(clips):
-        middle = frames_in[c].astype(single) + dot(contexts[c], wout) + obias
-        hidden = layer_norm(middle, gain2, bias2).astype(half)
-        middles.append(middle)
-        full2.append(jnp.concatenate(gather_all(hidden), axis=0))
-    actives, slopes, branches = [], [], []
-    for c in range(clips):
-        upper = dot(full2[c], wup) + ubias
-        cdf = 0.5 * (1.0 + lax.erf(upper * math.sqrt(0.5)))
-        actives.append((upper * cdf).astype(half))
-        slopes.append(
-            (cdf + upper * (jnp.exp(-0.5 * upper * upper) * (1.0 / math.sqrt(2.0 * math.pi)))).astype(half)
-        )
-        branches.append(scatter_sum(dot(actives[c], wdown).astype(half)))
-    outs, losses, grad_outs, fulls = [], [], [], []
-    for c in range(clips):
-        result = middles[c] + branches[c] + dbias
-        outs.append(result.astype(half))
-        diff = result - teacher[c].astype(single)
-        masked = diff * row_valid[c]
-        losses.append(jnp.sum(masked * diff) / (2.0 * width * count))
-        grad_out = masked * (float(lengths.shape[0] * seq_len) / count)
-        grad_outs.append(grad_out)
-        fulls.append(jnp.concatenate(gather_all(grad_out.astype(half)), axis=0))
-    frames_out = jnp.stack(outs)
+    step = Order()
+
+    n = frames
+    every = range(clips)
+    full1 = [None] * clips
+    qkvs, sums, moved, contexts = ([None] * clips for _ in range(4))
+    middles, hiddens, actives, slopes, branches = ([None] * clips for _ in range(5))
+    outs, losses, grad_outs, pieces = ([None] * clips for _ in range(4))
+    grad_uppers, grad_hidden2, grad_middles, grad_branches = ([None] * clips for _ in range(4))
+    grad_heads, grad_qkvs, grad_hidden1, grads_in = ([None] * clips for _ in range(4))
+    norm2_grads, norm1_grads = [None] * clips, [None] * clips
+
+    def rows_of(array, r):
+        return array[r * n : (r + 1) * n]
 
     def owned(grad):
-        return lax.psum_scatter(grad.astype(half), "fsdp", scatter_dimension=0, tiled=True)
-
-    grad_wdown = owned(sum(t_dot(actives[c], fulls[c]) for c in range(clips)))
-    grad_dbias = sum(jnp.sum(g.astype(half).astype(single), axis=0) for g in grad_outs)
-    grad_uppers = [
-        (dot_t(fulls[c], wdown) * slopes[c].astype(single)).astype(half) for c in range(clips)
-    ]
-    grad_hidden2 = [scatter_sum(dot_t(grad_uppers[c], wup).astype(half)) for c in range(clips)]
-    grad_wup = owned(sum(t_dot(full2[c], grad_uppers[c]) for c in range(clips)))
-    grad_ubias = sum(jnp.sum(g.astype(single), axis=0) for g in grad_uppers)
+        return lax.psum_scatter(grad, "fsdp", scatter_dimension=0, tiled=True)
 
     def norm_back(v, gain, bias, grad):
         _, back = jax.vjp(layer_norm, v, gain, bias)
         return back(grad)
 
-    grad_gain2 = grad_bias2 = 0.0
-    grad_middles, grad_branches, grad_heads = [], [], []
-    for c in range(clips):
-        gm, gg, gb = norm_back(middles[c], gain2, bias2, grad_hidden2[c])
-        grad_gain2 += gg
-        grad_bias2 += gb
-        grad_middles.append(grad_outs[c] + gm)
-        branch = grad_middles[c].astype(half)
-        grad_branches.append(branch)
-        grad_context = dot_t(branch, wout).astype(half)
-        grad_context = swap([grad_context[:, r * span : (r + 1) * span] for r in range(groups)])
-        grad_heads.append(jnp.concatenate(grad_context, axis=0))
+    def arriving(store, c):
+        near, far = store[c]
+        yield from near
+        far = gather_end(step.after(far))
+        store[c] = near + far
+        yield from far
+
+    def norm1(c):
+        near, far = states[c]
+        full1[c] = norm_blocks(near + gather_end(step.after(far)), gain1, bias1)
+        step.mark(full1[c])
+
+    def attention(c):
+        qkvs[c] = (dot(step.after(full1[c]), wqkv) + qkv_bias).astype(half)
+        context, sums[c] = attend(qkvs[c], masks[c], heads, dim, scale)
+        parts = [rows_of(context, r) for r in range(groups)]
+        step.mark(*parts)
+        moved[c] = swap(parts)
+
+    def project(c):
+        contexts[c] = jnp.concatenate([step.after(moved[c][0])] + moved[c][1:], axis=1)
+        middles[c] = frames_in[c].astype(single) + dot(contexts[c], wout) + obias
+        hidden = layer_norm(middles[c], gain2, bias2).astype(half)
+        step.mark(hidden)
+        hiddens[c] = gather_begin(hidden)
+
+    def up(c):
+        actives[c], slopes[c] = [], []
+        for block in arriving(hiddens, c):
+            upper = dot(step.after(block), wup) + ubias
+            cdf = 0.5 * (1.0 + lax.erf(upper * math.sqrt(0.5)))
+            actives[c].append((upper * cdf).astype(half))
+            slopes[c].append(
+                (cdf + upper * (jnp.exp(-0.5 * upper * upper) * (1.0 / math.sqrt(2.0 * math.pi)))).astype(half)
+            )
+            step.mark(actives[c][-1])
+
+    def down(c):
+        branches[c] = scatter_terms(
+            lambda r: dot(step.after(actives[c][r]), wdown).astype(half), step
+        )
+
+    def loss(c):
+        result = step.after(middles[c]) + add_terms(branches[c]) + dbias
+        outs[c] = result.astype(half)
+        diff = result - teacher[c].astype(single)
+        masked = diff * row_valid[c]
+        losses[c] = jnp.sum(masked * diff) / (2.0 * width * count)
+        grad_outs[c] = masked * (float(lengths.shape[0] * seq_len) / count)
+        branch = grad_outs[c].astype(half)
+        step.mark(branch)
+        pieces[c] = gather_begin(branch)
+
+    def back_up(c):
+        grad_uppers[c] = []
+        for block in arriving(pieces, c):
+            grad = dot_t(step.after(block), wdown) * slopes[c][len(grad_uppers[c])].astype(single)
+            grad_uppers[c].append(grad.astype(half))
+            step.mark(grad_uppers[c][-1])
+
+    def back_down(c):
+        grad_hidden2[c] = scatter_terms(
+            lambda r: dot_t(step.after(grad_uppers[c][r]), wup).astype(half), step
+        )
+
+    def norm2(c):
+        gm, *norm2_grads[c] = norm_back(
+            step.after(middles[c]), gain2, bias2, add_terms(grad_hidden2[c])
+        )
+        grad_middles[c] = grad_outs[c] + gm
+        grad_branches[c] = grad_middles[c].astype(half)
+        grad_context = dot_t(grad_branches[c], wout).astype(half)
+        parts = [grad_context[:, r * span : (r + 1) * span] for r in range(groups)]
+        step.mark(*parts)
+        grad_heads[c] = swap(parts)
+
+    def attention_back(c):
+        grad_head = jnp.concatenate([step.after(grad_heads[c][0])] + grad_heads[c][1:], axis=0)
+        grad_qkvs[c] = attend_back(qkvs[c], masks[c], grad_head, sums[c], heads, dim, scale)
+        step.mark(grad_qkvs[c])
+
+    def hidden_back(c):
+        grad_hidden1[c] = scatter_terms(
+            lambda r: dot_t(rows_of(step.after(grad_qkvs[c]), r), wqkv).astype(half), step
+        )
+
+    def norm1_back(c):
+        gs, *norm1_grads[c] = norm_back(
+            step.after(frames_in[c]).astype(single), gain1, bias1, add_terms(grad_hidden1[c])
+        )
+        grads_in[c] = grad_middles[c] + gs
+        step.mark(grads_in[c])
+
+    first_clip, *others = every
+    for c in every:
+        norm1(c)
+    attention(first_clip)
+    wout = arrange(
+        gather_blocks_kernel, quarters, jax.ShapeDtypeStruct((width, width), half), groups, me,
+        "place_output_weight",
+    )
+    for c in others:
+        attention(c)
+    for c in every:
+        project(c)
+    for c in every:
+        up(c)
+        down(c)
+    for c in every:
+        loss(c)
+    for c in every:
+        back_up(c)
+        back_down(c)
+
+    def flat(store):
+        return [x for blocks in store for x in blocks]
+
+    def ordered(lefts):
+        return [step.after(lefts[0])] + lefts[1:]
+
+    joined = part == depth
+    grad_wdown = products(ordered(flat(actives)), flat(pieces), half, slots=1 + joined)
+    step.mark(grad_wdown)
+    norm2(first_clip)
+    grad_wup = products(
+        ordered(flat(hiddens)), flat(grad_uppers), half,
+        **(dict(into=grad_wdown, slot=1, slots=2) if joined else {}),
+    )
+    step.mark(grad_wup)
+    if joined:
+        both = owned(grad_wup)
+        grad_wdown, grad_wup = both[:, :width], both[:, width:]
+    else:
+        grad_wdown, grad_wup = owned(grad_wdown), owned(grad_wup)
+    for c in others:
+        norm2(c)
+    grad_wout = products(ordered(contexts), grad_branches, half)
+    step.mark(grad_wout)
+    quarters = arrange(
+        scatter_blocks_kernel, [grad_wout],
+        [jax.ShapeDtypeStruct((width, span), half)] * groups, groups, me, "split_output_weight",
+    )
+    attention_back(first_clip)
+    hidden_back(first_clip)
+    early = products(ordered(full1[:-1]), grad_qkvs[:-1], single)
+    step.mark(early)
+    grad_wout = scatter_terms(lambda r: quarters[r], Order())
+    grad_wout = add_terms([step.after(grad_wout[0])] + grad_wout[1:]).astype(half)
+    step.mark(grad_wout)
+    for c in others:
+        attention_back(c)
+    step.also(grad_wup)
+    total = products(ordered(full1[-1:]), grad_qkvs[-1:], half, before=early, beside=grad_wout)
+    step.mark(total)
+    total = owned(total)
+    grad_wqkv, grad_wout = total[:, : 3 * span], total[:, 3 * span :]
+    for c in others:
+        hidden_back(c)
+    for c in every:
+        norm1_back(c)
+    frames_out = jnp.stack(outs)
+    grad_in = jnp.stack(grads_in)
+    grad_gain1, grad_bias1 = (sum(g) for g in zip(*norm1_grads))
+    grad_gain2, grad_bias2 = (sum(g) for g in zip(*norm2_grads))
+    grad_dbias = sum(jnp.sum(g.astype(half).astype(single), axis=0) for g in grad_outs)
+    grad_ubias = sum(jnp.sum(g.astype(single), axis=0) for blocks in grad_uppers for g in blocks)
     grad_obias = sum(jnp.sum(g.astype(single), axis=0) for g in grad_branches)
-
-    grad_wout = sum(t_dot(contexts[c], grad_branches[c]) for c in range(clips)).astype(half)
-    grad_wout = jnp.concatenate(
-        [lax.dynamic_slice_in_dim(grad_wout, (me ^ g) * span, span, 0) for g in range(groups)], axis=0
-    )
-    quarter = jnp.concatenate([columns(grad_wout, (me ^ r) * span, span) for r in range(groups)], axis=0)
-    grad_wout = owned(scatter_sum(quarter))
-
-    grad_qkvs = [
-        attend_back(qkvs[c], masks[c], grad_heads[c], sums[c], heads, dim, scale) for c in range(clips)
-    ]
-    grad_wqkv = owned(sum(t_dot(full1[c], grad_qkvs[c]) for c in range(clips)))
     grad_qkv_bias = sum(jnp.sum(g.astype(single), axis=0) for g in grad_qkvs)
-    grad_hidden1 = [scatter_sum(dot_t(grad_qkvs[c], wqkv).astype(half)) for c in range(clips)]
-    grad_gain1 = grad_bias1 = 0.0
-    grads_in = []
-    for c in range(clips):
-        gs, gg, gb = norm_back(frames_in[c].astype(single), gain1, bias1, grad_hidden1[c])
-        grad_gain1 += gg
-        grad_bias1 += gb
-        grads_in.append(grad_middles[c] + gs)
-    grad_in = jnp.stack(grads_in)
 
     def rows8(v):
         return v.reshape(owners, depth)
@@ -404,13 +713,10 @@
     small_up = rows[8 * depth : 8 * depth + units]
     clip_loss = rows[8 * depth + units :]
 
-    def whole(piece):
-        return jnp.take(jnp.stack(gather_all(piece)), me ^ jnp.arange(groups), axis=0).astype(single)
-
-    grad_wqkv = whole(grad_wqkv).reshape(groups, depth, 3, span).transpose(1, 2, 0, 3).reshape(depth, 3 * width)
-    grad_wout = whole(grad_wout).transpose(1, 0, 2).reshape(depth, width)
-    grad_wup = whole(grad_wup).reshape(groups, depth, owners, part).transpose(1, 2, 0, 3).reshape(depth, owners * units)
-    grad_wdown = whole(grad_wdown).reshape(units, width)
+    grad_wdown = assemble(gather_all(grad_wdown), 0, me)
+    grad_wup = assemble(gather_all(grad_wup), owners, me)
+    grad_wqkv = assemble(gather_all(grad_wqkv), 3, me)
+    grad_wout = assemble(gather_all(grad_wout), 1, me)
     return (
         frames_out, clip_loss, grad_in, small[0], small[1], grad_wqkv, small[2], small[3],
         grad_wout, small[4], small[5], small[6], grad_wup, small_up, grad_wdown, small[7],

time: 842 us -> 715 us (0.85)
  Pallas kernels: 113 us -> 217 us
  waiting for transfers between devices: 264 us -> 161 us
  local copies, waits for them, and re-layouts: 113 us -> 62.3 us
  matrix products: 176 us -> 134 us
  other arithmetic: 103 us -> 72 us
    ppermute x74, waiting for transfers between devices: 259 us -> 135 us  [flip(): lax.ppermute(tensor, axis, [(i, i ^ bits) for i in range(lax.axis_size(ax...]
    pallas_call x0 -> x13, Pallas kernels: none -> 105 us  [the longest x5 67.7 us: products(): pl.pallas_call(body, grid=(rows // tile,), in_specs=in_specs, out_specs=p...]
    dot_general x8 -> x0, matrix products: 57 us -> none  [t_dot(): lax.dot_general(a, b, (((0,), (0,)), ((), ())), preferred_element_type=si...]
    reshape x6 -> x0, local copies, waits for them, and re-layouts: 31.3 us -> none  [the longest x3 22.1 us: local(): whole(grad_wup).reshape(groups, depth, owners, part).transpose(1, 2, 0, 3)]
    dot_general x8 -> x20, matrix products: 54.9 us -> 71 us  [dot(): return jnp.dot(a, b, preferred_element_type=single)]
    all_gather x1, waiting for transfers between devices: 0.02 us -> 14.9 us  [local(): lax.all_gather(jnp.concatenate([wup, wdown], axis=1), 'fsdp', axis=0, til...]
    concatenate x4 -> x2, local copies, waits for them, and re-layouts: 18.8 us -> 4.91 us  [project(): jnp.concatenate([step.after(moved[c][0])] + moved[c][1:], axis=1)]
    reduce_scatter x3 -> x2, waiting for transfers between devices: 0.02 us -> 8.45 us  [owned(): return lax.psum_scatter(grad, 'fsdp', scatter_dimension=0, tiled=True)]
  transfers between devices with their start and end apart: 80 -> 78, of which waited for: 25 -> 22; matrix products, arithmetic and copies ran while one was open for 43% -> 32% of each run, Pallas kernels for 14% -> 27%
where the time goes in v2:
time: 715 us; the launch traced here: 710 us
  Pallas kernels  217 us (30%)
  waiting for transfers between devices  161 us (23%)
  matrix products  134 us (19%)
  other arithmetic  72 us (10%)
  local copies, waits for them, and re-layouts  62.3 us (9%)
  starting transfers between devices  46.3 us (6%)
  between operations  17.9 us (3%)
    ppermute x74, waiting for transfers between devices, flip(): lax.ppermute(tensor, axis, [(i, i ^ bits) for i in range(lax.axis_size(ax...  135 us
    pallas_call x2, Pallas kernels, attend_back(): pl.pallas_call(functools.partial(attend_back_kernel, heads, dim, block, s...  74.3 us
    dot_general x20, matrix products, dot(): return jnp.dot(a, b, preferred_element_type=single)  71 us
    pallas_call x5, Pallas kernels, products(): pl.pallas_call(body, grid=(rows // tile,), in_specs=in_specs, out_specs=p...  67.7 us
    dot_general x26, matrix products, dot_t(): lax.dot_general(a, b, (((1,), (1,)), ((), ())), preferred_element_type=si...  63.1 us
    ppermute x74, starting transfers between devices, flip(): lax.ppermute(tensor, axis, [(i, i ^ bits) for i in range(lax.axis_size(ax...  46.2 us
    pallas_call x2, Pallas kernels, attend(): pl.pallas_call(functools.partial(attend_kernel, heads, dim, block, scale)...  37.5 us
    pallas_call x2, Pallas kernels, norm_blocks(): pl.pallas_call(functools.partial(norm_kernel, groups, 64 if rows % 128 el...  15.7 us
  transfers between devices with their start and end apart: 78, of which 22 were waited for; matrix products, arithmetic and copies ran while one was open for 32% of the time, Pallas kernels for 27%

profile of v2, /device:TPU:0, one launch (start us, length us, event | category | flops | bytes accessed | tf_op | source)
XLA Modules:
  0.0 710.4 jit_solution(7362039518469787173)
XLA Ops:
  23.9 16.6 %collective-permute-done.1.refs_2_ = bf16[384,1280]{1,0:T(8,128)(2,1)} collective-permute-done((bf16[384,1280]{1,0:T(8,128)(2,1)S(1)}, bf16[384,1280]{1,0:T(8,128)(2,1)}, u32[]{:S(2)}, u32[]{:S(2)}) %collective-permute-start.1) | collective-permute-done | bytes 983072 | tf_op jit(solution)/shard_map/ppermute | solution.py:26
  47.7 8.2 %norm_blocks.2.refs_0_ = bf16[1536,1280]{1,0:T(8,128)(2,1)} custom-call(bf16[384,1280]{1,0:T(8,128)(2,1)} %copy-done.13, bf16[384,1280]{1,0:T(8,128)(2,1)} %collective-permute-done.refs_1_, bf16[384,1280]{1,0:T(8,128)(2,1)} %collective-permute-done.1.refs_2_, bf16[384,1280]{1,0:T(8,128)(2,1)} %collective-permute-done.2.refs_3_, f32[1,1280]{1,0:T(1,128)} %reshape.366.refs_4_, ...), custom_call_target="tpu_custom_call" | custom-call | flops 19660800 | bytes 7864320 | tf_op jit(solution)/shard_map/norm_blocks/pallas_call | solution.py:248
  55.8 5.4 collective-permute-done.7.refs_2_
  65.1 7.6 %norm_blocks.3.refs_0_ = bf16[1536,1280]{1,0:T(8,128)(2,1)} custom-call(bf16[384,1280]{1,0:T(8,128)(2,1)} %copy-done.11, bf16[384,1280]{1,0:T(8,128)(2,1)} %collective-permute-done.6.refs_1_, bf16[384,1280]{1,0:T(8,128)(2,1)} %collective-permute-done.7.refs_2_, bf16[384,1280]{1,0:T(8,128)(2,1)} %copy-done.55, f32[1,1280]{1,0:T(1,128)} %reshape.366.refs_4_, ...), custom_call_target="tpu_custom_call" | custom-call | flops 19660800 | bytes 7864320 | tf_op jit(solution)/shard_map/norm_blocks/pallas_call | solution.py:248
  79.7 7.2 %add_convert_fusion.1.qkv_ref = bf16[1536,960]{1,0:T(8,128)(2,1)S(1)} fusion(bf16[1536,1280]{1,0:T(8,128)(2,1)} %norm_blocks.2.refs_0_, f32[960]{0:T(1024)S(1)} %bitcast.98, bf16[1280,1280]{1,0:T(8,128)(2,1)} %all-gather.3.cloned.1.call-done), kind=kOutput, calls=%fused_computation.4 | convolution fusion | flops 3777822720 | bytes 9506560 | tf_op jit(solution)/shard_map/dot_general | solution.py:425
  86.9 18.9 %attend.2 = (bf16[1536,320]{1,0:T(8,128)(2,1)S(1)}, f32[1536,4]{1,0:T(8,128)S(1)}) custom-call(bf16[1536,960]{1,0:T(8,128)(2,1)S(1)} %add_convert_fusion.1.qkv_ref, bf16[1536,48]{1,0:T(8,128)(2,1)S(1)} %get-tuple-element.254.mask_ref), custom_call_target="tpu_custom_call" | custom-call | flops 9663676416 | bytes 4423680 | tf_op jit(solution)/shard_map/attend/pallas_call | solution.py:192
  107.8 4.5 add_convert_fusion.qkv_ref
  112.9 18.7 %attend.3 = (bf16[1536,320]{1,0:T(8,128)(2,1)S(1)}, f32[1536,4]{1,0:T(8,128)S(1)}) custom-call(bf16[1536,960]{1,0:T(8,128)(2,1)S(1)} %add_convert_fusion.qkv_ref, bf16[1536,48]{1,0:T(8,128)(2,1)S(1)} %get-tuple-element.253.mask_ref), custom_call_target="tpu_custom_call" | custom-call | flops 9663676416 | bytes 4423680 | tf_op jit(solution)/shard_map/attend/pallas_call | solution.py:192
  143.8 4.5 place_output_weight.1
  148.4 3.5 fusion.152
  158.2 4.1 fusion.153
  163.1 14.9 %all-gather.5.cloned.1.call-done = bf16[1280,2560]{1,0:T(8,128)(2,1)} async-done(((bf16[160,2560]{1,0:T(8,128)(2,1)}), bf16[1280,2560]{1,0:T(8,128)(2,1)}) %all-gather.5.cloned.1.call-update) | async-done | bytes 6553616 | tf_op jit(solution)/shard_map/all_gather | solution.py:456
  178.0 5.2 multiply_convert_fusion.7
  183.2 4.5 multiply_convert_fusion.6
  187.7 4.5 multiply_convert_fusion.5
  212.5 8.5 %collective-permute-done.23.refs_6_ = bf16[384,1280]{1,0:T(8,128)(2,1)S(1)} collective-permute-done((bf16[384,1280]{1,0:T(8,128)(2,1)S(1)}, bf16[384,1280]{1,0:T(8,128)(2,1)S(1)}, u32[]{:S(2)}, u32[]{:S(2)}) %collective-permute-start.23) | collective-permute-done | bytes 983072 | tf_op jit(solution)/shard_map/ppermute | solution.py:26
  221.0 3.5 multiply_convert_fusion.1
  233.3 3.7 convolution_convert_fusion.20
  240.1 4.4 convolution_convert_fusion.19
  246.1 3.8 convolution_convert_fusion.18
  249.9 6.7 collective-permute-done.27
  260.7 16.9 %collective-permute-done.29 = bf16[384,1280]{1,0:T(8,128)(2,1)} collective-permute-done((bf16[384,1280]{1,0:T(8,128)(2,1)}, bf16[384,1280]{1,0:T(8,128)(2,1)}, u32[]{:S(2)}, u32[]{:S(2)}) %collective-permute-start.29) | collective-permute-done | bytes 983072 | tf_op jit(solution)/shard_map/ppermute | solution.py:26
  277.6 3.7 fusion.27
  287.9 9.8 %collective-permute-done.31.refs_10_ = bf16[384,1280]{1,0:T(8,128)(2,1)S(1)} collective-permute-done((bf16[384,1280]{1,0:T(8,128)(2,1)S(1)}, bf16[384,1280]{1,0:T(8,128)(2,1)S(1)}, u32[]{:S(2)}, u32[]{:S(2)}) %collective-permute-start.31) | collective-permute-done | bytes 983072 | tf_op jit(solution)/shard_map/ppermute | solution.py:26
  317.9 10.4 %collective-permute-done.35.refs_14_ = bf16[384,1280]{1,0:T(8,128)(2,1)S(1)} collective-permute-done((bf16[384,1280]{1,0:T(8,128)(2,1)S(1)}, bf16[384,1280]{1,0:T(8,128)(2,1)S(1)}, u32[]{:S(2)}, u32[]{:S(2)}) %collective-permute-start.35) | collective-permute-done | bytes 983072 | tf_op jit(solution)/shard_map/ppermute | solution.py:26
  343.1 19.7 %products.5.refs_16_ = bf16[1280,2560]{1,0:T(8,128)(2,1)} custom-call(bf16[384,1280]{1,0:T(8,128)(2,1)} %copy-done.126, bf16[384,1280]{1,0:T(8,128)(2,1)} %copy-done.127, bf16[384,1280]{1,0:T(8,128)(2,1)} %copy-done.128, bf16[384,1280]{1,0:T(8,128)(2,1)} %copy-done.129, bf16[384,1280]{1,0:T(8,128)(2,1)} %get-tuple-element.113.refs_4_, ...), custom_call_target="tpu_custom_call" | custom-call | flops 10066329600 | bytes 15728640 | tf_op jit(solution)/shard_map/products/pallas_call | solution.py:299
  366.7 3.4 multiply_reduce_fusion.1
  378.4 20.1 %products.6 = bf16[1280,2560]{1,0:T(8,128)(2,1)} custom-call(bf16[384,1280]{1,0:T(8,128)(2,1)} %add_convert_fusion.11.refs_0_, bf16[384,1280]{1,0:T(8,128)(2,1)} %collective-permute-done.18.refs_1_, bf16[384,1280]{1,0:T(8,128)(2,1)} %collective-permute-done.19.refs_2_, bf16[384,1280]{1,0:T(8,128)(2,1)} %copy-done.106, ...), custom_call_target="tpu_custom_call", output_to_operand_aliasing={{}: (16, {})} | custom-call | flops 10066329600 | bytes 15728640 | tf_op jit(solution)/shard_map/products/pallas_call | solution.py:299
  406.3 20.6 %collective-permute-done.39 = bf16[384,1280]{1,0:T(8,128)(2,1)} collective-permute-done((bf16[384,1280]{1,0:T(8,128)(2,1)}, bf16[384,1280]{1,0:T(8,128)(2,1)}, u32[]{:S(2)}, u32[]{:S(2)}) %collective-permute-start.39) | collective-permute-done | bytes 983072 | tf_op jit(solution)/shard_map/ppermute | solution.py:26
  439.2 7.7 %products.7.full = bf16[1280,1280]{1,0:T(8,128)(2,1)} custom-call(bf16[384,1280]{1,0:T(8,128)(2,1)} %copy-done.46, bf16[384,1280]{1,0:T(8,128)(2,1)} %copy-done.47, bf16[384,1280]{1,0:T(8,128)(2,1)} %copy-done.49, bf16[384,1280]{1,0:T(8,128)(2,1)} %copy-done.56), custom_call_target="tpu_custom_call" | custom-call | flops 2516582400 | bytes 3932160 | tf_op jit(solution)/shard_map/products/pallas_call | solution.py:299
  447.0 4.7 split_output_weight.1
  457.4 37.3 %attend_back.2.refs_1_ = bf16[1536,960]{1,0:T(8,128)(2,1)} custom-call(bf16[1536,960]{1,0:T(8,128)(2,1)} %copy-done.5, bf16[1536,48]{1,0:T(8,128)(2,1)} %copy-done.3, bf16[1536,320]{1,0:T(8,128)(2,1)} %pad_maximum_fusion.2.grad_ref, f32[1536,4]{1,0:T(8,128)} %copy-done.7), custom_call_target="tpu_custom_call" | custom-call | flops 24159191040 | bytes 7372800 | tf_op jit(solution)/shard_map/attend_back/pallas_call | solution.py:213
  494.7 3.5 convolution_convert_fusion.7
  501.0 3.9 convolution_convert_fusion.6
  516.5 4.3 convolution_convert_fusion.5
  523.2 9.5 %products.8.refs_2_ = f32[1280,960]{1,0:T(8,128)} custom-call(bf16[1536,1280]{1,0:T(8,128)(2,1)} %norm_blocks.2.refs_0_, bf16[1536,960]{1,0:T(8,128)(2,1)} %attend_back.2.refs_1_), custom_call_target="tpu_custom_call" | custom-call | flops 3774873600 | bytes 6881280 | tf_op jit(solution)/shard_map/products/pallas_call | solution.py:299
  539.0 37.0 %attend_back.3.refs_1_ = bf16[1536,960]{1,0:T(8,128)(2,1)} custom-call(bf16[1536,960]{1,0:T(8,128)(2,1)} %copy-done.4, bf16[1536,48]{1,0:T(8,128)(2,1)} %copy-done.2, bf16[1536,320]{1,0:T(8,128)(2,1)} %pad_maximum_fusion.3.grad_ref, f32[1536,4]{1,0:T(8,128)} %copy-done.6), custom_call_target="tpu_custom_call" | custom-call | flops 24159191040 | bytes 7372800 | tf_op jit(solution)/shard_map/attend_back/pallas_call | solution.py:213
  578.5 10.6 %products.9 = bf16[1280,1280]{1,0:T(8,128)(2,1)} custom-call(bf16[1536,1280]{1,0:T(8,128)(2,1)} %norm_blocks.3.refs_0_, bf16[1536,960]{1,0:T(8,128)(2,1)} %attend_back.3.refs_1_, f32[1280,960]{1,0:T(8,128)} %products.8.refs_2_, bf16[1280,320]{1,0:T(8,128)(2,1)} %add_convert_fusion.3.refs_3_), custom_call_target="tpu_custom_call" | custom-call | flops 5033164800 | bytes 7864320 | tf_op jit(solution)/shard_map/products/pallas_call | solution.py:299
  589.1 4.3 convolution_convert_fusion.3
  595.8 9.6 %collective-permute-done.72.refs_2_ = bf16[160,1280]{1,0:T(8,128)(2,1)} collective-permute-done((bf16[160,1280]{1,0:T(8,128)(2,1)S(1)}, bf16[160,1280]{1,0:T(8,128)(2,1)}, u32[]{:S(2)}, u32[]{:S(2)}) %collective-permute-start.72) | collective-permute-done | bytes 409632 | tf_op jit(solution)/shard_map/ppermute | solution.py:26
  605.7 4.2 convolution_convert_fusion.2
  610.9 3.7 assemble.6
  614.6 3.5 assemble.7
  627.6 7.1 collective-permute-done.54
  642.2 13.1 %collective-permute-done.56 = bf16[384,1280]{1,0:T(8,128)(2,1)S(1)} collective-permute-done((bf16[384,1280]{1,0:T(8,128)(2,1)S(1)}, bf16[384,1280]{1,0:T(8,128)(2,1)S(1)}, u32[]{:S(2)}, u32[]{:S(2)}) %collective-permute-start.56) | collective-permute-done | bytes 983072 | tf_op jit(solution)/shard_map/ppermute | solution.py:26
  662.8 4.4 collective-permute-done.58
  671.1 8.5 %reduce-scatter.5.cloned.1.call-done = bf16[160,1280]{1,0:T(8,128)(2,1)} async-done(((bf16[1280,1280]{1,0:T(8,128)(2,1)}), bf16[160,1280]{1,0:T(8,128)(2,1)}) %reduce-scatter.5.cloned.1.call-update) | async-done | bytes 409616 | tf_op jit(solution)/shard_map/reduce_scatter | solution.py:515
  682.0 4.4 pad_maximum_fusion
  (627 shorter events, 247.7 us)
Async XLA Ops:
  7.2 68.0 %all-gather.3.cloned.1.call-start = ((), (), s32[]{:S(2)}) async-start(), calls=%async_computation.2 | async-start | bytes 3686400 | tf_op jit(solution)/shard_map/all_gather | solution.py:451
  9.8 168.3 %all-gather.5.cloned.1.call-start = ((), (), s32[]{:S(2)}) async-start(), calls=%async_computation.3 | async-start | bytes 7372800 | tf_op jit(solution)/shard_map/all_gather | solution.py:456
  12.9 563.1 %reduce-scatter.3.cloned.1.call-start = ((), (), s32[]{:S(2)}) async-start(), calls=%async_computation.4 | async-start | bytes 7372800 | tf_op jit(solution)/shard_map/reduce_scatter | solution.py:515
  15.1 25.3 %collective-permute-start.1 = (bf16[384,1280]{1,0:T(8,128)(2,1)S(1)}, bf16[384,1280]{1,0:T(8,128)(2,1)}, u32[]{:S(2)}, u32[]{:S(2)}) collective-permute-start(bf16[384,1280]{1,0:T(8,128)(2,1)S(1)} %get-tuple-element.158.refs_0_), channel_id=1, source_target_pairs={{0,2},{1,3},{2,0},{3,1},{4,6},{5,7},{6,4},{7,5},{8,10},{9,11},{10,... | collective-permute-start | bytes 2949128 | tf_op jit(solution)/shard_map/ppermute | solution.py:26
  21.6 18.8 %collective-permute-start.4 = (bf16[2,1920]{1,0:T(2,128)(2,1)S(1)}, bf16[2,1920]{1,0:T(2,128)(2,1)S(1)}, u32[]{:S(2)}, u32[]{:S(2)}) collective-permute-start(bf16[2,1920]{1,0:T(2,128)(2,1)S(1)} %pad_maximum_fusion.6), channel_id=1, source_target_pairs={{0,8},{4,12},{8,0},{12,4},{16,24},{20,28},{24,16},{28,20},{1,9},{5... | collective-permute-start | bytes 23048 | tf_op jit(solution)/shard_map/ppermute | solution.py:26
  23.3 38.0 %collective-permute-start.7 = (bf16[384,1280]{1,0:T(8,128)(2,1)S(1)}, bf16[384,1280]{1,0:T(8,128)(2,1)}, u32[]{:S(2)}, u32[]{:S(2)}) collective-permute-start(bf16[384,1280]{1,0:T(8,128)(2,1)S(1)} %get-tuple-element.159.refs_0_), channel_id=1, source_target_pairs={{0,2},{1,3},{2,0},{3,1},{4,6},{5,7},{6,4},{7,5},{8,10},{9,11},{10,... | collective-permute-start | bytes 2949128 | tf_op jit(solution)/shard_map/ppermute | solution.py:26
  47.6 16.5 %collective-permute-start.6 = (bf16[384,1280]{1,0:T(8,128)(2,1)S(1)}, bf16[384,1280]{1,0:T(8,128)(2,1)}, u32[]{:S(2)}, u32[]{:S(2)}) collective-permute-start(bf16[384,1280]{1,0:T(8,128)(2,1)S(1)} %get-tuple-element.159.refs_0_), channel_id=1, source_target_pairs={{0,1},{1,0},{2,3},{3,2},{4,5},{5,4},{6,7},{7,6},{8,9},{9,8},{10,11... | collective-permute-start | bytes 2949128 | tf_op jit(solution)/shard_map/ppermute | solution.py:26
  78.1 62.2 %collective-permute-start.12 = (bf16[1280,320]{0,1:T(8,128)(2,1)}, bf16[1280,320]{0,1:T(8,128)(2,1)}, u32[]{:S(2)}, u32[]{:S(2)}) collective-permute-start(bf16[1280,320]{0,1:T(8,128)(2,1)} %copy.50), channel_id=1, source_target_pairs={{0,1},{1,0},{2,3},{3,2},{4,5},{5,4},{6,7},{7,6},{8,9},{9,8},{10,11... | collective-permute-start | bytes 2457608 | tf_op jit(solution)/shard_map/ppermute | solution.py:26
  78.1 34.2 %collective-permute-start.13 = (bf16[1280,320]{0,1:T(8,128)(2,1)}, bf16[1280,320]{0,1:T(8,128)(2,1)}, u32[]{:S(2)}, u32[]{:S(2)}) collective-permute-start(bf16[1280,320]{0,1:T(8,128)(2,1)} %copy.50), channel_id=1, source_target_pairs={{0,2},{1,3},{2,0},{3,1},{4,6},{5,7},{6,4},{7,5},{8,10},{9,11},{10,... | collective-permute-start | bytes 2457608 | tf_op jit(solution)/shard_map/ppermute | solution.py:26
  105.9 26.8 %collective-permute-start.9 = (bf16[384,320]{1,0:T(8,128)(2,1)S(1)}, bf16[384,320]{1,0:T(8,128)(2,1)S(1)}, u32[]{:S(2)}, u32[]{:S(2)}) collective-permute-start(bf16[384,320]{1,0:T(8,128)(2,1)S(1)} %get-tuple-element.217), channel_id=1, source_target_pairs={{0,1},{1,0},{2,3},{3,2},{4,5},{5,4},{6,7},{7,6},{8,9},{9,8},{10,11... | collective-permute-start | bytes 737288 | tf_op jit(solution)/shard_map/ppermute | solution.py:26
  106.2 26.6 %collective-permute-start.10 = (bf16[384,320]{1,0:T(8,128)(2,1)S(1)}, bf16[384,320]{1,0:T(8,128)(2,1)S(1)}, u32[]{:S(2)}, u32[]{:S(2)}) collective-permute-start(bf16[384,320]{1,0:T(8,128)(2,1)S(1)} %get-tuple-element.216), channel_id=1, source_target_pairs={{0,2},{1,3},{2,0},{3,1},{4,6},{5,7},{6,4},{7,5},{8,10},{9,11},{10,... | collective-permute-start | bytes 737288 | tf_op jit(solution)/shard_map/ppermute | solution.py:26
  106.7 26.6 %collective-permute-start.11 = (bf16[384,320]{1,0:T(8,128)(2,1)S(1)}, bf16[384,320]{1,0:T(8,128)(2,1)S(1)}, u32[]{:S(2)}, u32[]{:S(2)}) collective-permute-start(bf16[384,320]{1,0:T(8,128)(2,1)S(1)} %get-tuple-element.215), channel_id=1, source_target_pairs={{0,3},{1,2},{2,1},{3,0},{4,7},{5,6},{6,5},{7,4},{8,11},{9,10},{10,... | collective-permute-start | bytes 737288 | tf_op jit(solution)/shard_map/ppermute | solution.py:26
  112.3 30.2 %collective-permute-start.14 = (bf16[1280,320]{0,1:T(8,128)(2,1)}, bf16[1280,320]{0,1:T(8,128)(2,1)S(1)}, u32[]{:S(2)}, u32[]{:S(2)}) collective-permute-start(bf16[1280,320]{0,1:T(8,128)(2,1)} %collective-permute-done.13), channel_id=1, source_target_pairs={{0,1},{1,0},{2,3},{3,2},{4,5},{5,4},{6,7},{7,6},{8,9},{9,8},{10,11... | collective-permute-start | bytes 2457608 | tf_op jit(solution)/shard_map/ppermute | solution.py:26
  132.7 22.9 %collective-permute-start.15 = (bf16[384,320]{1,0:T(8,128)(2,1)}, bf16[384,320]{1,0:T(8,128)(2,1)}, u32[]{:S(2)}, u32[]{:S(2)}) collective-permute-start(bf16[384,320]{1,0:T(8,128)(2,1)} %get-tuple-element.213), channel_id=1, source_target_pairs={{0,1},{1,0},{2,3},{3,2},{4,5},{5,4},{6,7},{7,6},{8,9},{9,8},{10,11... | collective-permute-start | bytes 737288 | tf_op jit(solution)/shard_map/ppermute | solution.py:26
  132.8 22.8 %collective-permute-start.16 = (bf16[384,320]{1,0:T(8,128)(2,1)}, bf16[384,320]{1,0:T(8,128)(2,1)}, u32[]{:S(2)}, u32[]{:S(2)}) collective-permute-start(bf16[384,320]{1,0:T(8,128)(2,1)} %get-tuple-element.212), channel_id=1, source_target_pairs={{0,2},{1,3},{2,0},{3,1},{4,6},{5,7},{6,4},{7,5},{8,10},{9,11},{10,... | collective-permute-start | bytes 737288 | tf_op jit(solution)/shard_map/ppermute | solution.py:26
  134.3 21.3 %collective-permute-start.17 = (bf16[384,320]{1,0:T(8,128)(2,1)S(1)}, bf16[384,320]{1,0:T(8,128)(2,1)}, u32[]{:S(2)}, u32[]{:S(2)}) collective-permute-start(bf16[384,320]{1,0:T(8,128)(2,1)S(1)} %get-tuple-element.211), channel_id=1, source_target_pairs={{0,3},{1,2},{2,1},{3,0},{4,7},{5,6},{6,5},{7,4},{8,11},{9,10},{10,... | collective-permute-start | bytes 737288 | tf_op jit(solution)/shard_map/ppermute | solution.py:26
  154.5 28.7 %collective-permute-start.18 = (bf16[384,1280]{1,0:T(8,128)(2,1)}, bf16[384,1280]{1,0:T(8,128)(2,1)}, u32[]{:S(2)}, u32[]{:S(2)}) collective-permute-start(bf16[384,1280]{1,0:T(8,128)(2,1)} %add_convert_fusion.11.refs_0_), channel_id=1, source_target_pairs={{0,1},{1,0},{2,3},{3,2},{4,5},{5,4},{6,7},{7,6},{8,9},{9,8},{10,11... | collective-permute-start | bytes 2949128 | tf_op jit(solution)/shard_map/ppermute | solution.py:26
  154.9 32.9 %collective-permute-start.19 = (bf16[384,1280]{1,0:T(8,128)(2,1)}, bf16[384,1280]{1,0:T(8,128)(2,1)}, u32[]{:S(2)}, u32[]{:S(2)}) collective-permute-start(bf16[384,1280]{1,0:T(8,128)(2,1)} %add_convert_fusion.11.refs_0_), channel_id=1, source_target_pairs={{0,2},{1,3},{2,0},{3,1},{4,6},{5,7},{6,4},{7,5},{8,10},{9,11},{10,... | collective-permute-start | bytes 2949128 | tf_op jit(solution)/shard_map/ppermute | solution.py:26
  197.2 23.8 %collective-permute-start.23 = (bf16[384,1280]{1,0:T(8,128)(2,1)S(1)}, bf16[384,1280]{1,0:T(8,128)(2,1)S(1)}, u32[]{:S(2)}, u32[]{:S(2)}) collective-permute-start(bf16[384,1280]{1,0:T(8,128)(2,1)S(1)} %add_convert_fusion.10.refs_4_), channel_id=1, source_target_pairs={{0,2},{1,3},{2,0},{3,1},{4,6},{5,7},{6,4},{7,5},{8,10},{9,11},{10,... | collective-permute-start | bytes 2949128 | tf_op jit(solution)/shard_map/ppermute | solution.py:26
  231.8 24.7 %collective-permute-start.27 = (bf16[384,1280]{1,0:T(8,128)(2,1)S(1)}, bf16[384,1280]{1,0:T(8,128)(2,1)}, u32[]{:S(2)}, u32[]{:S(2)}) collective-permute-start(bf16[384,1280]{1,0:T(8,128)(2,1)S(1)} %copy-done.52), channel_id=1, source_target_pairs={{0,2},{1,3},{2,0},{3,1},{4,6},{5,7},{6,4},{7,5},{8,10},{9,11},{10,... | collective-permute-start | bytes 2949128 | tf_op jit(solution)/shard_map/ppermute | solution.py:26
  233.3 23.3 %collective-permute-start.26 = (bf16[384,1280]{1,0:T(8,128)(2,1)}, bf16[384,1280]{1,0:T(8,128)(2,1)}, u32[]{:S(2)}, u32[]{:S(2)}) collective-permute-start(bf16[384,1280]{1,0:T(8,128)(2,1)} %convolution_convert_fusion.23), channel_id=1, source_target_pairs={{0,1},{1,0},{2,3},{3,2},{4,5},{5,4},{6,7},{7,6},{8,9},{9,8},{10,11... | collective-permute-start | bytes 2949128 | tf_op jit(solution)/shard_map/ppermute | solution.py:26
  239.5 38.1 %collective-permute-start.29 = (bf16[384,1280]{1,0:T(8,128)(2,1)}, bf16[384,1280]{1,0:T(8,128)(2,1)}, u32[]{:S(2)}, u32[]{:S(2)}) collective-permute-start(bf16[384,1280]{1,0:T(8,128)(2,1)} %add_convert_fusion.8), channel_id=1, source_target_pairs={{0,2},{1,3},{2,0},{3,1},{4,6},{5,7},{6,4},{7,5},{8,10},{9,11},{10,... | collective-permute-start | bytes 2949128 | tf_op jit(solution)/shard_map/ppermute | solution.py:26
  244.4 33.2 %collective-permute-start.28 = (bf16[384,1280]{1,0:T(8,128)(2,1)}, bf16[384,1280]{1,0:T(8,128)(2,1)}, u32[]{:S(2)}, u32[]{:S(2)}) collective-permute-start(bf16[384,1280]{1,0:T(8,128)(2,1)} %convolution_convert_fusion.19), channel_id=1, source_target_pairs={{0,1},{1,0},{2,3},{3,2},{4,5},{5,4},{6,7},{7,6},{8,9},{9,8},{10,11... | collective-permute-start | bytes 2949128 | tf_op jit(solution)/shard_map/ppermute | solution.py:26
  259.1 26.6 %collective-permute-start.30 = (bf16[384,1280]{1,0:T(8,128)(2,1)S(1)}, bf16[384,1280]{1,0:T(8,128)(2,1)S(1)}, u32[]{:S(2)}, u32[]{:S(2)}) collective-permute-start(bf16[384,1280]{1,0:T(8,128)(2,1)S(1)} %get-tuple-element.116.refs_8_), channel_id=1, source_target_pairs={{0,1},{1,0},{2,3},{3,2},{4,5},{5,4},{6,7},{7,6},{8,9},{9,8},{10,11... | collective-permute-start | bytes 2949128 | tf_op jit(solution)/shard_map/ppermute | solution.py:26
  259.2 38.5 %collective-permute-start.31 = (bf16[384,1280]{1,0:T(8,128)(2,1)S(1)}, bf16[384,1280]{1,0:T(8,128)(2,1)S(1)}, u32[]{:S(2)}, u32[]{:S(2)}) collective-permute-start(bf16[384,1280]{1,0:T(8,128)(2,1)S(1)} %get-tuple-element.116.refs_8_), channel_id=1, source_target_pairs={{0,2},{1,3},{2,0},{3,1},{4,6},{5,7},{6,4},{7,5},{8,10},{9,11},{10,... | collective-permute-start | bytes 2949128 | tf_op jit(solution)/shard_map/ppermute | solution.py:26
  304.6 23.8 %collective-permute-start.35 = (bf16[384,1280]{1,0:T(8,128)(2,1)S(1)}, bf16[384,1280]{1,0:T(8,128)(2,1)S(1)}, u32[]{:S(2)}, u32[]{:S(2)}) collective-permute-start(bf16[384,1280]{1,0:T(8,128)(2,1)S(1)} %get-tuple-element.125.refs_12_), channel_id=1, source_target_pairs={{0,2},{1,3},{2,0},{3,1},{4,6},{5,7},{6,4},{7,5},{8,10},{9,11},{10,... | collective-permute-start | bytes 2949128 | tf_op jit(solution)/shard_map/ppermute | solution.py:26
  335.0 31.6 %collective-permute-start.41 = (bf16[384,1280]{1,0:T(8,128)(2,1)}, bf16[384,1280]{1,0:T(8,128)(2,1)}, u32[]{:S(2)}, u32[]{:S(2)}) collective-permute-start(bf16[384,1280]{1,0:T(8,128)(2,1)} %add_convert_fusion.7), channel_id=1, source_target_pairs={{0,2},{1,3},{2,0},{3,1},{4,6},{5,7},{6,4},{7,5},{8,10},{9,11},{10,... | collective-permute-start | bytes 2949128 | tf_op jit(solution)/shard_map/ppermute | solution.py:26
  336.4 30.1 %collective-permute-start.40 = (bf16[384,1280]{1,0:T(8,128)(2,1)}, bf16[384,1280]{1,0:T(8,128)(2,1)}, u32[]{:S(2)}, u32[]{:S(2)}) collective-permute-start(bf16[384,1280]{1,0:T(8,128)(2,1)} %convolution_convert_fusion.15), channel_id=1, source_target_pairs={{0,1},{1,0},{2,3},{3,2},{4,5},{5,4},{6,7},{7,6},{8,9},{9,8},{10,11... | collective-permute-start | bytes 2949128 | tf_op jit(solution)/shard_map/ppermute | solution.py:26
  398.5 281.0 %reduce-scatter.5.cloned.1.call-start = ((), (), s32[]{:S(2)}) async-start(), calls=%async_computation.5 | async-start | bytes 3686400 | tf_op jit(solution)/shard_map/reduce_scatter | solution.py:515
  401.9 25.0 %collective-permute-start.39 = (bf16[384,1280]{1,0:T(8,128)(2,1)}, bf16[384,1280]{1,0:T(8,128)(2,1)}, u32[]{:S(2)}, u32[]{:S(2)}) collective-permute-start(bf16[384,1280]{1,0:T(8,128)(2,1)} %add_convert_fusion.6), channel_id=1, source_target_pairs={{0,2},{1,3},{2,0},{3,1},{4,6},{5,7},{6,4},{7,5},{8,10},{9,11},{10,... | collective-permute-start | bytes 2949128 | tf_op jit(solution)/shard_map/ppermute | solution.py:26
  402.8 24.1 %collective-permute-start.38 = (bf16[384,1280]{1,0:T(8,128)(2,1)}, bf16[384,1280]{1,0:T(8,128)(2,1)}, u32[]{:S(2)}, u32[]{:S(2)}) collective-permute-start(bf16[384,1280]{1,0:T(8,128)(2,1)} %convolution_convert_fusion.11), channel_id=1, source_target_pairs={{0,1},{1,0},{2,3},{3,2},{4,5},{5,4},{6,7},{7,6},{8,9},{9,8},{10,11... | collective-permute-start | bytes 2949128 | tf_op jit(solution)/shard_map/ppermute | solution.py:26
  403.6 50.4 %collective-permute-start.44 = (bf16[384,320]{1,0:T(8,128)(2,1)}, bf16[384,320]{1,0:T(8,128)(2,1)}, u32[]{:S(2)}, u32[]{:S(2)}) collective-permute-start(bf16[384,320]{1,0:T(8,128)(2,1)} %get-tuple-element.223), channel_id=1, source_target_pairs={{0,3},{1,2},{2,1},{3,0},{4,7},{5,6},{6,5},{7,4},{8,11},{9,10},{10,... | collective-permute-start | bytes 737288 | tf_op jit(solution)/shard_map/ppermute | solution.py:26
  404.9 50.2 %collective-permute-start.43 = (bf16[384,320]{1,0:T(8,128)(2,1)}, bf16[384,320]{1,0:T(8,128)(2,1)}, u32[]{:S(2)}, u32[]{:S(2)}) collective-permute-start(bf16[384,320]{1,0:T(8,128)(2,1)} %get-tuple-element.224), channel_id=1, source_target_pairs={{0,2},{1,3},{2,0},{3,1},{4,6},{5,7},{6,4},{7,5},{8,10},{9,11},{10,... | collective-permute-start | bytes 737288 | tf_op jit(solution)/shard_map/ppermute | solution.py:26
  405.8 49.3 %collective-permute-start.42 = (bf16[384,320]{1,0:T(8,128)(2,1)}, bf16[384,320]{1,0:T(8,128)(2,1)}, u32[]{:S(2)}, u32[]{:S(2)}) collective-permute-start(bf16[384,320]{1,0:T(8,128)(2,1)} %get-tuple-element.225), channel_id=1, source_target_pairs={{0,1},{1,0},{2,3},{3,2},{4,5},{5,4},{6,7},{7,6},{8,9},{9,8},{10,11... | collective-permute-start | bytes 737288 | tf_op jit(solution)/shard_map/ppermute | solution.py:26
  438.4 98.4 %collective-permute-start.51 = (bf16[384,320]{1,0:T(8,128)(2,1)}, bf16[384,320]{1,0:T(8,128)(2,1)}, u32[]{:S(2)}, u32[]{:S(2)}) collective-permute-start(bf16[384,320]{1,0:T(8,128)(2,1)} %get-tuple-element.220), channel_id=1, source_target_pairs={{0,3},{1,2},{2,1},{3,0},{4,7},{5,6},{6,5},{7,4},{8,11},{9,10},{10,... | collective-permute-start | bytes 737288 | tf_op jit(solution)/shard_map/ppermute | solution.py:26
  438.4 98.4 %collective-permute-start.50 = (bf16[384,320]{1,0:T(8,128)(2,1)}, bf16[384,320]{1,0:T(8,128)(2,1)}, u32[]{:S(2)}, u32[]{:S(2)}) collective-permute-start(bf16[384,320]{1,0:T(8,128)(2,1)} %get-tuple-element.221), channel_id=1, source_target_pairs={{0,2},{1,3},{2,0},{3,1},{4,6},{5,7},{6,4},{7,5},{8,10},{9,11},{10,... | collective-permute-start | bytes 737288 | tf_op jit(solution)/shard_map/ppermute | solution.py:26
  454.1 54.1 %collective-permute-start.47 = (bf16[1280,320]{0,1:T(8,128)(2,1)}, bf16[1280,320]{0,1:T(8,128)(2,1)}, u32[]{:S(2)}, u32[]{:S(2)}) collective-permute-start(bf16[1280,320]{0,1:T(8,128)(2,1)} %copy.57), channel_id=1, source_target_pairs={{0,1},{1,0},{2,3},{3,2},{4,5},{5,4},{6,7},{7,6},{8,9},{9,8},{10,11... | collective-permute-start | bytes 2457608 | tf_op jit(solution)/shard_map/ppermute | solution.py:26
  498.2 15.8 %collective-permute-start.45 = (bf16[384,1280]{1,0:T(8,128)(2,1)}, bf16[384,1280]{1,0:T(8,128)(2,1)}, u32[]{:S(2)}, u32[]{:S(2)}) collective-permute-start(bf16[384,1280]{1,0:T(8,128)(2,1)} %convolution_convert_fusion.7), channel_id=1, source_target_pairs={{0,1},{1,0},{2,3},{3,2},{4,5},{5,4},{6,7},{7,6},{8,9},{9,8},{10,11... | collective-permute-start | bytes 2949128 | tf_op jit(solution)/shard_map/ppermute | solution.py:26
  508.2 28.7 %collective-permute-start.49 = (bf16[384,320]{1,0:T(8,128)(2,1)}, bf16[384,320]{1,0:T(8,128)(2,1)S(1)}, u32[]{:S(2)}, u32[]{:S(2)}) collective-permute-start(bf16[384,320]{1,0:T(8,128)(2,1)} %get-tuple-element.222), channel_id=1, source_target_pairs={{0,1},{1,0},{2,3},{3,2},{4,5},{5,4},{6,7},{7,6},{8,9},{9,8},{10,11... | collective-permute-start | bytes 737288 | tf_op jit(solution)/shard_map/ppermute | solution.py:26
  511.4 21.3 %collective-permute-start.48 = (bf16[1280,320]{0,1:T(8,128)(2,1)}, bf16[1280,320]{0,1:T(8,128)(2,1)}, u32[]{:S(2)}, u32[]{:S(2)}) collective-permute-start(bf16[1280,320]{0,1:T(8,128)(2,1)} %copy.59), channel_id=1, source_target_pairs={{0,2},{1,3},{2,0},{3,1},{4,6},{5,7},{6,4},{7,5},{8,10},{9,11},{10,... | collective-permute-start | bytes 2457608 | tf_op jit(solution)/shard_map/ppermute | solution.py:26
  577.2 18.3 %collective-permute-start.69 = (bf16[160,1280]{1,0:T(8,128)(2,1)S(1)}, bf16[160,1280]{1,0:T(8,128)(2,1)S(1)}, u32[]{:S(2)}, u32[]{:S(2)}) collective-permute-start(bf16[160,1280]{1,0:T(8,128)(2,1)S(1)} %get-tuple-element.228.refs_0_), channel_id=1, source_target_pairs={{0,2},{1,3},{2,0},{3,1},{4,6},{5,7},{6,4},{7,5},{8,10},{9,11},{10,... | collective-permute-start | bytes 1228808 | tf_op jit(solution)/shard_map/ppermute | solution.py:26
  593.4 24.7 %collective-permute-start.52 = (bf16[384,1280]{1,0:T(8,128)(2,1)}, bf16[384,1280]{1,0:T(8,128)(2,1)}, u32[]{:S(2)}, u32[]{:S(2)}) collective-permute-start(bf16[384,1280]{1,0:T(8,128)(2,1)} %convolution_convert_fusion.3), channel_id=1, source_target_pairs={{0,1},{1,0},{2,3},{3,2},{4,5},{5,4},{6,7},{7,6},{8,9},{9,8},{10,11... | collective-permute-start | bytes 2949128 | tf_op jit(solution)/shard_map/ppermute | solution.py:26
  595.3 19.3 %collective-permute-start.71 = (bf16[160,1280]{1,0:T(8,128)(2,1)S(1)}, bf16[160,1280]{1,0:T(8,128)(2,1)}, u32[]{:S(2)}, u32[]{:S(2)}) collective-permute-start(bf16[160,1280]{1,0:T(8,128)(2,1)S(1)} %get-tuple-element.227.refs_0_), channel_id=1, source_target_pairs={{0,1},{1,0},{2,3},{3,2},{4,5},{5,4},{6,7},{7,6},{8,9},{9,8},{10,11... | collective-permute-start | bytes 1228808 | tf_op jit(solution)/shard_map/ppermute | solution.py:26
  609.9 24.8 %collective-permute-start.54 = (bf16[384,1280]{1,0:T(8,128)(2,1)}, bf16[384,1280]{1,0:T(8,128)(2,1)S(1)}, u32[]{:S(2)}, u32[]{:S(2)}) collective-permute-start(bf16[384,1280]{1,0:T(8,128)(2,1)} %add_convert_fusion.5), channel_id=1, source_target_pairs={{0,2},{1,3},{2,0},{3,1},{4,6},{5,7},{6,4},{7,5},{8,10},{9,11},{10,... | collective-permute-start | bytes 2949128 | tf_op jit(solution)/shard_map/ppermute | solution.py:26
  610.7 24.0 %collective-permute-start.53 = (bf16[384,1280]{1,0:T(8,128)(2,1)}, bf16[384,1280]{1,0:T(8,128)(2,1)S(1)}, u32[]{:S(2)}, u32[]{:S(2)}) collective-permute-start(bf16[384,1280]{1,0:T(8,128)(2,1)} %convolution_convert_fusion.5), channel_id=1, source_target_pairs={{0,1},{1,0},{2,3},{3,2},{4,5},{5,4},{6,7},{7,6},{8,9},{9,8},{10,11... | collective-permute-start | bytes 2949128 | tf_op jit(solution)/shard_map/ppermute | solution.py:26
  619.9 35.4 %collective-permute-start.56 = (bf16[384,1280]{1,0:T(8,128)(2,1)S(1)}, bf16[384,1280]{1,0:T(8,128)(2,1)S(1)}, u32[]{:S(2)}, u32[]{:S(2)}) collective-permute-start(bf16[384,1280]{1,0:T(8,128)(2,1)S(1)} %add_convert_fusion.2), channel_id=1, source_target_pairs={{0,2},{1,3},{2,0},{3,1},{4,6},{5,7},{6,4},{7,5},{8,10},{9,11},{10,... | collective-permute-start | bytes 2949128 | tf_op jit(solution)/shard_map/ppermute | solution.py:26
  624.4 30.9 %collective-permute-start.55 = (bf16[384,1280]{1,0:T(8,128)(2,1)S(1)}, bf16[384,1280]{1,0:T(8,128)(2,1)S(1)}, u32[]{:S(2)}, u32[]{:S(2)}) collective-permute-start(bf16[384,1280]{1,0:T(8,128)(2,1)S(1)} %convolution_convert_fusion.1), channel_id=1, source_target_pairs={{0,1},{1,0},{2,3},{3,2},{4,5},{5,4},{6,7},{7,6},{8,9},{9,8},{10,11... | collective-permute-start | bytes 2949128 | tf_op jit(solution)/shard_map/ppermute | solution.py:26
  671.1 15.4 %collective-permute-start.60 = (f32[1922]{0:T(1024)S(1)}, f32[1922]{0:T(1024)S(1)}, u32[]{:S(2)}, u32[]{:S(2)}) collective-permute-start(f32[1922]{0:T(1024)S(1)} %concatenate.53), channel_id=1, source_target_pairs={{0,1},{1,0},{2,3},{3,2},{4,5},{5,4},{6,7},{7,6},{8,9},{9,8},{10,11... | collective-permute-start | bytes 23072 | tf_op jit(solution)/shard_map/ppermute | solution.py:26
  (172 other events, 1494.6 us)
Sparse Core Ops, SparseCore 0:
  10.8 64.3 all-gather.2
  77.3 100.6 all-gather.4
  398.6 119.4 reduce-scatter.2
  605.8 73.6 reduce-scatter.4

commit v3 on v2

--- a/solution.py
+++ b/solution.py
@@ -15,11 +15,27 @@
 half = jnp.bfloat16
 
 
-def layer_norm(v, gain, bias):
+def norm_stats(v):
     mean = jnp.mean(v, axis=-1, keepdims=True)
     cent = v - mean
     var = jnp.mean(cent * cent, axis=-1, keepdims=True)
-    return cent * lax.rsqrt(var + 1e-05) * gain + bias
+    return mean, lax.rsqrt(var + 1e-05)
+
+
+def layer_norm(v, stats, gain, bias):
+    return (v - stats[0]) * stats[1] * gain + bias
+
+
+def norm_back(v, stats, gain, grad):
+    scaled = (v - stats[0]) * stats[1]
+    inner = grad * gain
+    first = jnp.mean(inner, axis=-1, keepdims=True)
+    second = jnp.mean(inner * scaled, axis=-1, keepdims=True)
+    return (
+        stats[1] * (inner - first - scaled * second),
+        jnp.sum(grad * scaled, axis=0),
+        jnp.sum(grad, axis=0),
+    )
 
 
 def flip(tensor, bits, axis="seq"):
@@ -222,7 +238,7 @@
         ],
         compiler_params=pltpu.CompilerParams(vmem_limit_bytes=56 << 20),
         cost_estimate=pl.CostEstimate(
-            flops=10 * heads * seq * seq * 256, bytes_accessed=qkv.size * 5, transcendentals=heads * seq * seq
+            flops=20 * heads * seq * seq * 256, bytes_accessed=qkv.size * 5, transcendentals=heads * seq * seq
         ),
         name="attend_back",
     )(qkv, mask, grad, lse)
@@ -236,7 +252,9 @@
         def some(i, carry, r=r):
             start = pl.multiple_of(i * chunk, chunk)
             v = blocks[r][pl.ds(start, chunk), :].astype(single)
-            out[pl.ds(r * rows + start, chunk), :] = layer_norm(v, gain_ref[...], bias_ref[...]).astype(half)
+            out[pl.ds(r * rows + start, chunk), :] = layer_norm(v, norm_stats(v), gain_ref[...], bias_ref[...]).astype(
+                half
+            )
             return carry
 
         lax.fori_loop(0, rows // chunk, some, 0)
@@ -266,11 +284,11 @@
         total = term if total is None else total + term
     total = total.astype(out.dtype)
     if beside:
-        total = jnp.concatenate([total, more[-1][...]], axis=1)
+        total = jnp.concatenate([total, more[-1][:, :beside]], axis=1)
     out[...] = total
 
 
-def products(lefts, rights, kind, before=None, beside=None, into=None, slot=0, slots=1):
+def products(lefts, rights, kind, before=None, beside=None, width=0, into=None, slot=0, slots=1):
     pairs = len(lefts)
     rows, cols = lefts[0].shape[1], rights[0].shape[1]
     tile = next(t for t in (256, 128, rows) if rows % t == 0)
@@ -284,8 +302,8 @@
     if beside is not None:
         more.append(beside)
         in_specs.append(pl.BlockSpec((tile, beside.shape[1]), lambda i: (i, 0)))
-        cols += beside.shape[1]
-    body = functools.partial(products_kernel, pairs, before is not None, beside is not None)
+        cols += width
+    body = functools.partial(products_kernel, pairs, before is not None, width)
     aliases = {}
     if into is not None:
         aliases = {2 * pairs + len(more): 0}
@@ -311,7 +329,27 @@
     )(*lefts, *rights, *more)
 
 
-def assemble_kernel(groups, counts, width, me_ref, *refs):
+def spread_kernel(grad, weight, *outs):
+    n = outs[0].shape[0]
+    for r, out in enumerate(outs):
+        out[...] = lax.dot_general(
+            grad[r * n : (r + 1) * n, :], weight[...], (((1,), (1,)), ((), ())),
+            preferred_element_type=single,
+        ).astype(half)
+
+
+def spread_terms(grad, weight, groups):
+    rows, cols = grad.shape[0] // groups, weight.shape[0]
+    return pl.pallas_call(
+        spread_kernel,
+        out_shape=[jax.ShapeDtypeStruct((rows, cols), half)] * groups,
+        compiler_params=pltpu.CompilerParams(vmem_limit_bytes=32 << 20),
+        cost_estimate=pl.CostEstimate(flops=0, bytes_accessed=0, transcendentals=0),
+        name="spread_terms",
+    )(grad, weight)
+
+
+def assemble_kernel(groups, counts, width, start, me_ref, *refs):
     pieces, out = refs[:groups], refs[groups]
     rows = pieces[0].shape[0]
     for v in range(groups):
@@ -324,19 +362,20 @@
                     out[g * rows : (g + 1) * rows, :] = piece[...].astype(single)
             if counts:
                 blocks = [
-                    pieces[v ^ g][:, k * width : (k + 1) * width]
+                    pieces[v ^ g][:, start + k * width : start + (k + 1) * width]
                     for k in range(counts)
                     for g in range(groups)
                 ]
                 out[...] = jnp.concatenate(blocks, axis=1).astype(single)
 
 
-def assemble(pieces, counts, me):
+def assemble(pieces, counts, me, start=0, cols=None):
     groups = len(pieces)
-    rows, cols = pieces[0].shape
+    rows = pieces[0].shape[0]
+    cols = cols or pieces[0].shape[1]
     shape = (rows, cols * groups) if counts else (rows * groups, cols)
     return pl.pallas_call(
-        functools.partial(assemble_kernel, groups, counts, cols // max(counts, 1)),
+        functools.partial(assemble_kernel, groups, counts, cols // max(counts, 1), start),
         out_shape=jax.ShapeDtypeStruct(shape, single),
         in_specs=[pl.BlockSpec(memory_space=pltpu.SMEM)]
         + [pl.BlockSpec(memory_space=pltpu.VMEM)] * groups,
@@ -362,16 +401,20 @@
 
 
 def scatter_blocks_kernel(groups, me_ref, full, *outs):
-    span = outs[0].shape[1]
+    span = full.shape[1] // groups
+    spare = outs[0].shape[1] - span
     for v in range(groups):
 
         @pl.when(me_ref[0] == v)
         def _():
             for r in range(groups):
                 for g in range(groups):
-                    outs[r][g * span : (g + 1) * span, :] = full[
+                    block = full[
                         (v ^ g) * span : ((v ^ g) + 1) * span, (v ^ r) * span : ((v ^ r) + 1) * span
                     ]
+                    if spare:
+                        block = jnp.concatenate([block, jnp.zeros((span, spare), block.dtype)], axis=1)
+                    outs[r][g * span : (g + 1) * span, :] = block
 
 
 def arrange(kernel, arrays, shapes, groups, me, name):
@@ -395,6 +438,9 @@
         if not self.tokens:
             return tensor
         return lax.optimization_barrier((tensor, *self.tokens))[0]
+
+    def after_all(self, tensors):
+        return list(lax.optimization_barrier((*tensors, *self.tokens))[: len(tensors)])
 
     def mark(self, *tensors):
         self.tokens = list(tensors)
@@ -506,6 +552,7 @@
     outs, losses, grad_outs, pieces = ([None] * clips for _ in range(4))
     grad_uppers, grad_hidden2, grad_middles, grad_branches = ([None] * clips for _ in range(4))
     grad_heads, grad_qkvs, grad_hidden1, grads_in = ([None] * clips for _ in range(4))
+    stats2 = [None] * clips
     norm2_grads, norm1_grads = [None] * clips, [None] * clips
 
     def rows_of(array, r):
@@ -513,10 +560,6 @@
 
     def owned(grad):
         return lax.psum_scatter(grad, "fsdp", scatter_dimension=0, tiled=True)
-
-    def norm_back(v, gain, bias, grad):
-        _, back = jax.vjp(layer_norm, v, gain, bias)
-        return back(grad)
 
     def arriving(store, c):
         near, far = store[c]
@@ -538,30 +581,33 @@
         moved[c] = swap(parts)
 
     def project(c):
-        contexts[c] = jnp.concatenate([step.after(moved[c][0])] + moved[c][1:], axis=1)
+        contexts[c] = jnp.concatenate(moved[c][:1] + step.after_all(moved[c][1:]), axis=1)
         middles[c] = frames_in[c].astype(single) + dot(contexts[c], wout) + obias
-        hidden = layer_norm(middles[c], gain2, bias2).astype(half)
+        stats2[c] = norm_stats(middles[c])
+        hidden = layer_norm(middles[c], stats2[c], gain2, bias2).astype(half)
         step.mark(hidden)
         hiddens[c] = gather_begin(hidden)
 
-    def up(c):
-        actives[c], slopes[c] = [], []
-        for block in arriving(hiddens, c):
-            upper = dot(step.after(block), wup) + ubias
+    def feed_forward(c):
+        near, far = hiddens[c]
+        hiddens[c] = near + gather_end(step.after(far))
+        actives[c], slopes[c] = [None] * groups, [None] * groups
+
+        def term(r):
+            upper = dot(step.after(hiddens[c][r]), wup) + ubias
             cdf = 0.5 * (1.0 + lax.erf(upper * math.sqrt(0.5)))
-            actives[c].append((upper * cdf).astype(half))
-            slopes[c].append(
-                (cdf + upper * (jnp.exp(-0.5 * upper * upper) * (1.0 / math.sqrt(2.0 * math.pi)))).astype(half)
-            )
-            step.mark(actives[c][-1])
-
-    def down(c):
-        branches[c] = scatter_terms(
-            lambda r: dot(step.after(actives[c][r]), wdown).astype(half), step
-        )
+            actives[c][r] = (upper * cdf).astype(half)
+            slopes[c][r] = (
+                cdf + upper * (jnp.exp(-0.5 * upper * upper) * (1.0 / math.sqrt(2.0 * math.pi)))
+            ).astype(half)
+            step.mark(actives[c][r])
+            return marked(dot(step.after(actives[c][r]), wdown).astype(half))
+
+        branches[c] = scatter_terms(term, step)
 
     def loss(c):
-        result = step.after(middles[c]) + add_terms(branches[c]) + dbias
+        branch = add_terms(branches[c][:1] + step.after_all(branches[c][1:]))
+        result = middles[c] + branch + dbias
         outs[c] = result.astype(half)
         diff = result - teacher[c].astype(single)
         masked = diff * row_valid[c]
@@ -580,13 +626,12 @@
 
     def back_down(c):
         grad_hidden2[c] = scatter_terms(
-            lambda r: dot_t(step.after(grad_uppers[c][r]), wup).astype(half), step
+            lambda r: marked(dot_t(step.after(grad_uppers[c][r]), wup).astype(half)), step
         )
 
     def norm2(c):
-        gm, *norm2_grads[c] = norm_back(
-            step.after(middles[c]), gain2, bias2, add_terms(grad_hidden2[c])
-        )
+        grad = add_terms(grad_hidden2[c][:1] + step.after_all(grad_hidden2[c][1:]))
+        gm, *norm2_grads[c] = norm_back(middles[c], stats2[c], gain2, grad)
         grad_middles[c] = grad_outs[c] + gm
         grad_branches[c] = grad_middles[c].astype(half)
         grad_context = dot_t(grad_branches[c], wout).astype(half)
@@ -595,19 +640,23 @@
         grad_heads[c] = swap(parts)
 
     def attention_back(c):
-        grad_head = jnp.concatenate([step.after(grad_heads[c][0])] + grad_heads[c][1:], axis=0)
+        grad_head = jnp.concatenate(grad_heads[c][:1] + step.after_all(grad_heads[c][1:]), axis=0)
         grad_qkvs[c] = attend_back(qkvs[c], masks[c], grad_head, sums[c], heads, dim, scale)
         step.mark(grad_qkvs[c])
 
+    def marked(tensor):
+        step.mark(tensor)
+        return tensor
+
     def hidden_back(c):
-        grad_hidden1[c] = scatter_terms(
-            lambda r: dot_t(rows_of(step.after(grad_qkvs[c]), r), wqkv).astype(half), step
-        )
+        found = spread_terms(step.after(grad_qkvs[c]), wqkv, groups)
+        step.mark(*found)
+        grad_hidden1[c] = scatter_terms(lambda r: found[r], step)
 
     def norm1_back(c):
-        gs, *norm1_grads[c] = norm_back(
-            step.after(frames_in[c]).astype(single), gain1, bias1, add_terms(grad_hidden1[c])
-        )
+        state = frames_in[c].astype(single)
+        grad = add_terms(grad_hidden1[c][:1] + step.after_all(grad_hidden1[c][1:]))
+        gs, *norm1_grads[c] = norm_back(state, norm_stats(state), gain1, grad)
         grads_in[c] = grad_middles[c] + gs
         step.mark(grads_in[c])
 
@@ -624,8 +673,7 @@
     for c in every:
         project(c)
     for c in every:
-        up(c)
-        down(c)
+        feed_forward(c)
     for c in every:
         loss(c)
     for c in every:
@@ -639,9 +687,9 @@
         return [step.after(lefts[0])] + lefts[1:]
 
     joined = part == depth
+    norm2(first_clip)
     grad_wdown = products(ordered(flat(actives)), flat(pieces), half, slots=1 + joined)
     step.mark(grad_wdown)
-    norm2(first_clip)
     grad_wup = products(
         ordered(flat(hiddens)), flat(grad_uppers), half,
         **(dict(into=grad_wdown, slot=1, slots=2) if joined else {}),
@@ -658,34 +706,32 @@
     step.mark(grad_wout)
     quarters = arrange(
         scatter_blocks_kernel, [grad_wout],
-        [jax.ShapeDtypeStruct((width, span), half)] * groups, groups, me, "split_output_weight",
+        [jax.ShapeDtypeStruct((width, -(-span // LANES) * LANES), half)] * groups, groups, me,
+        "split_output_weight",
     )
     attention_back(first_clip)
-    hidden_back(first_clip)
-    early = products(ordered(full1[:-1]), grad_qkvs[:-1], single)
-    step.mark(early)
     grad_wout = scatter_terms(lambda r: quarters[r], Order())
     grad_wout = add_terms([step.after(grad_wout[0])] + grad_wout[1:]).astype(half)
     step.mark(grad_wout)
     for c in others:
         attention_back(c)
     step.also(grad_wup)
-    total = products(ordered(full1[-1:]), grad_qkvs[-1:], half, before=early, beside=grad_wout)
+    total = products(ordered(full1), grad_qkvs, half, beside=grad_wout, width=span)
     step.mark(total)
     total = owned(total)
-    grad_wqkv, grad_wout = total[:, : 3 * span], total[:, 3 * span :]
-    for c in others:
+    for c in every:
         hidden_back(c)
     for c in every:
         norm1_back(c)
+    grad_wdown, grad_wup = (gather_all(g) for g in step.after_all([grad_wdown, grad_wup]))
+    late = step.after_all(grad_qkvs)
     frames_out = jnp.stack(outs)
-    grad_in = jnp.stack(grads_in)
     grad_gain1, grad_bias1 = (sum(g) for g in zip(*norm1_grads))
     grad_gain2, grad_bias2 = (sum(g) for g in zip(*norm2_grads))
     grad_dbias = sum(jnp.sum(g.astype(half).astype(single), axis=0) for g in grad_outs)
     grad_ubias = sum(jnp.sum(g.astype(single), axis=0) for blocks in grad_uppers for g in blocks)
     grad_obias = sum(jnp.sum(g.astype(single), axis=0) for g in grad_branches)
-    grad_qkv_bias = sum(jnp.sum(g.astype(single), axis=0) for g in grad_qkvs)
+    grad_qkv_bias = sum(jnp.sum(g.astype(single), axis=0) for g in late)
 
     def rows8(v):
         return v.reshape(owners, depth)
@@ -707,16 +753,25 @@
         rows = rows[:bits] + flip(rows[bits:], bits, "fsdp")
         bits //= 2
     rows = jnp.concatenate([rows[0], jnp.stack(losses)])
-    rows = rows + flip(rows, 1)
-    rows = rows + flip(rows, 2)
+    bits = 1
+    while bits < groups:
+        rows = rows + flip(rows, bits)
+        bits *= 2
+    step.mark(rows)
     small = [rows[k * depth : (k + 1) * depth] for k in range(8)]
     small_up = rows[8 * depth : 8 * depth + units]
     clip_loss = rows[8 * depth + units :]
 
-    grad_wdown = assemble(gather_all(grad_wdown), 0, me)
-    grad_wup = assemble(gather_all(grad_wup), owners, me)
-    grad_wqkv = assemble(gather_all(grad_wqkv), 3, me)
-    grad_wout = assemble(gather_all(grad_wout), 1, me)
+    total = step.after(total)
+    pieces_last = gather_all(total)
+    step.mark(total)
+    grad_in = jnp.stack(step.after_all(grads_in))
+    grad_wdown = assemble(step.after_all(grad_wdown), 0, me)
+    grad_wup = assemble(step.after_all(grad_wup), owners, me)
+    step.mark(grad_in, grad_wdown, grad_wup)
+    pieces_last = pieces_last[:1] + step.after_all(pieces_last[1:])
+    grad_wqkv = assemble(pieces_last, 3, me, 0, 3 * span)
+    grad_wout = assemble(pieces_last, 1, me, 3 * span, span)
     return (
         frames_out, clip_loss, grad_in, small[0], small[1], grad_wqkv, small[2], small[3],
         grad_wout, small[4], small[5], small[6], grad_wup, small_up, grad_wdown, small[7],

time: 715 us -> 683 us (0.955)
  matrix products: 134 us -> 104 us
  waiting for transfers between devices: 161 us -> 182 us
  other arithmetic: 72 us -> 54.6 us
  local copies, waits for them, and re-layouts: 62.3 us -> 54.6 us
    ppermute x74 -> x71, waiting for transfers between devices: 135 us -> 177 us  [flip(): lax.ppermute(tensor, axis, [(i, i ^ bits) for i in range(lax.axis_size(ax...]
    dot_general x26 -> x18, matrix products: 63.1 us -> 38.6 us  [dot_t(): lax.dot_general(a, b, (((1,), (1,)), ((), ())), preferred_element_type=si...]
    reduce_sum x20 -> x10, other arithmetic: 27.1 us -> 11.2 us  [the longest x2 4.44 us: norm_back(): jnp.sum(grad * scaled, axis=0)]
    all_gather x1, waiting for transfers between devices: 14.9 us -> 0.01 us  [local(): lax.all_gather(jnp.concatenate([wup, wdown], axis=1), 'fsdp', axis=0, til...]
    pallas_call x0 -> x2, Pallas kernels: none -> 10.5 us  [spread_terms(): pl.pallas_call(spread_kernel, out_shape=[jax.ShapeDtypeStruct((rows, cols...]
    reduce_scatter x2, waiting for transfers between devices: 8.45 us -> 0.01 us  [owned(): return lax.psum_scatter(grad, 'fsdp', scatter_dimension=0, tiled=True)]
    pallas_call x5 -> x4, Pallas kernels: 67.7 us -> 61.6 us  [products(): pl.pallas_call(body, grid=(rows // tile,), in_specs=in_specs, out_specs=p...]
    unnamed x284 -> x258, local copies, waits for them, and re-layouts: 12.8 us -> 16.5 us
  transfers between devices with their start and end apart: 78 -> 75, of which waited for: 22 -> 26; matrix products, arithmetic and copies ran while one was open for 32% -> 25% of each run, Pallas kernels for 27% -> 29%
where the time goes in v3:
time: 683 us; the launch traced here: 679 us
  Pallas kernels  222 us (33%)
  waiting for transfers between devices  182 us (27%)
  matrix products  104 us (15%)
  local copies, waits for them, and re-layouts  54.6 us (8%)
  other arithmetic  54.6 us (8%)
  starting transfers between devices  43.9 us (6%)
  between operations  17.8 us (3%)
    ppermute x71, waiting for transfers between devices, flip(): lax.ppermute(tensor, axis, [(i, i ^ bits) for i in range(lax.axis_size(ax...  177 us
    pallas_call x2, Pallas kernels, attend_back(): pl.pallas_call(functools.partial(attend_back_kernel, heads, dim, block, s...  74.4 us
    dot_general x20, matrix products, dot(): return jnp.dot(a, b, preferred_element_type=single)  65.6 us
    pallas_call x4, Pallas kernels, products(): pl.pallas_call(body, grid=(rows // tile,), in_specs=in_specs, out_specs=p...  61.6 us
    ppermute x71, starting transfers between devices, flip(): lax.ppermute(tensor, axis, [(i, i ^ bits) for i in range(lax.axis_size(ax...  43.8 us
    dot_general x18, matrix products, dot_t(): lax.dot_general(a, b, (((1,), (1,)), ((), ())), preferred_element_type=si...  38.6 us
    pallas_call x2, Pallas kernels, attend(): pl.pallas_call(functools.partial(attend_kernel, heads, dim, block, scale)...  37.8 us
    unnamed x258, local copies, waits for them, and re-layouts  16.5 us
  transfers between devices with their start and end apart: 75, of which 26 were waited for; matrix products, arithmetic and copies ran while one was open for 25% of the time, Pallas kernels for 29%

profile of v3, /device:TPU:0, one launch (start us, length us, event | category | flops | bytes accessed | tf_op | source)
XLA Modules:
  0.0 679.1 jit_solution(4453666181072962480)
XLA Ops:
  26.5 11.8 %collective-permute-done.1.refs_2_ = bf16[384,1280]{1,0:T(8,128)(2,1)} collective-permute-done((bf16[384,1280]{1,0:T(8,128)(2,1)}, bf16[384,1280]{1,0:T(8,128)(2,1)}, u32[]{:S(2)}, u32[]{:S(2)}) %collective-permute-start.1) | collective-permute-done | bytes 983072 | tf_op jit(solution)/shard_map/ppermute | solution.py:42
  38.3 3.2 collective-permute-start.5
  45.9 7.7 %norm_blocks.2.refs_0_ = bf16[1536,1280]{1,0:T(8,128)(2,1)} custom-call(bf16[384,1280]{1,0:T(8,128)(2,1)} %get-tuple-element.264.refs_0_, bf16[384,1280]{1,0:T(8,128)(2,1)} %collective-permute-done.refs_1_, bf16[384,1280]{1,0:T(8,128)(2,1)} %collective-permute-done.1.refs_2_, bf16[384,1280]{1,0:T(8,128)(2,1)} %copy-done.54, f32[1,1280]{1,0:T(1,128)} %reshape.306.refs_4_, ...), custom_call_target="tpu_custom_call" | custom-call | flops 19660800 | bytes 7864320 | tf_op jit(solution)/shard_map/norm_blocks/pallas_call | solution.py:266
  53.6 5.6 collective-permute-done.7.refs_2_
  62.2 7.6 %norm_blocks.3.refs_1_ = bf16[1536,1280]{1,0:T(8,128)(2,1)} custom-call(bf16[384,1280]{1,0:T(8,128)(2,1)} %copy-done.43, bf16[384,1280]{1,0:T(8,128)(2,1)} %collective-permute-done.6.refs_1_, bf16[384,1280]{1,0:T(8,128)(2,1)} %collective-permute-done.7.refs_2_, bf16[384,1280]{1,0:T(8,128)(2,1)} %collective-permute-done.8.refs_3_, ...), custom_call_target="tpu_custom_call" | custom-call | flops 19660800 | bytes 7864320 | tf_op jit(solution)/shard_map/norm_blocks/pallas_call | solution.py:266
  69.8 5.4 all-gather.3.cloned.1.call-done
  79.6 7.2 %add_convert_fusion.1.qkv_ref = bf16[1536,960]{1,0:T(8,128)(2,1)S(1)} fusion(bf16[1536,1280]{1,0:T(8,128)(2,1)} %norm_blocks.2.refs_0_, f32[960]{0:T(1024)S(1)} %bitcast.110, bf16[1280,1280]{1,0:T(8,128)(2,1)} %all-gather.3.cloned.1.call-done), kind=kOutput, calls=%fused_computation.4 | convolution fusion | flops 3777822720 | bytes 9506560 | tf_op jit(solution)/shard_map/dot_general | solution.py:471
  86.8 19.1 %attend.2 = (bf16[1536,320]{1,0:T(8,128)(2,1)S(1)}, f32[1536,4]{1,0:T(8,128)S(1)}) custom-call(bf16[1536,960]{1,0:T(8,128)(2,1)S(1)} %add_convert_fusion.1.qkv_ref, bf16[1536,48]{1,0:T(8,128)(2,1)S(1)} %get-tuple-element.319.mask_ref), custom_call_target="tpu_custom_call" | custom-call | flops 9663676416 | bytes 4423680 | tf_op jit(solution)/shard_map/attend/pallas_call | solution.py:208
  108.3 4.5 add_convert_fusion.qkv_ref
  113.1 18.7 %attend.3 = (bf16[1536,320]{1,0:T(8,128)(2,1)S(1)}, f32[1536,4]{1,0:T(8,128)S(1)}) custom-call(bf16[1536,960]{1,0:T(8,128)(2,1)S(1)} %add_convert_fusion.qkv_ref, bf16[1536,48]{1,0:T(8,128)(2,1)S(1)} %get-tuple-element.318.mask_ref), custom_call_target="tpu_custom_call" | custom-call | flops 9663676416 | bytes 4423680 | tf_op jit(solution)/shard_map/attend/pallas_call | solution.py:208
  143.1 4.5 place_output_weight.1
  147.6 3.5 fusion.130
  156.5 4.0 fusion.131
  161.8 15.6 %collective-permute-done.16.refs_2_ = bf16[384,1280]{1,0:T(8,128)(2,1)} collective-permute-done((bf16[384,1280]{1,0:T(8,128)(2,1)}, bf16[384,1280]{1,0:T(8,128)(2,1)}, u32[]{:S(2)}, u32[]{:S(2)}) %collective-permute-start.16) | collective-permute-done | bytes 983072 | tf_op jit(solution)/shard_map/ppermute | solution.py:42
  180.1 5.1 multiply_convert_fusion.7
  188.8 4.1 multiply_convert_fusion.6
  200.0 4.1 multiply_convert_fusion.4
  205.6 6.6 collective-permute-done.25.refs_6_
  215.1 5.0 multiply_convert_fusion.3
  220.1 4.7 convolution_convert_fusion.13
  227.3 4.0 multiply_convert_fusion.2
  231.4 3.8 convolution_convert_fusion.12
  244.4 7.0 %collective-permute-done.23 = bf16[384,1280]{1,0:T(8,128)(2,1)S(1)} collective-permute-done((bf16[384,1280]{1,0:T(8,128)(2,1)S(1)}, bf16[384,1280]{1,0:T(8,128)(2,1)S(1)}, u32[]{:S(2)}, u32[]{:S(2)}) %collective-permute-start.23) | collective-permute-done | bytes 983072 | tf_op jit(solution)/shard_map/ppermute | solution.py:42
  253.5 19.1 %collective-permute-done.29 = bf16[384,1280]{1,0:T(8,128)(2,1)S(1)} collective-permute-done((bf16[384,1280]{1,0:T(8,128)(2,1)S(1)}, bf16[384,1280]{1,0:T(8,128)(2,1)S(1)}, u32[]{:S(2)}, u32[]{:S(2)}) %collective-permute-start.29) | collective-permute-done | bytes 983072 | tf_op jit(solution)/shard_map/ppermute | solution.py:42
  282.3 10.7 %collective-permute-done.31.refs_10_ = bf16[384,1280]{1,0:T(8,128)(2,1)S(1)} collective-permute-done((bf16[384,1280]{1,0:T(8,128)(2,1)S(1)}, bf16[384,1280]{1,0:T(8,128)(2,1)S(1)}, u32[]{:S(2)}, u32[]{:S(2)}) %collective-permute-start.31) | collective-permute-done | bytes 983072 | tf_op jit(solution)/shard_map/ppermute | solution.py:42
  311.7 13.3 %collective-permute-done.37.refs_14_ = bf16[384,1280]{1,0:T(8,128)(2,1)S(1)} collective-permute-done((bf16[384,1280]{1,0:T(8,128)(2,1)S(1)}, bf16[384,1280]{1,0:T(8,128)(2,1)S(1)}, u32[]{:S(2)}, u32[]{:S(2)}) %collective-permute-start.37) | collective-permute-done | bytes 983072 | tf_op jit(solution)/shard_map/ppermute | solution.py:42
  342.3 14.9 %collective-permute-done.35 = bf16[384,1280]{1,0:T(8,128)(2,1)S(1)} collective-permute-done((bf16[384,1280]{1,0:T(8,128)(2,1)S(1)}, bf16[384,1280]{1,0:T(8,128)(2,1)S(1)}, u32[]{:S(2)}, u32[]{:S(2)}) %collective-permute-start.35) | collective-permute-done | bytes 983072 | tf_op jit(solution)/shard_map/ppermute | solution.py:42
  358.9 3.3 convert_reduce_fusion.15
  364.8 19.7 %products.4.refs_16_ = bf16[1280,2560]{1,0:T(8,128)(2,1)} custom-call(bf16[384,1280]{1,0:T(8,128)(2,1)} %copy-done.114, bf16[384,1280]{1,0:T(8,128)(2,1)} %copy-done.113, bf16[384,1280]{1,0:T(8,128)(2,1)} %copy-done.112, bf16[384,1280]{1,0:T(8,128)(2,1)} %copy-done.111, bf16[384,1280]{1,0:T(8,128)(2,1)} %copy-done.118, bf16[384,1280]{1,0:T(8,128)(2,1)} %copy-done.117, ...), custom_call_target="tpu_custom_call" | custom-call | flops 10066329600 | bytes 15728640 | tf_op jit(solution)/shard_map/products/pallas_call | solution.py:317
  384.5 20.1 %products.5 = bf16[1280,2560]{1,0:T(8,128)(2,1)} custom-call(bf16[384,1280]{1,0:T(8,128)(2,1)} %add_convert_fusion.11.refs_0_, bf16[384,1280]{1,0:T(8,128)(2,1)} %copy-done.96, bf16[384,1280]{1,0:T(8,128)(2,1)} %collective-permute-done.16.refs_2_, bf16[384,1280]{1,0:T(8,128)(2,1)} %copy-done.95, ...), custom_call_target="tpu_custom_call", output_to_operand_aliasing={{}: (16, {})} | custom-call | flops 10066329600 | bytes 15728640 | tf_op jit(solution)/shard_map/products/pallas_call | solution.py:317
  407.7 4.4 convert_reduce_fusion.14
  414.8 7.7 %products.6.full = bf16[1280,1280]{1,0:T(8,128)(2,1)} custom-call(bf16[384,1280]{1,0:T(8,128)(2,1)} %copy-done.50, bf16[384,1280]{1,0:T(8,128)(2,1)} %copy-done.51, bf16[384,1280]{1,0:T(8,128)(2,1)} %copy-done.55, bf16[384,1280]{1,0:T(8,128)(2,1)} %copy-done.57), custom_call_target="tpu_custom_call" | custom-call | flops 2516582400 | bytes 3932160 | tf_op jit(solution)/shard_map/products/pallas_call | solution.py:317
  422.5 4.7 split_output_weight.1
  434.1 4.5 collective-permute-done.41
  438.6 4.5 collective-permute-done.42
  448.4 37.3 %attend_back.2.refs_2_.grad = bf16[1536,960]{1,0:T(8,128)(2,1)} custom-call(bf16[1536,960]{1,0:T(8,128)(2,1)} %copy-done.19, bf16[1536,48]{1,0:T(8,128)(2,1)} %copy-done.15, bf16[1536,320]{1,0:T(8,128)(2,1)} %pad_maximum_fusion.2.grad_ref, f32[1536,4]{1,0:T(8,128)} %copy-done.21), custom_call_target="tpu_custom_call" | custom-call | flops 48318382080 | bytes 7372800 | tf_op jit(solution)/shard_map/attend_back/pallas_call | solution.py:229
  489.3 37.0 %attend_back.3.refs_3_.grad = bf16[1536,960]{1,0:T(8,128)(2,1)} custom-call(bf16[1536,960]{1,0:T(8,128)(2,1)} %copy-done.18, bf16[1536,48]{1,0:T(8,128)(2,1)} %copy-done.14, bf16[1536,320]{1,0:T(8,128)(2,1)} %pad_maximum_fusion.3.grad_ref, f32[1536,4]{1,0:T(8,128)} %copy-done.20), custom_call_target="tpu_custom_call" | custom-call | flops 48318382080 | bytes 7372800 | tf_op jit(solution)/shard_map/attend_back/pallas_call | solution.py:229
  528.3 14.0 %products.7 = bf16[1280,1280]{1,0:T(8,128)(2,1)} custom-call(bf16[1536,1280]{1,0:T(8,128)(2,1)} %norm_blocks.2.refs_0_, bf16[1536,1280]{1,0:T(8,128)(2,1)} %norm_blocks.3.refs_1_, bf16[1536,960]{1,0:T(8,128)(2,1)} %attend_back.2.refs_2_.grad, bf16[1536,960]{1,0:T(8,128)(2,1)} %attend_back.3.refs_3_.grad, bf16[1280,384]{1,0:T(8,128)(2,1)} %add_convert_fusion.4.refs_4_), custom_call_target="tpu_custom_call" | custom-call | flops 10066329600 | bytes 15728640 | tf_op jit(solution)/shard_map/products/pallas_call | solution.py:317
  544.2 5.2 spread_terms.2
  554.1 5.2 spread_terms.3
  569.3 20.0 %collective-permute-done.53 = bf16[384,1280]{1,0:T(8,128)(2,1)} collective-permute-done((bf16[384,1280]{1,0:T(8,128)(2,1)}, bf16[384,1280]{1,0:T(8,128)(2,1)}, u32[]{:S(2)}, u32[]{:S(2)}) %collective-permute-start.53) | collective-permute-done | bytes 983072 | tf_op jit(solution)/shard_map/ppermute | solution.py:42
  592.1 3.5 fusion.30
  595.6 14.0 %collective-permute-done.56 = bf16[384,1280]{1,0:T(8,128)(2,1)S(1)} collective-permute-done((bf16[384,1280]{1,0:T(8,128)(2,1)S(1)}, bf16[384,1280]{1,0:T(8,128)(2,1)S(1)}, u32[]{:S(2)}, u32[]{:S(2)}) %collective-permute-start.56) | collective-permute-done | bytes 983072 | tf_op jit(solution)/shard_map/ppermute | solution.py:42
  632.6 9.5 %collective-permute-done.61 = f32[1922]{0:T(1024)S(1)} collective-permute-done((f32[1922]{0:T(1024)S(1)}, f32[1922]{0:T(1024)S(1)}, u32[]{:S(2)}, u32[]{:S(2)}) %collective-permute-start.61) | collective-permute-done | bytes 7720 | tf_op jit(solution)/shard_map/ppermute | solution.py:42
  646.3 5.3 collective-permute-done.63.refs_2_
  654.9 3.7 assemble.5
  658.6 3.5 assemble.4
  662.0 3.7 pad_maximum_fusion
  (567 shorter events, 209.7 us)
Async XLA Ops:
  7.2 67.9 %all-gather.3.cloned.1.call-start = ((), (), s32[]{:S(2)}) async-start(), calls=%async_computation.2 | async-start | bytes 3686400 | tf_op jit(solution)/shard_map/all_gather | solution.py:497
  9.8 170.4 %all-gather.5.cloned.1.call-start = ((), (), s32[]{:S(2)}) async-start(), calls=%async_computation.3 | async-start | bytes 7372800 | tf_op jit(solution)/shard_map/all_gather | solution.py:502
  12.4 13.5 %collective-permute-start = (bf16[384,1280]{1,0:T(8,128)(2,1)}, bf16[384,1280]{1,0:T(8,128)(2,1)}, u32[]{:S(2)}, u32[]{:S(2)}) collective-permute-start(bf16[384,1280]{1,0:T(8,128)(2,1)} %get-tuple-element.264.refs_0_), channel_id=1, source_target_pairs={{0,1},{1,0},{2,3},{3,2},{4,5},{5,4},{6,7},{7,6},{8,9},{9,8},{10,11... | collective-permute-start | bytes 2949128 | tf_op jit(solution)/shard_map/ppermute | solution.py:42
  12.9 25.4 %collective-permute-start.1 = (bf16[384,1280]{1,0:T(8,128)(2,1)}, bf16[384,1280]{1,0:T(8,128)(2,1)}, u32[]{:S(2)}, u32[]{:S(2)}) collective-permute-start(bf16[384,1280]{1,0:T(8,128)(2,1)} %get-tuple-element.264.refs_0_), channel_id=1, source_target_pairs={{0,2},{1,3},{2,0},{3,1},{4,6},{5,7},{6,4},{7,5},{8,10},{9,11},{10,... | collective-permute-start | bytes 2949128 | tf_op jit(solution)/shard_map/ppermute | solution.py:42
  19.7 506.6 %reduce-scatter.3.cloned.1.call-start = ((), (), s32[]{:S(2)}) async-start(), calls=%async_computation.4 | async-start | bytes 7372800 | tf_op jit(solution)/shard_map/reduce_scatter | solution.py:562
  23.7 14.6 %collective-permute-start.4 = (bf16[2,1920]{1,0:T(2,128)(2,1)S(1)}, bf16[2,1920]{1,0:T(2,128)(2,1)S(1)}, u32[]{:S(2)}, u32[]{:S(2)}) collective-permute-start(bf16[2,1920]{1,0:T(2,128)(2,1)S(1)} %pad_maximum_fusion.6), channel_id=1, source_target_pairs={{0,8},{4,12},{8,0},{12,4},{16,24},{20,28},{24,16},{28,20},{1,9},{5... | collective-permute-start | bytes 23048 | tf_op jit(solution)/shard_map/ppermute | solution.py:42
  25.9 33.2 %collective-permute-start.7 = (bf16[384,1280]{1,0:T(8,128)(2,1)S(1)}, bf16[384,1280]{1,0:T(8,128)(2,1)}, u32[]{:S(2)}, u32[]{:S(2)}) collective-permute-start(bf16[384,1280]{1,0:T(8,128)(2,1)S(1)} %get-tuple-element.121.refs_0_), channel_id=1, source_target_pairs={{0,2},{1,3},{2,0},{3,1},{4,6},{5,7},{6,4},{7,5},{8,10},{9,11},{10,... | collective-permute-start | bytes 2949128 | tf_op jit(solution)/shard_map/ppermute | solution.py:42
  44.9 17.3 %collective-permute-start.6 = (bf16[384,1280]{1,0:T(8,128)(2,1)S(1)}, bf16[384,1280]{1,0:T(8,128)(2,1)}, u32[]{:S(2)}, u32[]{:S(2)}) collective-permute-start(bf16[384,1280]{1,0:T(8,128)(2,1)S(1)} %get-tuple-element.121.refs_0_), channel_id=1, source_target_pairs={{0,1},{1,0},{2,3},{3,2},{4,5},{5,4},{6,7},{7,6},{8,9},{9,8},{10,11... | collective-permute-start | bytes 2949128 | tf_op jit(solution)/shard_map/ppermute | solution.py:42
  78.1 34.7 %collective-permute-start.13 = (bf16[1280,320]{0,1:T(8,128)(2,1)}, bf16[1280,320]{0,1:T(8,128)(2,1)S(1)}, u32[]{:S(2)}, u32[]{:S(2)}) collective-permute-start(bf16[1280,320]{0,1:T(8,128)(2,1)} %copy.37), channel_id=1, source_target_pairs={{0,2},{1,3},{2,0},{3,1},{4,6},{5,7},{6,4},{7,5},{8,10},{9,11},{10,... | collective-permute-start | bytes 2457608 | tf_op jit(solution)/shard_map/ppermute | solution.py:42
  79.6 59.1 %collective-permute-start.12 = (bf16[1280,320]{0,1:T(8,128)(2,1)}, bf16[1280,320]{0,1:T(8,128)(2,1)}, u32[]{:S(2)}, u32[]{:S(2)}) collective-permute-start(bf16[1280,320]{0,1:T(8,128)(2,1)} %copy.37), channel_id=1, source_target_pairs={{0,1},{1,0},{2,3},{3,2},{4,5},{5,4},{6,7},{7,6},{8,9},{9,8},{10,11... | collective-permute-start | bytes 2457608 | tf_op jit(solution)/shard_map/ppermute | solution.py:42
  106.1 26.9 %collective-permute-start.10 = (bf16[384,320]{1,0:T(8,128)(2,1)S(1)}, bf16[384,320]{1,0:T(8,128)(2,1)S(1)}, u32[]{:S(2)}, u32[]{:S(2)}) collective-permute-start(bf16[384,320]{1,0:T(8,128)(2,1)S(1)} %get-tuple-element.281), channel_id=1, source_target_pairs={{0,2},{1,3},{2,0},{3,1},{4,6},{5,7},{6,4},{7,5},{8,10},{9,11},{10,... | collective-permute-start | bytes 737288 | tf_op jit(solution)/shard_map/ppermute | solution.py:42
  106.7 26.6 %collective-permute-start.11 = (bf16[384,320]{1,0:T(8,128)(2,1)S(1)}, bf16[384,320]{1,0:T(8,128)(2,1)S(1)}, u32[]{:S(2)}, u32[]{:S(2)}) collective-permute-start(bf16[384,320]{1,0:T(8,128)(2,1)S(1)} %get-tuple-element.280), channel_id=1, source_target_pairs={{0,3},{1,2},{2,1},{3,0},{4,7},{5,6},{6,5},{7,4},{8,11},{9,10},{10,... | collective-permute-start | bytes 737288 | tf_op jit(solution)/shard_map/ppermute | solution.py:42
  108.0 25.9 %collective-permute-start.9 = (bf16[384,320]{1,0:T(8,128)(2,1)S(1)}, bf16[384,320]{1,0:T(8,128)(2,1)S(1)}, u32[]{:S(2)}, u32[]{:S(2)}) collective-permute-start(bf16[384,320]{1,0:T(8,128)(2,1)S(1)} %get-tuple-element.282), channel_id=1, source_target_pairs={{0,1},{1,0},{2,3},{3,2},{4,5},{5,4},{6,7},{7,6},{8,9},{9,8},{10,11... | collective-permute-start | bytes 737288 | tf_op jit(solution)/shard_map/ppermute | solution.py:42
  112.8 28.0 %collective-permute-start.14 = (bf16[1280,320]{0,1:T(8,128)(2,1)S(1)}, bf16[1280,320]{0,1:T(8,128)(2,1)}, u32[]{:S(2)}, u32[]{:S(2)}) collective-permute-start(bf16[1280,320]{0,1:T(8,128)(2,1)S(1)} %collective-permute-done.13), channel_id=1, source_target_pairs={{0,1},{1,0},{2,3},{3,2},{4,5},{5,4},{6,7},{7,6},{8,9},{9,8},{10,11... | collective-permute-start | bytes 2457608 | tf_op jit(solution)/shard_map/ppermute | solution.py:42
  133.1 20.9 %collective-permute-start.17 = (bf16[384,320]{1,0:T(8,128)(2,1)}, bf16[384,320]{1,0:T(8,128)(2,1)}, u32[]{:S(2)}, u32[]{:S(2)}) collective-permute-start(bf16[384,320]{1,0:T(8,128)(2,1)} %get-tuple-element.278), channel_id=1, source_target_pairs={{0,1},{1,0},{2,3},{3,2},{4,5},{5,4},{6,7},{7,6},{8,9},{9,8},{10,11... | collective-permute-start | bytes 737288 | tf_op jit(solution)/shard_map/ppermute | solution.py:42
  133.3 20.6 %collective-permute-start.18 = (bf16[384,320]{1,0:T(8,128)(2,1)}, bf16[384,320]{1,0:T(8,128)(2,1)}, u32[]{:S(2)}, u32[]{:S(2)}) collective-permute-start(bf16[384,320]{1,0:T(8,128)(2,1)} %get-tuple-element.277), channel_id=1, source_target_pairs={{0,2},{1,3},{2,0},{3,1},{4,6},{5,7},{6,4},{7,5},{8,10},{9,11},{10,... | collective-permute-start | bytes 737288 | tf_op jit(solution)/shard_map/ppermute | solution.py:42
  133.9 20.0 %collective-permute-start.19 = (bf16[384,320]{1,0:T(8,128)(2,1)}, bf16[384,320]{1,0:T(8,128)(2,1)}, u32[]{:S(2)}, u32[]{:S(2)}) collective-permute-start(bf16[384,320]{1,0:T(8,128)(2,1)} %get-tuple-element.276), channel_id=1, source_target_pairs={{0,3},{1,2},{2,1},{3,0},{4,7},{5,6},{6,5},{7,4},{8,11},{9,10},{10,... | collective-permute-start | bytes 737288 | tf_op jit(solution)/shard_map/ppermute | solution.py:42
  152.8 24.6 %collective-permute-start.16 = (bf16[384,1280]{1,0:T(8,128)(2,1)}, bf16[384,1280]{1,0:T(8,128)(2,1)}, u32[]{:S(2)}, u32[]{:S(2)}) collective-permute-start(bf16[384,1280]{1,0:T(8,128)(2,1)} %add_convert_fusion.11.refs_0_), channel_id=1, source_target_pairs={{0,2},{1,3},{2,0},{3,1},{4,6},{5,7},{6,4},{7,5},{8,10},{9,11},{10,... | collective-permute-start | bytes 2949128 | tf_op jit(solution)/shard_map/ppermute | solution.py:42
  188.2 23.9 %collective-permute-start.25 = (bf16[384,1280]{1,0:T(8,128)(2,1)S(1)}, bf16[384,1280]{1,0:T(8,128)(2,1)}, u32[]{:S(2)}, u32[]{:S(2)}) collective-permute-start(bf16[384,1280]{1,0:T(8,128)(2,1)S(1)} %add_convert_fusion.10.refs_4_), channel_id=1, source_target_pairs={{0,2},{1,3},{2,0},{3,1},{4,6},{5,7},{6,4},{7,5},{8,10},{9,11},{10,... | collective-permute-start | bytes 2949128 | tf_op jit(solution)/shard_map/ppermute | solution.py:42
  226.7 17.7 %collective-permute-start.22 = (bf16[384,1280]{1,0:T(8,128)(2,1)}, bf16[384,1280]{1,0:T(8,128)(2,1)S(1)}, u32[]{:S(2)}, u32[]{:S(2)}) collective-permute-start(bf16[384,1280]{1,0:T(8,128)(2,1)} %convolution_convert_fusion.15), channel_id=1, source_target_pairs={{0,1},{1,0},{2,3},{3,2},{4,5},{5,4},{6,7},{7,6},{8,9},{9,8},{10,11... | collective-permute-start | bytes 2949128 | tf_op jit(solution)/shard_map/ppermute | solution.py:42
  226.8 24.6 %collective-permute-start.23 = (bf16[384,1280]{1,0:T(8,128)(2,1)S(1)}, bf16[384,1280]{1,0:T(8,128)(2,1)S(1)}, u32[]{:S(2)}, u32[]{:S(2)}) collective-permute-start(bf16[384,1280]{1,0:T(8,128)(2,1)S(1)} %add_convert_fusion.9), channel_id=1, source_target_pairs={{0,2},{1,3},{2,0},{3,1},{4,6},{5,7},{6,4},{7,5},{8,10},{9,11},{10,... | collective-permute-start | bytes 2949128 | tf_op jit(solution)/shard_map/ppermute | solution.py:42
  239.7 13.8 %collective-permute-start.28 = (bf16[384,1280]{1,0:T(8,128)(2,1)S(1)}, bf16[384,1280]{1,0:T(8,128)(2,1)S(1)}, u32[]{:S(2)}, u32[]{:S(2)}) collective-permute-start(bf16[384,1280]{1,0:T(8,128)(2,1)S(1)} %convolution_convert_fusion.11), channel_id=1, source_target_pairs={{0,1},{1,0},{2,3},{3,2},{4,5},{5,4},{6,7},{7,6},{8,9},{9,8},{10,11... | collective-permute-start | bytes 2949128 | tf_op jit(solution)/shard_map/ppermute | solution.py:42
  239.8 32.7 %collective-permute-start.29 = (bf16[384,1280]{1,0:T(8,128)(2,1)S(1)}, bf16[384,1280]{1,0:T(8,128)(2,1)S(1)}, u32[]{:S(2)}, u32[]{:S(2)}) collective-permute-start(bf16[384,1280]{1,0:T(8,128)(2,1)S(1)} %add_convert_fusion.8), channel_id=1, source_target_pairs={{0,2},{1,3},{2,0},{3,1},{4,6},{5,7},{6,4},{7,5},{8,10},{9,11},{10,... | collective-permute-start | bytes 2949128 | tf_op jit(solution)/shard_map/ppermute | solution.py:42
  252.9 26.7 %collective-permute-start.30 = (bf16[384,1280]{1,0:T(8,128)(2,1)S(1)}, bf16[384,1280]{1,0:T(8,128)(2,1)S(1)}, u32[]{:S(2)}, u32[]{:S(2)}) collective-permute-start(bf16[384,1280]{1,0:T(8,128)(2,1)S(1)} %get-tuple-element.155.refs_8_), channel_id=1, source_target_pairs={{0,1},{1,0},{2,3},{3,2},{4,5},{5,4},{6,7},{7,6},{8,9},{9,8},{10,11... | collective-permute-start | bytes 2949128 | tf_op jit(solution)/shard_map/ppermute | solution.py:42
  252.9 40.0 %collective-permute-start.31 = (bf16[384,1280]{1,0:T(8,128)(2,1)S(1)}, bf16[384,1280]{1,0:T(8,128)(2,1)S(1)}, u32[]{:S(2)}, u32[]{:S(2)}) collective-permute-start(bf16[384,1280]{1,0:T(8,128)(2,1)S(1)} %get-tuple-element.155.refs_8_), channel_id=1, source_target_pairs={{0,2},{1,3},{2,0},{3,1},{4,6},{5,7},{6,4},{7,5},{8,10},{9,11},{10,... | collective-permute-start | bytes 2949128 | tf_op jit(solution)/shard_map/ppermute | solution.py:42
  301.0 24.1 %collective-permute-start.37 = (bf16[384,1280]{1,0:T(8,128)(2,1)S(1)}, bf16[384,1280]{1,0:T(8,128)(2,1)S(1)}, u32[]{:S(2)}, u32[]{:S(2)}) collective-permute-start(bf16[384,1280]{1,0:T(8,128)(2,1)S(1)} %get-tuple-element.164.refs_12_), channel_id=1, source_target_pairs={{0,2},{1,3},{2,0},{3,1},{4,6},{5,7},{6,4},{7,5},{8,10},{9,11},{10,... | collective-permute-start | bytes 2949128 | tf_op jit(solution)/shard_map/ppermute | solution.py:42
  332.6 24.6 %collective-permute-start.35 = (bf16[384,1280]{1,0:T(8,128)(2,1)S(1)}, bf16[384,1280]{1,0:T(8,128)(2,1)S(1)}, u32[]{:S(2)}, u32[]{:S(2)}) collective-permute-start(bf16[384,1280]{1,0:T(8,128)(2,1)S(1)} %add_convert_fusion.7), channel_id=1, source_target_pairs={{0,2},{1,3},{2,0},{3,1},{4,6},{5,7},{6,4},{7,5},{8,10},{9,11},{10,... | collective-permute-start | bytes 2949128 | tf_op jit(solution)/shard_map/ppermute | solution.py:42
  338.3 66.4 %collective-permute-start.43 = (bf16[384,1280]{1,0:T(8,128)(2,1)}, bf16[384,1280]{1,0:T(8,128)(2,1)S(1)}, u32[]{:S(2)}, u32[]{:S(2)}) collective-permute-start(bf16[384,1280]{1,0:T(8,128)(2,1)} %convolution_convert_fusion.3), channel_id=1, source_target_pairs={{0,1},{1,0},{2,3},{3,2},{4,5},{5,4},{6,7},{7,6},{8,9},{9,8},{10,11... | collective-permute-start | bytes 2949128 | tf_op jit(solution)/shard_map/ppermute | solution.py:42
  338.7 66.0 %collective-permute-start.44 = (bf16[384,1280]{1,0:T(8,128)(2,1)}, bf16[384,1280]{1,0:T(8,128)(2,1)}, u32[]{:S(2)}, u32[]{:S(2)}) collective-permute-start(bf16[384,1280]{1,0:T(8,128)(2,1)} %add_convert_fusion.6), channel_id=1, source_target_pairs={{0,2},{1,3},{2,0},{3,1},{4,6},{5,7},{6,4},{7,5},{8,10},{9,11},{10,... | collective-permute-start | bytes 2949128 | tf_op jit(solution)/shard_map/ppermute | solution.py:42
  404.7 237.5 %reduce-scatter.5.cloned.1.call-start = ((), (), s32[]{:S(2)}) async-start(), calls=%async_computation.5 | async-start | bytes 3686400 | tf_op jit(solution)/shard_map/reduce_scatter | solution.py:562
  427.3 19.0 %collective-permute-start.49 = (bf16[1280,384]{1,0:T(8,128)(2,1)}, bf16[1280,384]{1,0:T(8,128)(2,1)}, u32[]{:S(2)}, u32[]{:S(2)}) collective-permute-start(bf16[1280,384]{1,0:T(8,128)(2,1)} %get-tuple-element.188), channel_id=1, source_target_pairs={{0,1},{1,0},{2,3},{3,2},{4,5},{5,4},{6,7},{7,6},{8,9},{9,8},{10,11... | collective-permute-start | bytes 2949128 | tf_op jit(solution)/shard_map/ppermute | solution.py:42
  429.1 14.1 %collective-permute-start.42 = (bf16[384,320]{1,0:T(8,128)(2,1)S(1)}, bf16[384,320]{1,0:T(8,128)(2,1)S(1)}, u32[]{:S(2)}, u32[]{:S(2)}) collective-permute-start(bf16[384,320]{1,0:T(8,128)(2,1)S(1)} %copy-done.62), channel_id=1, source_target_pairs={{0,3},{1,2},{2,1},{3,0},{4,7},{5,6},{6,5},{7,4},{8,11},{9,10},{10,... | collective-permute-start | bytes 737288 | tf_op jit(solution)/shard_map/ppermute | solution.py:42
  432.9 54.2 %collective-permute-start.45 = (bf16[384,320]{1,0:T(8,128)(2,1)}, bf16[384,320]{1,0:T(8,128)(2,1)}, u32[]{:S(2)}, u32[]{:S(2)}) collective-permute-start(bf16[384,320]{1,0:T(8,128)(2,1)} %get-tuple-element.286), channel_id=1, source_target_pairs={{0,1},{1,0},{2,3},{3,2},{4,5},{5,4},{6,7},{7,6},{8,9},{9,8},{10,11... | collective-permute-start | bytes 737288 | tf_op jit(solution)/shard_map/ppermute | solution.py:42
  433.8 53.3 %collective-permute-start.46 = (bf16[384,320]{1,0:T(8,128)(2,1)S(1)}, bf16[384,320]{1,0:T(8,128)(2,1)}, u32[]{:S(2)}, u32[]{:S(2)}) collective-permute-start(bf16[384,320]{1,0:T(8,128)(2,1)S(1)} %copy-done.64), channel_id=1, source_target_pairs={{0,2},{1,3},{2,0},{3,1},{4,6},{5,7},{6,4},{7,5},{8,10},{9,11},{10,... | collective-permute-start | bytes 737288 | tf_op jit(solution)/shard_map/ppermute | solution.py:42
  438.6 48.4 %collective-permute-start.47 = (bf16[384,320]{1,0:T(8,128)(2,1)S(1)}, bf16[384,320]{1,0:T(8,128)(2,1)}, u32[]{:S(2)}, u32[]{:S(2)}) collective-permute-start(bf16[384,320]{1,0:T(8,128)(2,1)S(1)} %copy-done.63), channel_id=1, source_target_pairs={{0,3},{1,2},{2,1},{3,0},{4,7},{5,6},{6,5},{7,4},{8,11},{9,10},{10,... | collective-permute-start | bytes 737288 | tf_op jit(solution)/shard_map/ppermute | solution.py:42
  443.1 42.6 %collective-permute-start.48 = (bf16[1280,384]{1,0:T(8,128)(2,1)}, bf16[1280,384]{1,0:T(8,128)(2,1)S(1)}, u32[]{:S(2)}, u32[]{:S(2)}) collective-permute-start(bf16[1280,384]{1,0:T(8,128)(2,1)} %get-tuple-element.186), channel_id=1, source_target_pairs={{0,1},{1,0},{2,3},{3,2},{4,5},{5,4},{6,7},{7,6},{8,9},{9,8},{10,11... | collective-permute-start | bytes 2949128 | tf_op jit(solution)/shard_map/ppermute | solution.py:42
  447.8 37.9 %collective-permute-start.50 = (bf16[1280,384]{1,0:T(8,128)(2,1)S(1)}, bf16[1280,384]{1,0:T(8,128)(2,1)S(1)}, u32[]{:S(2)}, u32[]{:S(2)}) collective-permute-start(bf16[1280,384]{1,0:T(8,128)(2,1)S(1)} %add_convert_fusion.5), channel_id=1, source_target_pairs={{0,2},{1,3},{2,0},{3,1},{4,6},{5,7},{6,4},{7,5},{8,10},{9,11},{10,... | collective-permute-start | bytes 2949128 | tf_op jit(solution)/shard_map/ppermute | solution.py:42
  551.4 10.6 %collective-permute-start.52 = (bf16[384,1280]{1,0:T(8,128)(2,1)}, bf16[384,1280]{1,0:T(8,128)(2,1)}, u32[]{:S(2)}, u32[]{:S(2)}) collective-permute-start(bf16[384,1280]{1,0:T(8,128)(2,1)} %get-tuple-element.198), channel_id=1, source_target_pairs={{0,1},{1,0},{2,3},{3,2},{4,5},{5,4},{6,7},{7,6},{8,9},{9,8},{10,11... | collective-permute-start | bytes 2949128 | tf_op jit(solution)/shard_map/ppermute | solution.py:42
  564.3 24.9 %collective-permute-start.53 = (bf16[384,1280]{1,0:T(8,128)(2,1)}, bf16[384,1280]{1,0:T(8,128)(2,1)}, u32[]{:S(2)}, u32[]{:S(2)}) collective-permute-start(bf16[384,1280]{1,0:T(8,128)(2,1)} %add_convert_fusion.3), channel_id=1, source_target_pairs={{0,2},{1,3},{2,0},{3,1},{4,6},{5,7},{6,4},{7,5},{8,10},{9,11},{10,... | collective-permute-start | bytes 2949128 | tf_op jit(solution)/shard_map/ppermute | solution.py:42
  567.0 28.6 %collective-permute-start.54 = (bf16[384,1280]{1,0:T(8,128)(2,1)S(1)}, bf16[384,1280]{1,0:T(8,128)(2,1)S(1)}, u32[]{:S(2)}, u32[]{:S(2)}) collective-permute-start(bf16[384,1280]{1,0:T(8,128)(2,1)S(1)} %copy-done.17), channel_id=1, source_target_pairs={{0,1},{1,0},{2,3},{3,2},{4,5},{5,4},{6,7},{7,6},{8,9},{9,8},{10,11... | collective-permute-start | bytes 2949128 | tf_op jit(solution)/shard_map/ppermute | solution.py:42
  568.7 40.9 %collective-permute-start.56 = (bf16[384,1280]{1,0:T(8,128)(2,1)S(1)}, bf16[384,1280]{1,0:T(8,128)(2,1)S(1)}, u32[]{:S(2)}, u32[]{:S(2)}) collective-permute-start(bf16[384,1280]{1,0:T(8,128)(2,1)S(1)} %add_convert_fusion.2), channel_id=1, source_target_pairs={{0,2},{1,3},{2,0},{3,1},{4,6},{5,7},{6,4},{7,5},{8,10},{9,11},{10,... | collective-permute-start | bytes 2949128 | tf_op jit(solution)/shard_map/ppermute | solution.py:42
  623.8 20.0 %collective-permute-start.69 = (bf16[160,1280]{1,0:T(8,128)(2,1)S(1)}, bf16[160,1280]{1,0:T(8,128)(2,1)}, u32[]{:S(2)}, u32[]{:S(2)}) collective-permute-start(bf16[160,1280]{1,0:T(8,128)(2,1)S(1)} %copy-done.47), channel_id=1, source_target_pairs={{0,2},{1,3},{2,0},{3,1},{4,6},{5,7},{6,4},{7,5},{8,10},{9,11},{10,... | collective-permute-start | bytes 1228808 | tf_op jit(solution)/shard_map/ppermute | solution.py:42
  625.4 18.9 %collective-permute-start.66 = (bf16[160,1280]{1,0:T(8,128)(2,1)S(1)}, bf16[160,1280]{1,0:T(8,128)(2,1)}, u32[]{:S(2)}, u32[]{:S(2)}) collective-permute-start(bf16[160,1280]{1,0:T(8,128)(2,1)S(1)} %get-tuple-element.214.refs_0_), channel_id=1, source_target_pairs={{0,2},{1,3},{2,0},{3,1},{4,6},{5,7},{6,4},{7,5},{8,10},{9,11},{10,... | collective-permute-start | bytes 1228808 | tf_op jit(solution)/shard_map/ppermute | solution.py:42
  631.2 11.0 %collective-permute-start.61 = (f32[1922]{0:T(1024)S(1)}, f32[1922]{0:T(1024)S(1)}, u32[]{:S(2)}, u32[]{:S(2)}) collective-permute-start(f32[1922]{0:T(1024)S(1)} %add.680), channel_id=1, source_target_pairs={{0,2},{1,3},{2,0},{3,1},{4,6},{5,7},{6,4},{7,5},{8,10},{9,11},{10,... | collective-permute-start | bytes 23072 | tf_op jit(solution)/shard_map/ppermute | solution.py:42
  632.6 13.2 %collective-permute-start.68 = (bf16[160,1280]{1,0:T(8,128)(2,1)S(1)}, bf16[160,1280]{1,0:T(8,128)(2,1)}, u32[]{:S(2)}, u32[]{:S(2)}) collective-permute-start(bf16[160,1280]{1,0:T(8,128)(2,1)S(1)} %copy-done.47), channel_id=1, source_target_pairs={{0,1},{1,0},{2,3},{3,2},{4,5},{5,4},{6,7},{7,6},{8,9},{9,8},{10,11... | collective-permute-start | bytes 1228808 | tf_op jit(solution)/shard_map/ppermute | solution.py:42
  644.3 10.6 %collective-permute-start.67 = (bf16[160,1280]{1,0:T(8,128)(2,1)}, bf16[160,1280]{1,0:T(8,128)(2,1)}, u32[]{:S(2)}, u32[]{:S(2)}) collective-permute-start(bf16[160,1280]{1,0:T(8,128)(2,1)} %collective-permute-done.66.refs_2_), channel_id=1, source_target_pairs={{0,1},{1,0},{2,3},{3,2},{4,5},{5,4},{6,7},{7,6},{8,9},{9,8},{10,11... | collective-permute-start | bytes 1228808 | tf_op jit(solution)/shard_map/ppermute | solution.py:42
  645.8 19.9 %collective-permute-start.62 = (bf16[160,1280]{1,0:T(8,128)(2,1)S(1)}, bf16[160,1280]{1,0:T(8,128)(2,1)S(1)}, u32[]{:S(2)}, u32[]{:S(2)}) collective-permute-start(bf16[160,1280]{1,0:T(8,128)(2,1)S(1)} %copy-done.48), channel_id=1, source_target_pairs={{0,1},{1,0},{2,3},{3,2},{4,5},{5,4},{6,7},{7,6},{8,9},{9,8},{10,11... | collective-permute-start | bytes 1228808 | tf_op jit(solution)/shard_map/ppermute | solution.py:42
  651.6 14.1 %collective-permute-start.64 = (bf16[160,1280]{1,0:T(8,128)(2,1)}, bf16[160,1280]{1,0:T(8,128)(2,1)}, u32[]{:S(2)}, u32[]{:S(2)}) collective-permute-start(bf16[160,1280]{1,0:T(8,128)(2,1)} %collective-permute-done.63.refs_2_), channel_id=1, source_target_pairs={{0,1},{1,0},{2,3},{3,2},{4,5},{5,4},{6,7},{7,6},{8,9},{9,8},{10,11... | collective-permute-start | bytes 1228808 | tf_op jit(solution)/shard_map/ppermute | solution.py:42
  (156 other events, 1276.8 us)
Sparse Core Ops, SparseCore 0:
  10.8 64.3 all-gather.2
  77.3 100.5 all-gather.4
  404.8 119.6 reduce-scatter.2
  566.5 74.1 reduce-scatter.4

commit v4 on v3

--- a/solution.py
+++ b/solution.py
@@ -204,7 +204,7 @@
 
 def attend(qkv, mask, heads, dim, scale):
     seq = qkv.shape[0]
-    block = 256
+    block = next(b for b in (768, 512, 256, seq) if seq % b == 0)
     return pl.pallas_call(
         functools.partial(attend_kernel, heads, dim, block, scale),
         out_shape=(
@@ -225,7 +225,7 @@
 
 def attend_back(qkv, mask, grad, lse, heads, dim, scale):
     seq = qkv.shape[0]
-    block = 256
+    block = next(b for b in (768, 512, 256, seq) if seq % b == 0)
     return pl.pallas_call(
         functools.partial(attend_back_kernel, heads, dim, block, scale),
         out_shape=jax.ShapeDtypeStruct(qkv.shape, half),
@@ -687,9 +687,9 @@
         return [step.after(lefts[0])] + lefts[1:]
 
     joined = part == depth
-    norm2(first_clip)
     grad_wdown = products(ordered(flat(actives)), flat(pieces), half, slots=1 + joined)
     step.mark(grad_wdown)
+    norm2(first_clip)
     grad_wup = products(
         ordered(flat(hiddens)), flat(grad_uppers), half,
         **(dict(into=grad_wdown, slot=1, slots=2) if joined else {}),
@@ -702,6 +702,7 @@
         grad_wdown, grad_wup = owned(grad_wdown), owned(grad_wup)
     for c in others:
         norm2(c)
+    step.also(*grad_heads[first_clip][1:])
     grad_wout = products(ordered(contexts), grad_branches, half)
     step.mark(grad_wout)
     quarters = arrange(

time: 683 us -> 675 us (0.988)
  Pallas kernels: 222 us -> 209 us
  waiting for transfers between devices: 182 us -> 172 us
    ppermute x71, waiting for transfers between devices: 177 us -> 148 us  [flip(): lax.ppermute(tensor, axis, [(i, i ^ bits) for i in range(lax.axis_size(ax...]
    reduce_scatter x2, waiting for transfers between devices: 0.01 us -> 16.5 us  [owned(): return lax.psum_scatter(grad, 'fsdp', scatter_dimension=0, tiled=True)]
    pallas_call x2, Pallas kernels: 74.4 us -> 65.6 us  [attend_back(): pl.pallas_call(functools.partial(attend_back_kernel, heads, dim, block, s...]
    unnamed x258 -> x262, local copies, waits for them, and re-layouts: 16.5 us -> 16.6 us
  transfers between devices with their start and end apart: 75 -> 75, of which waited for: 26 -> 23; matrix products, arithmetic and copies ran while one was open for 25% -> 26% of each run, Pallas kernels for 29% -> 28%
where the time goes in v4:
time: 675 us; the launch traced here: 665 us
  Pallas kernels  209 us (31%)
  waiting for transfers between devices  172 us (25%)
  matrix products  106 us (16%)
  other arithmetic  60.1 us (9%)
  local copies, waits for them, and re-layouts  54.4 us (8%)
  starting transfers between devices  47.3 us (7%)
  between operations  17.6 us (3%)
    ppermute x71, waiting for transfers between devices, flip(): lax.ppermute(tensor, axis, [(i, i ^ bits) for i in range(lax.axis_size(ax...  148 us
    pallas_call x2, Pallas kernels, attend_back(): pl.pallas_call(functools.partial(attend_back_kernel, heads, dim, block, s...  65.6 us
    dot_general x20, matrix products, dot(): return jnp.dot(a, b, preferred_element_type=single)  65.1 us
    pallas_call x4, Pallas kernels, products(): pl.pallas_call(body, grid=(rows // tile,), in_specs=in_specs, out_specs=p...  61.5 us
    ppermute x71, starting transfers between devices, flip(): lax.ppermute(tensor, axis, [(i, i ^ bits) for i in range(lax.axis_size(ax...  47.1 us
    dot_general x18, matrix products, dot_t(): lax.dot_general(a, b, (((1,), (1,)), ((), ())), preferred_element_type=si...  40.4 us
    pallas_call x2, Pallas kernels, attend(): pl.pallas_call(functools.partial(attend_kernel, heads, dim, block, scale)...  33.5 us
    unnamed x262, local copies, waits for them, and re-layouts  16.6 us
  transfers between devices with their start and end apart: 75, of which 23 were waited for; matrix products, arithmetic and copies ran while one was open for 26% of the time, Pallas kernels for 28%

profile of v4, /device:TPU:0, one launch (start us, length us, event | category | flops | bytes accessed | tf_op | source)
XLA Modules:
  0.0 665.3 jit_solution(5737634470450014294)
XLA Ops:
  26.4 11.8 %collective-permute-done.1.refs_2_ = bf16[384,1280]{1,0:T(8,128)(2,1)} collective-permute-done((bf16[384,1280]{1,0:T(8,128)(2,1)}, bf16[384,1280]{1,0:T(8,128)(2,1)}, u32[]{:S(2)}, u32[]{:S(2)}) %collective-permute-start.1) | collective-permute-done | bytes 983072 | tf_op jit(solution)/shard_map/ppermute | solution.py:42
  38.3 3.2 collective-permute-start.5
  45.8 7.5 %norm_blocks.2.refs_0_ = bf16[1536,1280]{1,0:T(8,128)(2,1)} custom-call(bf16[384,1280]{1,0:T(8,128)(2,1)} %get-tuple-element.264.refs_0_, bf16[384,1280]{1,0:T(8,128)(2,1)} %collective-permute-done.refs_1_, bf16[384,1280]{1,0:T(8,128)(2,1)} %collective-permute-done.1.refs_2_, bf16[384,1280]{1,0:T(8,128)(2,1)} %copy-done.57, f32[1,1280]{1,0:T(1,128)} %reshape.306.refs_4_, ...), custom_call_target="tpu_custom_call" | custom-call | flops 19660800 | bytes 7864320 | tf_op jit(solution)/shard_map/norm_blocks/pallas_call | solution.py:266
  53.4 5.8 collective-permute-done.7.refs_2_
  62.2 7.6 %norm_blocks.3.refs_1_ = bf16[1536,1280]{1,0:T(8,128)(2,1)} custom-call(bf16[384,1280]{1,0:T(8,128)(2,1)} %copy-done.46, bf16[384,1280]{1,0:T(8,128)(2,1)} %collective-permute-done.6.refs_1_, bf16[384,1280]{1,0:T(8,128)(2,1)} %collective-permute-done.7.refs_2_, bf16[384,1280]{1,0:T(8,128)(2,1)} %collective-permute-done.8.refs_3_, ...), custom_call_target="tpu_custom_call" | custom-call | flops 19660800 | bytes 7864320 | tf_op jit(solution)/shard_map/norm_blocks/pallas_call | solution.py:266
  69.8 5.4 all-gather.3.cloned.1.call-done
  79.6 7.2 %add_convert_fusion.1.qkv_ref = bf16[1536,960]{1,0:T(8,128)(2,1)S(1)} fusion(bf16[1536,1280]{1,0:T(8,128)(2,1)} %norm_blocks.2.refs_0_, f32[960]{0:T(1024)S(1)} %bitcast.110, bf16[1280,1280]{1,0:T(8,128)(2,1)} %all-gather.3.cloned.1.call-done), kind=kOutput, calls=%fused_computation.4 | convolution fusion | flops 3777822720 | bytes 9506560 | tf_op jit(solution)/shard_map/dot_general | solution.py:471
  86.8 16.9 %attend.2 = (bf16[1536,320]{1,0:T(8,128)(2,1)S(1)}, f32[1536,4]{1,0:T(8,128)S(1)}) custom-call(bf16[1536,960]{1,0:T(8,128)(2,1)S(1)} %add_convert_fusion.1.qkv_ref, bf16[1536,48]{1,0:T(8,128)(2,1)S(1)} %get-tuple-element.319.mask_ref), custom_call_target="tpu_custom_call" | custom-call | flops 9663676416 | bytes 4423680 | tf_op jit(solution)/shard_map/attend/pallas_call | solution.py:208
  106.1 4.5 add_convert_fusion.qkv_ref
  110.9 16.6 %attend.3 = (bf16[1536,320]{1,0:T(8,128)(2,1)S(1)}, f32[1536,4]{1,0:T(8,128)S(1)}) custom-call(bf16[1536,960]{1,0:T(8,128)(2,1)S(1)} %add_convert_fusion.qkv_ref, bf16[1536,48]{1,0:T(8,128)(2,1)S(1)} %get-tuple-element.318.mask_ref), custom_call_target="tpu_custom_call" | custom-call | flops 9663676416 | bytes 4423680 | tf_op jit(solution)/shard_map/attend/pallas_call | solution.py:208
  138.8 5.0 place_output_weight.1
  143.8 3.5 fusion.130
  152.4 3.8 fusion.131
  157.5 16.0 %collective-permute-done.16.refs_2_ = bf16[384,1280]{1,0:T(8,128)(2,1)} collective-permute-done((bf16[384,1280]{1,0:T(8,128)(2,1)}, bf16[384,1280]{1,0:T(8,128)(2,1)}, u32[]{:S(2)}, u32[]{:S(2)}) %collective-permute-start.16) | collective-permute-done | bytes 983072 | tf_op jit(solution)/shard_map/ppermute | solution.py:42
  178.0 4.9 multiply_convert_fusion.7
  187.3 4.1 multiply_convert_fusion.6
  198.5 4.1 multiply_convert_fusion.4
  204.1 5.6 collective-permute-done.25.refs_6_
  212.6 5.0 multiply_convert_fusion.3
  217.6 4.7 convolution_convert_fusion.13
  225.8 4.0 multiply_convert_fusion.2
  229.8 3.8 convolution_convert_fusion.12
  241.9 7.0 %collective-permute-done.23 = bf16[384,1280]{1,0:T(8,128)(2,1)S(1)} collective-permute-done((bf16[384,1280]{1,0:T(8,128)(2,1)S(1)}, bf16[384,1280]{1,0:T(8,128)(2,1)S(1)}, u32[]{:S(2)}, u32[]{:S(2)}) %collective-permute-start.23) | collective-permute-done | bytes 983072 | tf_op jit(solution)/shard_map/ppermute | solution.py:42
  251.9 18.2 %collective-permute-done.29 = bf16[384,1280]{1,0:T(8,128)(2,1)S(1)} collective-permute-done((bf16[384,1280]{1,0:T(8,128)(2,1)S(1)}, bf16[384,1280]{1,0:T(8,128)(2,1)S(1)}, u32[]{:S(2)}, u32[]{:S(2)}) %collective-permute-start.29) | collective-permute-done | bytes 983072 | tf_op jit(solution)/shard_map/ppermute | solution.py:42
  279.9 10.6 %collective-permute-done.31.refs_10_ = bf16[384,1280]{1,0:T(8,128)(2,1)S(1)} collective-permute-done((bf16[384,1280]{1,0:T(8,128)(2,1)S(1)}, bf16[384,1280]{1,0:T(8,128)(2,1)S(1)}, u32[]{:S(2)}, u32[]{:S(2)}) %collective-permute-start.31) | collective-permute-done | bytes 983072 | tf_op jit(solution)/shard_map/ppermute | solution.py:42
  312.7 9.6 %collective-permute-done.37.refs_14_ = bf16[384,1280]{1,0:T(8,128)(2,1)S(1)} collective-permute-done((bf16[384,1280]{1,0:T(8,128)(2,1)S(1)}, bf16[384,1280]{1,0:T(8,128)(2,1)S(1)}, u32[]{:S(2)}, u32[]{:S(2)}) %collective-permute-start.37) | collective-permute-done | bytes 983072 | tf_op jit(solution)/shard_map/ppermute | solution.py:42
  340.0 19.7 %products.4.refs_16_ = bf16[1280,2560]{1,0:T(8,128)(2,1)} custom-call(bf16[384,1280]{1,0:T(8,128)(2,1)} %copy-done.116, bf16[384,1280]{1,0:T(8,128)(2,1)} %copy-done.115, bf16[384,1280]{1,0:T(8,128)(2,1)} %copy-done.114, bf16[384,1280]{1,0:T(8,128)(2,1)} %copy-done.113, bf16[384,1280]{1,0:T(8,128)(2,1)} %copy-done.120, bf16[384,1280]{1,0:T(8,128)(2,1)} %copy-done.119, ...), custom_call_target="tpu_custom_call" | custom-call | flops 10066329600 | bytes 15728640 | tf_op jit(solution)/shard_map/products/pallas_call | solution.py:317
  359.7 3.6 multiply_reduce_fusion.1
  363.4 4.6 convert_reduce_fusion.15
  372.5 19.9 %products.5 = bf16[1280,2560]{1,0:T(8,128)(2,1)} custom-call(bf16[384,1280]{1,0:T(8,128)(2,1)} %add_convert_fusion.11.refs_0_, bf16[384,1280]{1,0:T(8,128)(2,1)} %copy-done.98, bf16[384,1280]{1,0:T(8,128)(2,1)} %collective-permute-done.16.refs_2_, bf16[384,1280]{1,0:T(8,128)(2,1)} %copy-done.97, ...), custom_call_target="tpu_custom_call", output_to_operand_aliasing={{}: (16, {})} | custom-call | flops 10066329600 | bytes 15728640 | tf_op jit(solution)/shard_map/products/pallas_call | solution.py:317
  395.4 4.4 convert_reduce_fusion.14
  402.4 7.8 %products.6.full = bf16[1280,1280]{1,0:T(8,128)(2,1)} custom-call(bf16[384,1280]{1,0:T(8,128)(2,1)} %copy-done.53, bf16[384,1280]{1,0:T(8,128)(2,1)} %copy-done.54, bf16[384,1280]{1,0:T(8,128)(2,1)} %copy-done.58, bf16[384,1280]{1,0:T(8,128)(2,1)} %copy-done.60), custom_call_target="tpu_custom_call" | custom-call | flops 2516582400 | bytes 3932160 | tf_op jit(solution)/shard_map/products/pallas_call | solution.py:317
  410.2 4.7 split_output_weight.1
  426.4 33.2 %attend_back.2.refs_2_.grad = bf16[1536,960]{1,0:T(8,128)(2,1)} custom-call(bf16[1536,960]{1,0:T(8,128)(2,1)} %copy-done.19, bf16[1536,48]{1,0:T(8,128)(2,1)} %copy-done.15, bf16[1536,320]{1,0:T(8,128)(2,1)} %pad_maximum_fusion.2.grad_ref, f32[1536,4]{1,0:T(8,128)} %copy-done.21), custom_call_target="tpu_custom_call" | custom-call | flops 48318382080 | bytes 7372800 | tf_op jit(solution)/shard_map/attend_back/pallas_call | solution.py:229
  463.2 32.5 %attend_back.3.refs_3_.grad = bf16[1536,960]{1,0:T(8,128)(2,1)} custom-call(bf16[1536,960]{1,0:T(8,128)(2,1)} %copy-done.18, bf16[1536,48]{1,0:T(8,128)(2,1)} %copy-done.14, bf16[1536,320]{1,0:T(8,128)(2,1)} %pad_maximum_fusion.3.grad_ref, f32[1536,4]{1,0:T(8,128)} %copy-done.20), custom_call_target="tpu_custom_call" | custom-call | flops 48318382080 | bytes 7372800 | tf_op jit(solution)/shard_map/attend_back/pallas_call | solution.py:229
  495.7 16.5 %reduce-scatter.3.cloned.1.call-done = bf16[160,2560]{1,0:T(8,128)(2,1)} async-done(((bf16[1280,2560]{1,0:T(8,128)(2,1)}), bf16[160,2560]{1,0:T(8,128)(2,1)}) %reduce-scatter.3.cloned.1.call-update) | async-done | bytes 819216 | tf_op jit(solution)/shard_map/reduce_scatter | solution.py:562
  514.1 14.2 %products.7 = bf16[1280,1280]{1,0:T(8,128)(2,1)} custom-call(bf16[1536,1280]{1,0:T(8,128)(2,1)} %norm_blocks.2.refs_0_, bf16[1536,1280]{1,0:T(8,128)(2,1)} %norm_blocks.3.refs_1_, bf16[1536,960]{1,0:T(8,128)(2,1)} %attend_back.2.refs_2_.grad, bf16[1536,960]{1,0:T(8,128)(2,1)} %attend_back.3.refs_3_.grad, bf16[1280,384]{1,0:T(8,128)(2,1)} %add_convert_fusion.4.refs_4_), custom_call_target="tpu_custom_call" | custom-call | flops 10066329600 | bytes 15728640 | tf_op jit(solution)/shard_map/products/pallas_call | solution.py:317
  530.2 5.2 spread_terms.2
  540.1 5.2 spread_terms.3
  555.3 20.0 %collective-permute-done.53 = bf16[384,1280]{1,0:T(8,128)(2,1)} collective-permute-done((bf16[384,1280]{1,0:T(8,128)(2,1)}, bf16[384,1280]{1,0:T(8,128)(2,1)}, u32[]{:S(2)}, u32[]{:S(2)}) %collective-permute-start.53) | collective-permute-done | bytes 983072 | tf_op jit(solution)/shard_map/ppermute | solution.py:42
  578.2 3.5 fusion.30
  581.7 14.0 %collective-permute-done.56 = bf16[384,1280]{1,0:T(8,128)(2,1)S(1)} collective-permute-done((bf16[384,1280]{1,0:T(8,128)(2,1)S(1)}, bf16[384,1280]{1,0:T(8,128)(2,1)S(1)}, u32[]{:S(2)}, u32[]{:S(2)}) %collective-permute-start.56) | collective-permute-done | bytes 983072 | tf_op jit(solution)/shard_map/ppermute | solution.py:42
  605.1 3.2 collective-permute-done.57
  618.8 8.8 %collective-permute-done.61 = f32[1922]{0:T(1024)S(1)} collective-permute-done((f32[1922]{0:T(1024)S(1)}, f32[1922]{0:T(1024)S(1)}, u32[]{:S(2)}, u32[]{:S(2)}) %collective-permute-start.61) | collective-permute-done | bytes 7720 | tf_op jit(solution)/shard_map/ppermute | solution.py:42
  631.6 6.5 collective-permute-done.63.refs_2_
  641.3 3.7 assemble.5
  645.0 3.5 assemble.4
  648.5 3.7 pad_maximum_fusion
  (571 shorter events, 213.3 us)
Async XLA Ops:
  7.2 67.9 %all-gather.3.cloned.1.call-start = ((), (), s32[]{:S(2)}) async-start(), calls=%async_computation.2 | async-start | bytes 3686400 | tf_op jit(solution)/shard_map/all_gather | solution.py:497
  9.8 168.2 %all-gather.5.cloned.1.call-start = ((), (), s32[]{:S(2)}) async-start(), calls=%async_computation.3 | async-start | bytes 7372800 | tf_op jit(solution)/shard_map/all_gather | solution.py:502
  12.4 13.5 %collective-permute-start = (bf16[384,1280]{1,0:T(8,128)(2,1)}, bf16[384,1280]{1,0:T(8,128)(2,1)}, u32[]{:S(2)}, u32[]{:S(2)}) collective-permute-start(bf16[384,1280]{1,0:T(8,128)(2,1)} %get-tuple-element.264.refs_0_), channel_id=1, source_target_pairs={{0,1},{1,0},{2,3},{3,2},{4,5},{5,4},{6,7},{7,6},{8,9},{9,8},{10,11... | collective-permute-start | bytes 2949128 | tf_op jit(solution)/shard_map/ppermute | solution.py:42
  12.9 25.4 %collective-permute-start.1 = (bf16[384,1280]{1,0:T(8,128)(2,1)}, bf16[384,1280]{1,0:T(8,128)(2,1)}, u32[]{:S(2)}, u32[]{:S(2)}) collective-permute-start(bf16[384,1280]{1,0:T(8,128)(2,1)} %get-tuple-element.264.refs_0_), channel_id=1, source_target_pairs={{0,2},{1,3},{2,0},{3,1},{4,6},{5,7},{6,4},{7,5},{8,10},{9,11},{10,... | collective-permute-start | bytes 2949128 | tf_op jit(solution)/shard_map/ppermute | solution.py:42
  19.7 492.5 %reduce-scatter.3.cloned.1.call-start = ((), (), s32[]{:S(2)}) async-start(), calls=%async_computation.4 | async-start | bytes 7372800 | tf_op jit(solution)/shard_map/reduce_scatter | solution.py:562
  23.7 14.6 %collective-permute-start.4 = (bf16[2,1920]{1,0:T(2,128)(2,1)S(1)}, bf16[2,1920]{1,0:T(2,128)(2,1)S(1)}, u32[]{:S(2)}, u32[]{:S(2)}) collective-permute-start(bf16[2,1920]{1,0:T(2,128)(2,1)S(1)} %pad_maximum_fusion.6), channel_id=1, source_target_pairs={{0,8},{4,12},{8,0},{12,4},{16,24},{20,28},{24,16},{28,20},{1,9},{5... | collective-permute-start | bytes 23048 | tf_op jit(solution)/shard_map/ppermute | solution.py:42
  25.9 33.3 %collective-permute-start.7 = (bf16[384,1280]{1,0:T(8,128)(2,1)S(1)}, bf16[384,1280]{1,0:T(8,128)(2,1)}, u32[]{:S(2)}, u32[]{:S(2)}) collective-permute-start(bf16[384,1280]{1,0:T(8,128)(2,1)S(1)} %get-tuple-element.121.refs_0_), channel_id=1, source_target_pairs={{0,2},{1,3},{2,0},{3,1},{4,6},{5,7},{6,4},{7,5},{8,10},{9,11},{10,... | collective-permute-start | bytes 2949128 | tf_op jit(solution)/shard_map/ppermute | solution.py:42
  44.9 17.3 %collective-permute-start.6 = (bf16[384,1280]{1,0:T(8,128)(2,1)S(1)}, bf16[384,1280]{1,0:T(8,128)(2,1)}, u32[]{:S(2)}, u32[]{:S(2)}) collective-permute-start(bf16[384,1280]{1,0:T(8,128)(2,1)S(1)} %get-tuple-element.121.refs_0_), channel_id=1, source_target_pairs={{0,1},{1,0},{2,3},{3,2},{4,5},{5,4},{6,7},{7,6},{8,9},{9,8},{10,11... | collective-permute-start | bytes 2949128 | tf_op jit(solution)/shard_map/ppermute | solution.py:42
  78.1 32.5 %collective-permute-start.13 = (bf16[1280,320]{0,1:T(8,128)(2,1)}, bf16[1280,320]{0,1:T(8,128)(2,1)S(1)}, u32[]{:S(2)}, u32[]{:S(2)}) collective-permute-start(bf16[1280,320]{0,1:T(8,128)(2,1)} %copy.37), channel_id=1, source_target_pairs={{0,2},{1,3},{2,0},{3,1},{4,6},{5,7},{6,4},{7,5},{8,10},{9,11},{10,... | collective-permute-start | bytes 2457608 | tf_op jit(solution)/shard_map/ppermute | solution.py:42
  79.6 54.8 %collective-permute-start.12 = (bf16[1280,320]{0,1:T(8,128)(2,1)}, bf16[1280,320]{0,1:T(8,128)(2,1)}, u32[]{:S(2)}, u32[]{:S(2)}) collective-permute-start(bf16[1280,320]{0,1:T(8,128)(2,1)} %copy.37), channel_id=1, source_target_pairs={{0,1},{1,0},{2,3},{3,2},{4,5},{5,4},{6,7},{7,6},{8,9},{9,8},{10,11... | collective-permute-start | bytes 2457608 | tf_op jit(solution)/shard_map/ppermute | solution.py:42
  103.9 24.9 %collective-permute-start.10 = (bf16[384,320]{1,0:T(8,128)(2,1)S(1)}, bf16[384,320]{1,0:T(8,128)(2,1)S(1)}, u32[]{:S(2)}, u32[]{:S(2)}) collective-permute-start(bf16[384,320]{1,0:T(8,128)(2,1)S(1)} %get-tuple-element.281), channel_id=1, source_target_pairs={{0,2},{1,3},{2,0},{3,1},{4,6},{5,7},{6,4},{7,5},{8,10},{9,11},{10,... | collective-permute-start | bytes 737288 | tf_op jit(solution)/shard_map/ppermute | solution.py:42
  104.5 24.6 %collective-permute-start.11 = (bf16[384,320]{1,0:T(8,128)(2,1)S(1)}, bf16[384,320]{1,0:T(8,128)(2,1)S(1)}, u32[]{:S(2)}, u32[]{:S(2)}) collective-permute-start(bf16[384,320]{1,0:T(8,128)(2,1)S(1)} %get-tuple-element.280), channel_id=1, source_target_pairs={{0,3},{1,2},{2,1},{3,0},{4,7},{5,6},{6,5},{7,4},{8,11},{9,10},{10,... | collective-permute-start | bytes 737288 | tf_op jit(solution)/shard_map/ppermute | solution.py:42
  105.8 23.8 %collective-permute-start.9 = (bf16[384,320]{1,0:T(8,128)(2,1)S(1)}, bf16[384,320]{1,0:T(8,128)(2,1)S(1)}, u32[]{:S(2)}, u32[]{:S(2)}) collective-permute-start(bf16[384,320]{1,0:T(8,128)(2,1)S(1)} %get-tuple-element.282), channel_id=1, source_target_pairs={{0,1},{1,0},{2,3},{3,2},{4,5},{5,4},{6,7},{7,6},{8,9},{9,8},{10,11... | collective-permute-start | bytes 737288 | tf_op jit(solution)/shard_map/ppermute | solution.py:42
  110.6 26.0 %collective-permute-start.14 = (bf16[1280,320]{0,1:T(8,128)(2,1)S(1)}, bf16[1280,320]{0,1:T(8,128)(2,1)}, u32[]{:S(2)}, u32[]{:S(2)}) collective-permute-start(bf16[1280,320]{0,1:T(8,128)(2,1)S(1)} %collective-permute-done.13), channel_id=1, source_target_pairs={{0,1},{1,0},{2,3},{3,2},{4,5},{5,4},{6,7},{7,6},{8,9},{9,8},{10,11... | collective-permute-start | bytes 2457608 | tf_op jit(solution)/shard_map/ppermute | solution.py:42
  128.8 21.3 %collective-permute-start.17 = (bf16[384,320]{1,0:T(8,128)(2,1)}, bf16[384,320]{1,0:T(8,128)(2,1)}, u32[]{:S(2)}, u32[]{:S(2)}) collective-permute-start(bf16[384,320]{1,0:T(8,128)(2,1)} %get-tuple-element.278), channel_id=1, source_target_pairs={{0,1},{1,0},{2,3},{3,2},{4,5},{5,4},{6,7},{7,6},{8,9},{9,8},{10,11... | collective-permute-start | bytes 737288 | tf_op jit(solution)/shard_map/ppermute | solution.py:42
  129.1 21.0 %collective-permute-start.18 = (bf16[384,320]{1,0:T(8,128)(2,1)}, bf16[384,320]{1,0:T(8,128)(2,1)}, u32[]{:S(2)}, u32[]{:S(2)}) collective-permute-start(bf16[384,320]{1,0:T(8,128)(2,1)} %get-tuple-element.277), channel_id=1, source_target_pairs={{0,2},{1,3},{2,0},{3,1},{4,6},{5,7},{6,4},{7,5},{8,10},{9,11},{10,... | collective-permute-start | bytes 737288 | tf_op jit(solution)/shard_map/ppermute | solution.py:42
  129.6 20.4 %collective-permute-start.19 = (bf16[384,320]{1,0:T(8,128)(2,1)}, bf16[384,320]{1,0:T(8,128)(2,1)}, u32[]{:S(2)}, u32[]{:S(2)}) collective-permute-start(bf16[384,320]{1,0:T(8,128)(2,1)} %get-tuple-element.276), channel_id=1, source_target_pairs={{0,3},{1,2},{2,1},{3,0},{4,7},{5,6},{6,5},{7,4},{8,11},{9,10},{10,... | collective-permute-start | bytes 737288 | tf_op jit(solution)/shard_map/ppermute | solution.py:42
  148.9 24.6 %collective-permute-start.16 = (bf16[384,1280]{1,0:T(8,128)(2,1)}, bf16[384,1280]{1,0:T(8,128)(2,1)}, u32[]{:S(2)}, u32[]{:S(2)}) collective-permute-start(bf16[384,1280]{1,0:T(8,128)(2,1)} %add_convert_fusion.11.refs_0_), channel_id=1, source_target_pairs={{0,2},{1,3},{2,0},{3,1},{4,6},{5,7},{6,4},{7,5},{8,10},{9,11},{10,... | collective-permute-start | bytes 2949128 | tf_op jit(solution)/shard_map/ppermute | solution.py:42
  185.8 23.8 %collective-permute-start.25 = (bf16[384,1280]{1,0:T(8,128)(2,1)S(1)}, bf16[384,1280]{1,0:T(8,128)(2,1)}, u32[]{:S(2)}, u32[]{:S(2)}) collective-permute-start(bf16[384,1280]{1,0:T(8,128)(2,1)S(1)} %add_convert_fusion.10.refs_4_), channel_id=1, source_target_pairs={{0,2},{1,3},{2,0},{3,1},{4,6},{5,7},{6,4},{7,5},{8,10},{9,11},{10,... | collective-permute-start | bytes 2949128 | tf_op jit(solution)/shard_map/ppermute | solution.py:42
  224.2 17.7 %collective-permute-start.22 = (bf16[384,1280]{1,0:T(8,128)(2,1)}, bf16[384,1280]{1,0:T(8,128)(2,1)S(1)}, u32[]{:S(2)}, u32[]{:S(2)}) collective-permute-start(bf16[384,1280]{1,0:T(8,128)(2,1)} %convolution_convert_fusion.15), channel_id=1, source_target_pairs={{0,1},{1,0},{2,3},{3,2},{4,5},{5,4},{6,7},{7,6},{8,9},{9,8},{10,11... | collective-permute-start | bytes 2949128 | tf_op jit(solution)/shard_map/ppermute | solution.py:42
  224.4 24.6 %collective-permute-start.23 = (bf16[384,1280]{1,0:T(8,128)(2,1)S(1)}, bf16[384,1280]{1,0:T(8,128)(2,1)S(1)}, u32[]{:S(2)}, u32[]{:S(2)}) collective-permute-start(bf16[384,1280]{1,0:T(8,128)(2,1)S(1)} %add_convert_fusion.9), channel_id=1, source_target_pairs={{0,2},{1,3},{2,0},{3,1},{4,6},{5,7},{6,4},{7,5},{8,10},{9,11},{10,... | collective-permute-start | bytes 2949128 | tf_op jit(solution)/shard_map/ppermute | solution.py:42
  238.2 13.7 %collective-permute-start.28 = (bf16[384,1280]{1,0:T(8,128)(2,1)S(1)}, bf16[384,1280]{1,0:T(8,128)(2,1)S(1)}, u32[]{:S(2)}, u32[]{:S(2)}) collective-permute-start(bf16[384,1280]{1,0:T(8,128)(2,1)S(1)} %convolution_convert_fusion.11), channel_id=1, source_target_pairs={{0,1},{1,0},{2,3},{3,2},{4,5},{5,4},{6,7},{7,6},{8,9},{9,8},{10,11... | collective-permute-start | bytes 2949128 | tf_op jit(solution)/shard_map/ppermute | solution.py:42
  238.3 31.7 %collective-permute-start.29 = (bf16[384,1280]{1,0:T(8,128)(2,1)S(1)}, bf16[384,1280]{1,0:T(8,128)(2,1)S(1)}, u32[]{:S(2)}, u32[]{:S(2)}) collective-permute-start(bf16[384,1280]{1,0:T(8,128)(2,1)S(1)} %add_convert_fusion.8), channel_id=1, source_target_pairs={{0,2},{1,3},{2,0},{3,1},{4,6},{5,7},{6,4},{7,5},{8,10},{9,11},{10,... | collective-permute-start | bytes 2949128 | tf_op jit(solution)/shard_map/ppermute | solution.py:42
  250.4 26.8 %collective-permute-start.30 = (bf16[384,1280]{1,0:T(8,128)(2,1)S(1)}, bf16[384,1280]{1,0:T(8,128)(2,1)S(1)}, u32[]{:S(2)}, u32[]{:S(2)}) collective-permute-start(bf16[384,1280]{1,0:T(8,128)(2,1)S(1)} %get-tuple-element.155.refs_8_), channel_id=1, source_target_pairs={{0,1},{1,0},{2,3},{3,2},{4,5},{5,4},{6,7},{7,6},{8,9},{9,8},{10,11... | collective-permute-start | bytes 2949128 | tf_op jit(solution)/shard_map/ppermute | solution.py:42
  250.4 40.1 %collective-permute-start.31 = (bf16[384,1280]{1,0:T(8,128)(2,1)S(1)}, bf16[384,1280]{1,0:T(8,128)(2,1)S(1)}, u32[]{:S(2)}, u32[]{:S(2)}) collective-permute-start(bf16[384,1280]{1,0:T(8,128)(2,1)S(1)} %get-tuple-element.155.refs_8_), channel_id=1, source_target_pairs={{0,2},{1,3},{2,0},{3,1},{4,6},{5,7},{6,4},{7,5},{8,10},{9,11},{10,... | collective-permute-start | bytes 2949128 | tf_op jit(solution)/shard_map/ppermute | solution.py:42
  298.2 11.8 %collective-permute-start.36 = (bf16[384,1280]{1,0:T(8,128)(2,1)S(1)}, bf16[384,1280]{1,0:T(8,128)(2,1)S(1)}, u32[]{:S(2)}, u32[]{:S(2)}) collective-permute-start(bf16[384,1280]{1,0:T(8,128)(2,1)S(1)} %get-tuple-element.164.refs_12_), channel_id=1, source_target_pairs={{0,1},{1,0},{2,3},{3,2},{4,5},{5,4},{6,7},{7,6},{8,9},{9,8},{10,11... | collective-permute-start | bytes 2949128 | tf_op jit(solution)/shard_map/ppermute | solution.py:42
  298.3 24.1 %collective-permute-start.37 = (bf16[384,1280]{1,0:T(8,128)(2,1)S(1)}, bf16[384,1280]{1,0:T(8,128)(2,1)S(1)}, u32[]{:S(2)}, u32[]{:S(2)}) collective-permute-start(bf16[384,1280]{1,0:T(8,128)(2,1)S(1)} %get-tuple-element.164.refs_12_), channel_id=1, source_target_pairs={{0,2},{1,3},{2,0},{3,1},{4,6},{5,7},{6,4},{7,5},{8,10},{9,11},{10,... | collective-permute-start | bytes 2949128 | tf_op jit(solution)/shard_map/ppermute | solution.py:42
  329.9 29.8 %collective-permute-start.34 = (bf16[384,1280]{1,0:T(8,128)(2,1)}, bf16[384,1280]{1,0:T(8,128)(2,1)}, u32[]{:S(2)}, u32[]{:S(2)}) collective-permute-start(bf16[384,1280]{1,0:T(8,128)(2,1)} %convolution_convert_fusion.7), channel_id=1, source_target_pairs={{0,1},{1,0},{2,3},{3,2},{4,5},{5,4},{6,7},{7,6},{8,9},{9,8},{10,11... | collective-permute-start | bytes 2949128 | tf_op jit(solution)/shard_map/ppermute | solution.py:42
  329.9 29.8 %collective-permute-start.35 = (bf16[384,1280]{1,0:T(8,128)(2,1)}, bf16[384,1280]{1,0:T(8,128)(2,1)}, u32[]{:S(2)}, u32[]{:S(2)}) collective-permute-start(bf16[384,1280]{1,0:T(8,128)(2,1)} %add_convert_fusion.7), channel_id=1, source_target_pairs={{0,2},{1,3},{2,0},{3,1},{4,6},{5,7},{6,4},{7,5},{8,10},{9,11},{10,... | collective-permute-start | bytes 2949128 | tf_op jit(solution)/shard_map/ppermute | solution.py:42
  336.5 55.9 %collective-permute-start.43 = (bf16[384,1280]{1,0:T(8,128)(2,1)}, bf16[384,1280]{1,0:T(8,128)(2,1)S(1)}, u32[]{:S(2)}, u32[]{:S(2)}) collective-permute-start(bf16[384,1280]{1,0:T(8,128)(2,1)} %convolution_convert_fusion.3), channel_id=1, source_target_pairs={{0,1},{1,0},{2,3},{3,2},{4,5},{5,4},{6,7},{7,6},{8,9},{9,8},{10,11... | collective-permute-start | bytes 2949128 | tf_op jit(solution)/shard_map/ppermute | solution.py:42
  336.7 55.8 %collective-permute-start.44 = (bf16[384,1280]{1,0:T(8,128)(2,1)}, bf16[384,1280]{1,0:T(8,128)(2,1)}, u32[]{:S(2)}, u32[]{:S(2)}) collective-permute-start(bf16[384,1280]{1,0:T(8,128)(2,1)} %add_convert_fusion.6), channel_id=1, source_target_pairs={{0,2},{1,3},{2,0},{3,1},{4,6},{5,7},{6,4},{7,5},{8,10},{9,11},{10,... | collective-permute-start | bytes 2949128 | tf_op jit(solution)/shard_map/ppermute | solution.py:42
  370.6 31.8 %collective-permute-start.40 = (bf16[384,320]{1,0:T(8,128)(2,1)}, bf16[384,320]{1,0:T(8,128)(2,1)}, u32[]{:S(2)}, u32[]{:S(2)}) collective-permute-start(bf16[384,320]{1,0:T(8,128)(2,1)} %get-tuple-element.291), channel_id=1, source_target_pairs={{0,1},{1,0},{2,3},{3,2},{4,5},{5,4},{6,7},{7,6},{8,9},{9,8},{10,11... | collective-permute-start | bytes 737288 | tf_op jit(solution)/shard_map/ppermute | solution.py:42
  370.6 31.8 %collective-permute-start.41 = (bf16[384,320]{1,0:T(8,128)(2,1)}, bf16[384,320]{1,0:T(8,128)(2,1)}, u32[]{:S(2)}, u32[]{:S(2)}) collective-permute-start(bf16[384,320]{1,0:T(8,128)(2,1)} %get-tuple-element.290), channel_id=1, source_target_pairs={{0,2},{1,3},{2,0},{3,1},{4,6},{5,7},{6,4},{7,5},{8,10},{9,11},{10,... | collective-permute-start | bytes 737288 | tf_op jit(solution)/shard_map/ppermute | solution.py:42
  371.8 30.5 %collective-permute-start.42 = (bf16[384,320]{1,0:T(8,128)(2,1)}, bf16[384,320]{1,0:T(8,128)(2,1)}, u32[]{:S(2)}, u32[]{:S(2)}) collective-permute-start(bf16[384,320]{1,0:T(8,128)(2,1)} %get-tuple-element.289), channel_id=1, source_target_pairs={{0,3},{1,2},{2,1},{3,0},{4,7},{5,6},{6,5},{7,4},{8,11},{9,10},{10,... | collective-permute-start | bytes 737288 | tf_op jit(solution)/shard_map/ppermute | solution.py:42
  392.4 235.3 %reduce-scatter.5.cloned.1.call-start = ((), (), s32[]{:S(2)}) async-start(), calls=%async_computation.5 | async-start | bytes 3686400 | tf_op jit(solution)/shard_map/reduce_scatter | solution.py:562
  418.9 42.0 %collective-permute-start.45 = (bf16[384,320]{1,0:T(8,128)(2,1)S(1)}, bf16[384,320]{1,0:T(8,128)(2,1)}, u32[]{:S(2)}, u32[]{:S(2)}) collective-permute-start(bf16[384,320]{1,0:T(8,128)(2,1)S(1)} %copy-done.66), channel_id=1, source_target_pairs={{0,1},{1,0},{2,3},{3,2},{4,5},{5,4},{6,7},{7,6},{8,9},{9,8},{10,11... | collective-permute-start | bytes 737288 | tf_op jit(solution)/shard_map/ppermute | solution.py:42
  419.1 41.7 %collective-permute-start.46 = (bf16[384,320]{1,0:T(8,128)(2,1)S(1)}, bf16[384,320]{1,0:T(8,128)(2,1)}, u32[]{:S(2)}, u32[]{:S(2)}) collective-permute-start(bf16[384,320]{1,0:T(8,128)(2,1)S(1)} %copy-done.65), channel_id=1, source_target_pairs={{0,2},{1,3},{2,0},{3,1},{4,6},{5,7},{6,4},{7,5},{8,10},{9,11},{10,... | collective-permute-start | bytes 737288 | tf_op jit(solution)/shard_map/ppermute | solution.py:42
  420.3 40.5 %collective-permute-start.47 = (bf16[384,320]{1,0:T(8,128)(2,1)S(1)}, bf16[384,320]{1,0:T(8,128)(2,1)}, u32[]{:S(2)}, u32[]{:S(2)}) collective-permute-start(bf16[384,320]{1,0:T(8,128)(2,1)S(1)} %get-tuple-element.284), channel_id=1, source_target_pairs={{0,3},{1,2},{2,1},{3,0},{4,7},{5,6},{6,5},{7,4},{8,11},{9,10},{10,... | collective-permute-start | bytes 737288 | tf_op jit(solution)/shard_map/ppermute | solution.py:42
  420.8 38.7 %collective-permute-start.48 = (bf16[1280,384]{1,0:T(8,128)(2,1)}, bf16[1280,384]{1,0:T(8,128)(2,1)S(1)}, u32[]{:S(2)}, u32[]{:S(2)}) collective-permute-start(bf16[1280,384]{1,0:T(8,128)(2,1)} %get-tuple-element.186), channel_id=1, source_target_pairs={{0,1},{1,0},{2,3},{3,2},{4,5},{5,4},{6,7},{7,6},{8,9},{9,8},{10,11... | collective-permute-start | bytes 2949128 | tf_op jit(solution)/shard_map/ppermute | solution.py:42
  425.2 34.4 %collective-permute-start.50 = (bf16[1280,384]{1,0:T(8,128)(2,1)S(1)}, bf16[1280,384]{1,0:T(8,128)(2,1)S(1)}, u32[]{:S(2)}, u32[]{:S(2)}) collective-permute-start(bf16[1280,384]{1,0:T(8,128)(2,1)S(1)} %add_convert_fusion.5), channel_id=1, source_target_pairs={{0,2},{1,3},{2,0},{3,1},{4,6},{5,7},{6,4},{7,5},{8,10},{9,11},{10,... | collective-permute-start | bytes 2949128 | tf_op jit(solution)/shard_map/ppermute | solution.py:42
  550.4 24.9 %collective-permute-start.53 = (bf16[384,1280]{1,0:T(8,128)(2,1)}, bf16[384,1280]{1,0:T(8,128)(2,1)}, u32[]{:S(2)}, u32[]{:S(2)}) collective-permute-start(bf16[384,1280]{1,0:T(8,128)(2,1)} %add_convert_fusion.3), channel_id=1, source_target_pairs={{0,2},{1,3},{2,0},{3,1},{4,6},{5,7},{6,4},{7,5},{8,10},{9,11},{10,... | collective-permute-start | bytes 2949128 | tf_op jit(solution)/shard_map/ppermute | solution.py:42
  553.0 28.6 %collective-permute-start.54 = (bf16[384,1280]{1,0:T(8,128)(2,1)S(1)}, bf16[384,1280]{1,0:T(8,128)(2,1)S(1)}, u32[]{:S(2)}, u32[]{:S(2)}) collective-permute-start(bf16[384,1280]{1,0:T(8,128)(2,1)S(1)} %copy-done.17), channel_id=1, source_target_pairs={{0,1},{1,0},{2,3},{3,2},{4,5},{5,4},{6,7},{7,6},{8,9},{9,8},{10,11... | collective-permute-start | bytes 2949128 | tf_op jit(solution)/shard_map/ppermute | solution.py:42
  554.7 40.9 %collective-permute-start.56 = (bf16[384,1280]{1,0:T(8,128)(2,1)S(1)}, bf16[384,1280]{1,0:T(8,128)(2,1)S(1)}, u32[]{:S(2)}, u32[]{:S(2)}) collective-permute-start(bf16[384,1280]{1,0:T(8,128)(2,1)S(1)} %add_convert_fusion.2), channel_id=1, source_target_pairs={{0,2},{1,3},{2,0},{3,1},{4,6},{5,7},{6,4},{7,5},{8,10},{9,11},{10,... | collective-permute-start | bytes 2949128 | tf_op jit(solution)/shard_map/ppermute | solution.py:42
  609.2 19.9 %collective-permute-start.69 = (bf16[160,1280]{1,0:T(8,128)(2,1)S(1)}, bf16[160,1280]{1,0:T(8,128)(2,1)}, u32[]{:S(2)}, u32[]{:S(2)}) collective-permute-start(bf16[160,1280]{1,0:T(8,128)(2,1)S(1)} %copy-done.50), channel_id=1, source_target_pairs={{0,2},{1,3},{2,0},{3,1},{4,6},{5,7},{6,4},{7,5},{8,10},{9,11},{10,... | collective-permute-start | bytes 1228808 | tf_op jit(solution)/shard_map/ppermute | solution.py:42
  610.7 18.9 %collective-permute-start.66 = (bf16[160,1280]{1,0:T(8,128)(2,1)S(1)}, bf16[160,1280]{1,0:T(8,128)(2,1)}, u32[]{:S(2)}, u32[]{:S(2)}) collective-permute-start(bf16[160,1280]{1,0:T(8,128)(2,1)S(1)} %get-tuple-element.214.refs_0_), channel_id=1, source_target_pairs={{0,2},{1,3},{2,0},{3,1},{4,6},{5,7},{6,4},{7,5},{8,10},{9,11},{10,... | collective-permute-start | bytes 1228808 | tf_op jit(solution)/shard_map/ppermute | solution.py:42
  618.8 12.3 %collective-permute-start.68 = (bf16[160,1280]{1,0:T(8,128)(2,1)S(1)}, bf16[160,1280]{1,0:T(8,128)(2,1)}, u32[]{:S(2)}, u32[]{:S(2)}) collective-permute-start(bf16[160,1280]{1,0:T(8,128)(2,1)S(1)} %copy-done.50), channel_id=1, source_target_pairs={{0,1},{1,0},{2,3},{3,2},{4,5},{5,4},{6,7},{7,6},{8,9},{9,8},{10,11... | collective-permute-start | bytes 1228808 | tf_op jit(solution)/shard_map/ppermute | solution.py:42
  631.1 21.1 %collective-permute-start.62 = (bf16[160,1280]{1,0:T(8,128)(2,1)S(1)}, bf16[160,1280]{1,0:T(8,128)(2,1)S(1)}, u32[]{:S(2)}, u32[]{:S(2)}) collective-permute-start(bf16[160,1280]{1,0:T(8,128)(2,1)S(1)} %copy-done.51), channel_id=1, source_target_pairs={{0,1},{1,0},{2,3},{3,2},{4,5},{5,4},{6,7},{7,6},{8,9},{9,8},{10,11... | collective-permute-start | bytes 1228808 | tf_op jit(solution)/shard_map/ppermute | solution.py:42
  638.1 14.2 %collective-permute-start.64 = (bf16[160,1280]{1,0:T(8,128)(2,1)}, bf16[160,1280]{1,0:T(8,128)(2,1)}, u32[]{:S(2)}, u32[]{:S(2)}) collective-permute-start(bf16[160,1280]{1,0:T(8,128)(2,1)} %collective-permute-done.63.refs_2_), channel_id=1, source_target_pairs={{0,1},{1,0},{2,3},{3,2},{4,5},{5,4},{6,7},{7,6},{8,9},{9,8},{10,11... | collective-permute-start | bytes 1228808 | tf_op jit(solution)/shard_map/ppermute | solution.py:42
  (158 other events, 1287.9 us)
Sparse Core Ops, SparseCore 0:
  10.8 64.3 all-gather.2
  77.3 100.5 all-gather.4
  392.5 119.6 reduce-scatter.2
  552.5 74.4 reduce-scatter.4

commit v5 on v4

--- a/solution.py
+++ b/solution.py
@@ -238,7 +238,7 @@
         ],
         compiler_params=pltpu.CompilerParams(vmem_limit_bytes=56 << 20),
         cost_estimate=pl.CostEstimate(
-            flops=20 * heads * seq * seq * 256, bytes_accessed=qkv.size * 5, transcendentals=heads * seq * seq
+            flops=16 * heads * seq * seq * 256, bytes_accessed=qkv.size * 5, transcendentals=heads * seq * seq
         ),
         name="attend_back",
     )(qkv, mask, grad, lse)
@@ -716,10 +716,9 @@
     step.mark(grad_wout)
     for c in others:
         attention_back(c)
-    step.also(grad_wup)
     total = products(ordered(full1), grad_qkvs, half, beside=grad_wout, width=span)
     step.mark(total)
-    total = owned(total)
+    total = owned(lax.optimization_barrier((total, grad_wup))[0])
     for c in every:
         hidden_back(c)
     for c in every:

time: 675 us -> 666 us (0.987)
  waiting for transfers between devices: 172 us -> 158 us
  matrix products: 106 us -> 113 us
    reduce_scatter x2, waiting for transfers between devices: 16.5 us -> 0.01 us  [owned(): return lax.psum_scatter(grad, 'fsdp', scatter_dimension=0, tiled=True)]
    dot_general x18, matrix products: 40.4 us -> 48.2 us  [dot_t(): lax.dot_general(a, b, (((1,), (1,)), ((), ())), preferred_element_type=si...]
    unnamed x262 -> x264, local copies, waits for them, and re-layouts: 16.6 us -> 17.4 us
  transfers between devices with their start and end apart: 75 -> 75, of which waited for: 23 -> 22; matrix products, arithmetic and copies ran while one was open for 26% -> 28% of each run, Pallas kernels for 28% -> 31%
where the time goes in v5:
time: 666 us; the launch traced here: 656 us
  Pallas kernels  209 us (31%)
  waiting for transfers between devices  158 us (24%)
  matrix products  113 us (17%)
  other arithmetic  60.5 us (9%)
  local copies, waits for them, and re-layouts  55.1 us (8%)
  starting transfers between devices  42.9 us (6%)
  between operations  17.6 us (3%)
    ppermute x71, waiting for transfers between devices, flip(): lax.ppermute(tensor, axis, [(i, i ^ bits) for i in range(lax.axis_size(ax...  151 us
    pallas_call x2, Pallas kernels, attend_back(): pl.pallas_call(functools.partial(attend_back_kernel, heads, dim, block, s...  65.7 us
    dot_general x20, matrix products, dot(): return jnp.dot(a, b, preferred_element_type=single)  65.3 us
    pallas_call x4, Pallas kernels, products(): pl.pallas_call(body, grid=(rows // tile,), in_specs=in_specs, out_specs=p...  61.6 us
    dot_general x18, matrix products, dot_t(): lax.dot_general(a, b, (((1,), (1,)), ((), ())), preferred_element_type=si...  48.2 us
    ppermute x71, starting transfers between devices, flip(): lax.ppermute(tensor, axis, [(i, i ^ bits) for i in range(lax.axis_size(ax...  42.7 us
    pallas_call x2, Pallas kernels, attend(): pl.pallas_call(functools.partial(attend_kernel, heads, dim, block, scale)...  33.5 us
    unnamed x264, local copies, waits for them, and re-layouts  17.4 us
  transfers between devices with their start and end apart: 75, of which 22 were waited for; matrix products, arithmetic and copies ran while one was open for 28% of the time, Pallas kernels for 31%

profile of v5, /device:TPU:0, one launch (start us, length us, event | category | flops | bytes accessed | tf_op | source)
XLA Modules:
  0.0 656.4 jit_solution(16747819618998984215)
XLA Ops:
  26.5 11.8 %collective-permute-done.1.refs_2_ = bf16[384,1280]{1,0:T(8,128)(2,1)} collective-permute-done((bf16[384,1280]{1,0:T(8,128)(2,1)}, bf16[384,1280]{1,0:T(8,128)(2,1)}, u32[]{:S(2)}, u32[]{:S(2)}) %collective-permute-start.1) | collective-permute-done | bytes 983072 | tf_op jit(solution)/shard_map/ppermute | solution.py:42
  45.9 7.5 %norm_blocks.2.refs_0_ = bf16[1536,1280]{1,0:T(8,128)(2,1)} custom-call(bf16[384,1280]{1,0:T(8,128)(2,1)} %get-tuple-element.266.refs_0_, bf16[384,1280]{1,0:T(8,128)(2,1)} %collective-permute-done.refs_1_, bf16[384,1280]{1,0:T(8,128)(2,1)} %collective-permute-done.1.refs_2_, bf16[384,1280]{1,0:T(8,128)(2,1)} %copy-done.54, f32[1,1280]{1,0:T(1,128)} %reshape.306.refs_4_, ...), custom_call_target="tpu_custom_call" | custom-call | flops 19660800 | bytes 7864320 | tf_op jit(solution)/shard_map/norm_blocks/pallas_call | solution.py:266
  53.4 5.8 collective-permute-done.7.refs_2_
  62.2 7.6 %norm_blocks.3.refs_1_ = bf16[1536,1280]{1,0:T(8,128)(2,1)} custom-call(bf16[384,1280]{1,0:T(8,128)(2,1)} %copy-done.44, bf16[384,1280]{1,0:T(8,128)(2,1)} %collective-permute-done.6.refs_1_, bf16[384,1280]{1,0:T(8,128)(2,1)} %collective-permute-done.7.refs_2_, bf16[384,1280]{1,0:T(8,128)(2,1)} %collective-permute-done.8.refs_3_, ...), custom_call_target="tpu_custom_call" | custom-call | flops 19660800 | bytes 7864320 | tf_op jit(solution)/shard_map/norm_blocks/pallas_call | solution.py:266
  69.8 5.4 all-gather.3.cloned.1.call-done
  79.6 7.2 %add_convert_fusion.1.qkv_ref = bf16[1536,960]{1,0:T(8,128)(2,1)S(1)} fusion(bf16[1536,1280]{1,0:T(8,128)(2,1)} %norm_blocks.2.refs_0_, f32[960]{0:T(1024)S(1)} %bitcast.110, bf16[1280,1280]{1,0:T(8,128)(2,1)} %all-gather.3.cloned.1.call-done), kind=kOutput, calls=%fused_computation.4 | convolution fusion | flops 3777822720 | bytes 9506560 | tf_op jit(solution)/shard_map/dot_general | solution.py:471
  86.8 16.9 %attend.2 = (bf16[1536,320]{1,0:T(8,128)(2,1)S(1)}, f32[1536,4]{1,0:T(8,128)S(1)}) custom-call(bf16[1536,960]{1,0:T(8,128)(2,1)S(1)} %add_convert_fusion.1.qkv_ref, bf16[1536,48]{1,0:T(8,128)(2,1)S(1)} %get-tuple-element.321.mask_ref), custom_call_target="tpu_custom_call" | custom-call | flops 9663676416 | bytes 4423680 | tf_op jit(solution)/shard_map/attend/pallas_call | solution.py:208
  106.1 4.5 add_convert_fusion.qkv_ref
  110.9 16.6 %attend.3 = (bf16[1536,320]{1,0:T(8,128)(2,1)S(1)}, f32[1536,4]{1,0:T(8,128)S(1)}) custom-call(bf16[1536,960]{1,0:T(8,128)(2,1)S(1)} %add_convert_fusion.qkv_ref, bf16[1536,48]{1,0:T(8,128)(2,1)S(1)} %get-tuple-element.320.mask_ref), custom_call_target="tpu_custom_call" | custom-call | flops 9663676416 | bytes 4423680 | tf_op jit(solution)/shard_map/attend/pallas_call | solution.py:208
  138.7 5.0 place_output_weight.1
  143.7 3.5 fusion.130
  152.4 3.8 fusion.131
  157.5 16.0 %collective-permute-done.16.refs_2_ = bf16[384,1280]{1,0:T(8,128)(2,1)} collective-permute-done((bf16[384,1280]{1,0:T(8,128)(2,1)}, bf16[384,1280]{1,0:T(8,128)(2,1)}, u32[]{:S(2)}, u32[]{:S(2)}) %collective-permute-start.16) | collective-permute-done | bytes 983072 | tf_op jit(solution)/shard_map/ppermute | solution.py:42
  178.0 4.9 multiply_convert_fusion.7
  187.3 4.2 multiply_convert_fusion.6
  198.6 4.2 multiply_convert_fusion.4
  204.2 5.4 collective-permute-done.25.refs_6_
  212.6 5.0 multiply_convert_fusion.3
  217.6 4.7 convolution_convert_fusion.13
  225.8 4.0 multiply_convert_fusion.2
  229.8 3.8 convolution_convert_fusion.12
  241.9 7.1 %collective-permute-done.23 = bf16[384,1280]{1,0:T(8,128)(2,1)S(1)} collective-permute-done((bf16[384,1280]{1,0:T(8,128)(2,1)S(1)}, bf16[384,1280]{1,0:T(8,128)(2,1)S(1)}, u32[]{:S(2)}, u32[]{:S(2)}) %collective-permute-start.23) | collective-permute-done | bytes 983072 | tf_op jit(solution)/shard_map/ppermute | solution.py:42
  252.0 18.1 %collective-permute-done.29 = bf16[384,1280]{1,0:T(8,128)(2,1)S(1)} collective-permute-done((bf16[384,1280]{1,0:T(8,128)(2,1)S(1)}, bf16[384,1280]{1,0:T(8,128)(2,1)S(1)}, u32[]{:S(2)}, u32[]{:S(2)}) %collective-permute-start.29) | collective-permute-done | bytes 983072 | tf_op jit(solution)/shard_map/ppermute | solution.py:42
  279.9 10.6 %collective-permute-done.31.refs_10_ = bf16[384,1280]{1,0:T(8,128)(2,1)S(1)} collective-permute-done((bf16[384,1280]{1,0:T(8,128)(2,1)S(1)}, bf16[384,1280]{1,0:T(8,128)(2,1)S(1)}, u32[]{:S(2)}, u32[]{:S(2)}) %collective-permute-start.31) | collective-permute-done | bytes 983072 | tf_op jit(solution)/shard_map/ppermute | solution.py:42
  307.4 3.5 convert_reduce_fusion.7
  310.9 3.5 convert_reduce_fusion.6
  314.4 8.0 %collective-permute-done.37.refs_14_ = bf16[384,1280]{1,0:T(8,128)(2,1)S(1)} collective-permute-done((bf16[384,1280]{1,0:T(8,128)(2,1)S(1)}, bf16[384,1280]{1,0:T(8,128)(2,1)S(1)}, u32[]{:S(2)}, u32[]{:S(2)}) %collective-permute-start.37) | collective-permute-done | bytes 983072 | tf_op jit(solution)/shard_map/ppermute | solution.py:42
  322.4 3.5 convert_reduce_fusion.5
  334.3 3.8 convolution_convert_fusion.4
  339.4 4.5 convolution_convert_fusion.3
  347.1 19.8 %products.4.refs_16_ = bf16[1280,2560]{1,0:T(8,128)(2,1)} custom-call(bf16[384,1280]{1,0:T(8,128)(2,1)} %copy-done.116, bf16[384,1280]{1,0:T(8,128)(2,1)} %copy-done.115, bf16[384,1280]{1,0:T(8,128)(2,1)} %copy-done.114, bf16[384,1280]{1,0:T(8,128)(2,1)} %copy-done.113, bf16[384,1280]{1,0:T(8,128)(2,1)} %copy-done.120, bf16[384,1280]{1,0:T(8,128)(2,1)} %copy-done.119, ...), custom_call_target="tpu_custom_call" | custom-call | flops 10066329600 | bytes 15728640 | tf_op jit(solution)/shard_map/products/pallas_call | solution.py:317
  370.1 4.6 convert_reduce_fusion.15
  379.2 19.9 %products.5 = bf16[1280,2560]{1,0:T(8,128)(2,1)} custom-call(bf16[384,1280]{1,0:T(8,128)(2,1)} %add_convert_fusion.11.refs_0_, bf16[384,1280]{1,0:T(8,128)(2,1)} %copy-done.98, bf16[384,1280]{1,0:T(8,128)(2,1)} %collective-permute-done.16.refs_2_, bf16[384,1280]{1,0:T(8,128)(2,1)} %copy-done.97, ...), custom_call_target="tpu_custom_call", output_to_operand_aliasing={{}: (16, {})} | custom-call | flops 10066329600 | bytes 15728640 | tf_op jit(solution)/shard_map/products/pallas_call | solution.py:317
  402.6 4.4 convert_reduce_fusion.14
  409.5 7.8 %products.6.full = bf16[1280,1280]{1,0:T(8,128)(2,1)} custom-call(bf16[384,1280]{1,0:T(8,128)(2,1)} %copy-done.50, bf16[384,1280]{1,0:T(8,128)(2,1)} %copy-done.51, bf16[384,1280]{1,0:T(8,128)(2,1)} %copy-done.55, bf16[384,1280]{1,0:T(8,128)(2,1)} %copy-done.57), custom_call_target="tpu_custom_call" | custom-call | flops 2516582400 | bytes 3932160 | tf_op jit(solution)/shard_map/products/pallas_call | solution.py:317
  417.3 4.7 split_output_weight.1
  432.3 33.2 %attend_back.2.refs_2_.grad = bf16[1536,960]{1,0:T(8,128)(2,1)} custom-call(bf16[1536,960]{1,0:T(8,128)(2,1)} %copy-done.17, bf16[1536,48]{1,0:T(8,128)(2,1)} %copy-done.15, bf16[1536,320]{1,0:T(8,128)(2,1)} %pad_maximum_fusion.2.grad_ref, f32[1536,4]{1,0:T(8,128)} %copy-done.19), custom_call_target="tpu_custom_call" | custom-call | flops 38654705664 | bytes 7372800 | tf_op jit(solution)/shard_map/attend_back/pallas_call | solution.py:229
  469.1 32.5 %attend_back.3.refs_3_.grad = bf16[1536,960]{1,0:T(8,128)(2,1)} custom-call(bf16[1536,960]{1,0:T(8,128)(2,1)} %copy-done.16, bf16[1536,48]{1,0:T(8,128)(2,1)} %copy-done.14, bf16[1536,320]{1,0:T(8,128)(2,1)} %pad_maximum_fusion.3.grad_ref, f32[1536,4]{1,0:T(8,128)} %copy-done.18), custom_call_target="tpu_custom_call" | custom-call | flops 38654705664 | bytes 7372800 | tf_op jit(solution)/shard_map/attend_back/pallas_call | solution.py:229
  501.7 14.2 %products.7 = bf16[1280,1280]{1,0:T(8,128)(2,1)} custom-call(bf16[1536,1280]{1,0:T(8,128)(2,1)} %norm_blocks.2.refs_0_, bf16[1536,1280]{1,0:T(8,128)(2,1)} %norm_blocks.3.refs_1_, bf16[1536,960]{1,0:T(8,128)(2,1)} %attend_back.2.refs_2_.grad, bf16[1536,960]{1,0:T(8,128)(2,1)} %attend_back.3.refs_3_.grad, bf16[1280,384]{1,0:T(8,128)(2,1)} %add_convert_fusion.4.refs_4_), custom_call_target="tpu_custom_call" | custom-call | flops 10066329600 | bytes 15728640 | tf_op jit(solution)/shard_map/products/pallas_call | solution.py:317
  517.9 5.2 spread_terms.2
  527.8 5.2 spread_terms.3
  544.3 18.0 %collective-permute-done.53 = bf16[384,1280]{1,0:T(8,128)(2,1)S(1)} collective-permute-done((bf16[384,1280]{1,0:T(8,128)(2,1)}, bf16[384,1280]{1,0:T(8,128)(2,1)S(1)}, u32[]{:S(2)}, u32[]{:S(2)}) %collective-permute-start.53) | collective-permute-done | bytes 983072 | tf_op jit(solution)/shard_map/ppermute | solution.py:42
  566.6 15.9 %collective-permute-done.56 = bf16[384,1280]{1,0:T(8,128)(2,1)S(1)} collective-permute-done((bf16[384,1280]{1,0:T(8,128)(2,1)S(1)}, bf16[384,1280]{1,0:T(8,128)(2,1)S(1)}, u32[]{:S(2)}, u32[]{:S(2)}) %collective-permute-start.56) | collective-permute-done | bytes 983072 | tf_op jit(solution)/shard_map/ppermute | solution.py:42
  585.3 3.5 fusion.24
  607.6 8.7 %collective-permute-done.61 = f32[1922]{0:T(1024)S(1)} collective-permute-done((f32[1922]{0:T(1024)S(1)}, f32[1922]{0:T(1024)S(1)}, u32[]{:S(2)}, u32[]{:S(2)}) %collective-permute-start.61) | collective-permute-done | bytes 7720 | tf_op jit(solution)/shard_map/ppermute | solution.py:42
  620.6 8.0 %collective-permute-done.63.refs_2_ = bf16[160,1280]{1,0:T(8,128)(2,1)} collective-permute-done((bf16[160,1280]{1,0:T(8,128)(2,1)}, bf16[160,1280]{1,0:T(8,128)(2,1)}, u32[]{:S(2)}, u32[]{:S(2)}) %collective-permute-start.63) | collective-permute-done | bytes 409632 | tf_op jit(solution)/shard_map/ppermute | solution.py:42
  631.8 3.7 assemble.5
  638.8 3.7 pad_maximum_fusion
  (574 shorter events, 215.4 us)
Async XLA Ops:
  7.2 67.9 %all-gather.3.cloned.1.call-start = ((), (), s32[]{:S(2)}) async-start(), calls=%async_computation.2 | async-start | bytes 3686400 | tf_op jit(solution)/shard_map/all_gather | solution.py:497
  9.8 168.2 %all-gather.5.cloned.1.call-start = ((), (), s32[]{:S(2)}) async-start(), calls=%async_computation.3 | async-start | bytes 7372800 | tf_op jit(solution)/shard_map/all_gather | solution.py:502
  12.4 13.5 %collective-permute-start = (bf16[384,1280]{1,0:T(8,128)(2,1)}, bf16[384,1280]{1,0:T(8,128)(2,1)}, u32[]{:S(2)}, u32[]{:S(2)}) collective-permute-start(bf16[384,1280]{1,0:T(8,128)(2,1)} %get-tuple-element.266.refs_0_), channel_id=1, source_target_pairs={{0,1},{1,0},{2,3},{3,2},{4,5},{5,4},{6,7},{7,6},{8,9},{9,8},{10,11... | collective-permute-start | bytes 2949128 | tf_op jit(solution)/shard_map/ppermute | solution.py:42
  12.9 25.4 %collective-permute-start.1 = (bf16[384,1280]{1,0:T(8,128)(2,1)}, bf16[384,1280]{1,0:T(8,128)(2,1)}, u32[]{:S(2)}, u32[]{:S(2)}) collective-permute-start(bf16[384,1280]{1,0:T(8,128)(2,1)} %get-tuple-element.266.refs_0_), channel_id=1, source_target_pairs={{0,2},{1,3},{2,0},{3,1},{4,6},{5,7},{6,4},{7,5},{8,10},{9,11},{10,... | collective-permute-start | bytes 2949128 | tf_op jit(solution)/shard_map/ppermute | solution.py:42
  19.7 518.2 %reduce-scatter.3.cloned.1.call-start = ((), (), s32[]{:S(2)}) async-start(), calls=%async_computation.4 | async-start | bytes 7372800 | tf_op jit(solution)/shard_map/reduce_scatter | solution.py:562
  23.7 14.6 %collective-permute-start.4 = (bf16[2,1920]{1,0:T(2,128)(2,1)S(1)}, bf16[2,1920]{1,0:T(2,128)(2,1)S(1)}, u32[]{:S(2)}, u32[]{:S(2)}) collective-permute-start(bf16[2,1920]{1,0:T(2,128)(2,1)S(1)} %pad_maximum_fusion.6), channel_id=1, source_target_pairs={{0,8},{4,12},{8,0},{12,4},{16,24},{20,28},{24,16},{28,20},{1,9},{5... | collective-permute-start | bytes 23048 | tf_op jit(solution)/shard_map/ppermute | solution.py:42
  25.9 33.2 %collective-permute-start.7 = (bf16[384,1280]{1,0:T(8,128)(2,1)S(1)}, bf16[384,1280]{1,0:T(8,128)(2,1)}, u32[]{:S(2)}, u32[]{:S(2)}) collective-permute-start(bf16[384,1280]{1,0:T(8,128)(2,1)S(1)} %get-tuple-element.122.refs_0_), channel_id=1, source_target_pairs={{0,2},{1,3},{2,0},{3,1},{4,6},{5,7},{6,4},{7,5},{8,10},{9,11},{10,... | collective-permute-start | bytes 2949128 | tf_op jit(solution)/shard_map/ppermute | solution.py:42
  44.9 17.3 %collective-permute-start.6 = (bf16[384,1280]{1,0:T(8,128)(2,1)S(1)}, bf16[384,1280]{1,0:T(8,128)(2,1)}, u32[]{:S(2)}, u32[]{:S(2)}) collective-permute-start(bf16[384,1280]{1,0:T(8,128)(2,1)S(1)} %get-tuple-element.122.refs_0_), channel_id=1, source_target_pairs={{0,1},{1,0},{2,3},{3,2},{4,5},{5,4},{6,7},{7,6},{8,9},{9,8},{10,11... | collective-permute-start | bytes 2949128 | tf_op jit(solution)/shard_map/ppermute | solution.py:42
  78.1 32.5 %collective-permute-start.13 = (bf16[1280,320]{0,1:T(8,128)(2,1)}, bf16[1280,320]{0,1:T(8,128)(2,1)S(1)}, u32[]{:S(2)}, u32[]{:S(2)}) collective-permute-start(bf16[1280,320]{0,1:T(8,128)(2,1)} %copy.37), channel_id=1, source_target_pairs={{0,2},{1,3},{2,0},{3,1},{4,6},{5,7},{6,4},{7,5},{8,10},{9,11},{10,... | collective-permute-start | bytes 2457608 | tf_op jit(solution)/shard_map/ppermute | solution.py:42
  79.6 54.8 %collective-permute-start.12 = (bf16[1280,320]{0,1:T(8,128)(2,1)}, bf16[1280,320]{0,1:T(8,128)(2,1)}, u32[]{:S(2)}, u32[]{:S(2)}) collective-permute-start(bf16[1280,320]{0,1:T(8,128)(2,1)} %copy.37), channel_id=1, source_target_pairs={{0,1},{1,0},{2,3},{3,2},{4,5},{5,4},{6,7},{7,6},{8,9},{9,8},{10,11... | collective-permute-start | bytes 2457608 | tf_op jit(solution)/shard_map/ppermute | solution.py:42
  103.9 24.9 %collective-permute-start.10 = (bf16[384,320]{1,0:T(8,128)(2,1)S(1)}, bf16[384,320]{1,0:T(8,128)(2,1)S(1)}, u32[]{:S(2)}, u32[]{:S(2)}) collective-permute-start(bf16[384,320]{1,0:T(8,128)(2,1)S(1)} %get-tuple-element.283), channel_id=1, source_target_pairs={{0,2},{1,3},{2,0},{3,1},{4,6},{5,7},{6,4},{7,5},{8,10},{9,11},{10,... | collective-permute-start | bytes 737288 | tf_op jit(solution)/shard_map/ppermute | solution.py:42
  104.5 24.5 %collective-permute-start.11 = (bf16[384,320]{1,0:T(8,128)(2,1)S(1)}, bf16[384,320]{1,0:T(8,128)(2,1)S(1)}, u32[]{:S(2)}, u32[]{:S(2)}) collective-permute-start(bf16[384,320]{1,0:T(8,128)(2,1)S(1)} %get-tuple-element.282), channel_id=1, source_target_pairs={{0,3},{1,2},{2,1},{3,0},{4,7},{5,6},{6,5},{7,4},{8,11},{9,10},{10,... | collective-permute-start | bytes 737288 | tf_op jit(solution)/shard_map/ppermute | solution.py:42
  105.8 23.8 %collective-permute-start.9 = (bf16[384,320]{1,0:T(8,128)(2,1)S(1)}, bf16[384,320]{1,0:T(8,128)(2,1)S(1)}, u32[]{:S(2)}, u32[]{:S(2)}) collective-permute-start(bf16[384,320]{1,0:T(8,128)(2,1)S(1)} %get-tuple-element.284), channel_id=1, source_target_pairs={{0,1},{1,0},{2,3},{3,2},{4,5},{5,4},{6,7},{7,6},{8,9},{9,8},{10,11... | collective-permute-start | bytes 737288 | tf_op jit(solution)/shard_map/ppermute | solution.py:42
  110.6 25.9 %collective-permute-start.14 = (bf16[1280,320]{0,1:T(8,128)(2,1)S(1)}, bf16[1280,320]{0,1:T(8,128)(2,1)}, u32[]{:S(2)}, u32[]{:S(2)}) collective-permute-start(bf16[1280,320]{0,1:T(8,128)(2,1)S(1)} %collective-permute-done.13), channel_id=1, source_target_pairs={{0,1},{1,0},{2,3},{3,2},{4,5},{5,4},{6,7},{7,6},{8,9},{9,8},{10,11... | collective-permute-start | bytes 2457608 | tf_op jit(solution)/shard_map/ppermute | solution.py:42
  128.7 21.3 %collective-permute-start.17 = (bf16[384,320]{1,0:T(8,128)(2,1)}, bf16[384,320]{1,0:T(8,128)(2,1)}, u32[]{:S(2)}, u32[]{:S(2)}) collective-permute-start(bf16[384,320]{1,0:T(8,128)(2,1)} %get-tuple-element.280), channel_id=1, source_target_pairs={{0,1},{1,0},{2,3},{3,2},{4,5},{5,4},{6,7},{7,6},{8,9},{9,8},{10,11... | collective-permute-start | bytes 737288 | tf_op jit(solution)/shard_map/ppermute | solution.py:42
  129.0 21.0 %collective-permute-start.18 = (bf16[384,320]{1,0:T(8,128)(2,1)}, bf16[384,320]{1,0:T(8,128)(2,1)}, u32[]{:S(2)}, u32[]{:S(2)}) collective-permute-start(bf16[384,320]{1,0:T(8,128)(2,1)} %get-tuple-element.279), channel_id=1, source_target_pairs={{0,2},{1,3},{2,0},{3,1},{4,6},{5,7},{6,4},{7,5},{8,10},{9,11},{10,... | collective-permute-start | bytes 737288 | tf_op jit(solution)/shard_map/ppermute | solution.py:42
  129.6 20.4 %collective-permute-start.19 = (bf16[384,320]{1,0:T(8,128)(2,1)}, bf16[384,320]{1,0:T(8,128)(2,1)}, u32[]{:S(2)}, u32[]{:S(2)}) collective-permute-start(bf16[384,320]{1,0:T(8,128)(2,1)} %get-tuple-element.278), channel_id=1, source_target_pairs={{0,3},{1,2},{2,1},{3,0},{4,7},{5,6},{6,5},{7,4},{8,11},{9,10},{10,... | collective-permute-start | bytes 737288 | tf_op jit(solution)/shard_map/ppermute | solution.py:42
  148.9 24.6 %collective-permute-start.16 = (bf16[384,1280]{1,0:T(8,128)(2,1)}, bf16[384,1280]{1,0:T(8,128)(2,1)}, u32[]{:S(2)}, u32[]{:S(2)}) collective-permute-start(bf16[384,1280]{1,0:T(8,128)(2,1)} %add_convert_fusion.11.refs_0_), channel_id=1, source_target_pairs={{0,2},{1,3},{2,0},{3,1},{4,6},{5,7},{6,4},{7,5},{8,10},{9,11},{10,... | collective-permute-start | bytes 2949128 | tf_op jit(solution)/shard_map/ppermute | solution.py:42
  185.8 23.8 %collective-permute-start.25 = (bf16[384,1280]{1,0:T(8,128)(2,1)S(1)}, bf16[384,1280]{1,0:T(8,128)(2,1)}, u32[]{:S(2)}, u32[]{:S(2)}) collective-permute-start(bf16[384,1280]{1,0:T(8,128)(2,1)S(1)} %add_convert_fusion.10.refs_4_), channel_id=1, source_target_pairs={{0,2},{1,3},{2,0},{3,1},{4,6},{5,7},{6,4},{7,5},{8,10},{9,11},{10,... | collective-permute-start | bytes 2949128 | tf_op jit(solution)/shard_map/ppermute | solution.py:42
  224.2 17.7 %collective-permute-start.22 = (bf16[384,1280]{1,0:T(8,128)(2,1)}, bf16[384,1280]{1,0:T(8,128)(2,1)S(1)}, u32[]{:S(2)}, u32[]{:S(2)}) collective-permute-start(bf16[384,1280]{1,0:T(8,128)(2,1)} %convolution_convert_fusion.15), channel_id=1, source_target_pairs={{0,1},{1,0},{2,3},{3,2},{4,5},{5,4},{6,7},{7,6},{8,9},{9,8},{10,11... | collective-permute-start | bytes 2949128 | tf_op jit(solution)/shard_map/ppermute | solution.py:42
  224.4 24.6 %collective-permute-start.23 = (bf16[384,1280]{1,0:T(8,128)(2,1)S(1)}, bf16[384,1280]{1,0:T(8,128)(2,1)S(1)}, u32[]{:S(2)}, u32[]{:S(2)}) collective-permute-start(bf16[384,1280]{1,0:T(8,128)(2,1)S(1)} %add_convert_fusion.9), channel_id=1, source_target_pairs={{0,2},{1,3},{2,0},{3,1},{4,6},{5,7},{6,4},{7,5},{8,10},{9,11},{10,... | collective-permute-start | bytes 2949128 | tf_op jit(solution)/shard_map/ppermute | solution.py:42
  238.2 13.8 %collective-permute-start.28 = (bf16[384,1280]{1,0:T(8,128)(2,1)S(1)}, bf16[384,1280]{1,0:T(8,128)(2,1)S(1)}, u32[]{:S(2)}, u32[]{:S(2)}) collective-permute-start(bf16[384,1280]{1,0:T(8,128)(2,1)S(1)} %convolution_convert_fusion.11), channel_id=1, source_target_pairs={{0,1},{1,0},{2,3},{3,2},{4,5},{5,4},{6,7},{7,6},{8,9},{9,8},{10,11... | collective-permute-start | bytes 2949128 | tf_op jit(solution)/shard_map/ppermute | solution.py:42
  238.3 31.8 %collective-permute-start.29 = (bf16[384,1280]{1,0:T(8,128)(2,1)S(1)}, bf16[384,1280]{1,0:T(8,128)(2,1)S(1)}, u32[]{:S(2)}, u32[]{:S(2)}) collective-permute-start(bf16[384,1280]{1,0:T(8,128)(2,1)S(1)} %add_convert_fusion.8), channel_id=1, source_target_pairs={{0,2},{1,3},{2,0},{3,1},{4,6},{5,7},{6,4},{7,5},{8,10},{9,11},{10,... | collective-permute-start | bytes 2949128 | tf_op jit(solution)/shard_map/ppermute | solution.py:42
  250.5 26.7 %collective-permute-start.30 = (bf16[384,1280]{1,0:T(8,128)(2,1)S(1)}, bf16[384,1280]{1,0:T(8,128)(2,1)S(1)}, u32[]{:S(2)}, u32[]{:S(2)}) collective-permute-start(bf16[384,1280]{1,0:T(8,128)(2,1)S(1)} %get-tuple-element.156.refs_8_), channel_id=1, source_target_pairs={{0,1},{1,0},{2,3},{3,2},{4,5},{5,4},{6,7},{7,6},{8,9},{9,8},{10,11... | collective-permute-start | bytes 2949128 | tf_op jit(solution)/shard_map/ppermute | solution.py:42
  250.5 40.0 %collective-permute-start.31 = (bf16[384,1280]{1,0:T(8,128)(2,1)S(1)}, bf16[384,1280]{1,0:T(8,128)(2,1)S(1)}, u32[]{:S(2)}, u32[]{:S(2)}) collective-permute-start(bf16[384,1280]{1,0:T(8,128)(2,1)S(1)} %get-tuple-element.156.refs_8_), channel_id=1, source_target_pairs={{0,2},{1,3},{2,0},{3,1},{4,6},{5,7},{6,4},{7,5},{8,10},{9,11},{10,... | collective-permute-start | bytes 2949128 | tf_op jit(solution)/shard_map/ppermute | solution.py:42
  298.3 24.1 %collective-permute-start.37 = (bf16[384,1280]{1,0:T(8,128)(2,1)S(1)}, bf16[384,1280]{1,0:T(8,128)(2,1)S(1)}, u32[]{:S(2)}, u32[]{:S(2)}) collective-permute-start(bf16[384,1280]{1,0:T(8,128)(2,1)S(1)} %get-tuple-element.165.refs_12_), channel_id=1, source_target_pairs={{0,2},{1,3},{2,0},{3,1},{4,6},{5,7},{6,4},{7,5},{8,10},{9,11},{10,... | collective-permute-start | bytes 2949128 | tf_op jit(solution)/shard_map/ppermute | solution.py:42
  332.8 34.1 %collective-permute-start.34 = (bf16[384,1280]{1,0:T(8,128)(2,1)}, bf16[384,1280]{1,0:T(8,128)(2,1)}, u32[]{:S(2)}, u32[]{:S(2)}) collective-permute-start(bf16[384,1280]{1,0:T(8,128)(2,1)} %convolution_convert_fusion.7), channel_id=1, source_target_pairs={{0,1},{1,0},{2,3},{3,2},{4,5},{5,4},{6,7},{7,6},{8,9},{9,8},{10,11... | collective-permute-start | bytes 2949128 | tf_op jit(solution)/shard_map/ppermute | solution.py:42
  332.8 34.1 %collective-permute-start.35 = (bf16[384,1280]{1,0:T(8,128)(2,1)}, bf16[384,1280]{1,0:T(8,128)(2,1)}, u32[]{:S(2)}, u32[]{:S(2)}) collective-permute-start(bf16[384,1280]{1,0:T(8,128)(2,1)} %add_convert_fusion.7), channel_id=1, source_target_pairs={{0,2},{1,3},{2,0},{3,1},{4,6},{5,7},{6,4},{7,5},{8,10},{9,11},{10,... | collective-permute-start | bytes 2949128 | tf_op jit(solution)/shard_map/ppermute | solution.py:42
  343.9 55.3 %collective-permute-start.43 = (bf16[384,1280]{1,0:T(8,128)(2,1)}, bf16[384,1280]{1,0:T(8,128)(2,1)S(1)}, u32[]{:S(2)}, u32[]{:S(2)}) collective-permute-start(bf16[384,1280]{1,0:T(8,128)(2,1)} %convolution_convert_fusion.3), channel_id=1, source_target_pairs={{0,1},{1,0},{2,3},{3,2},{4,5},{5,4},{6,7},{7,6},{8,9},{9,8},{10,11... | collective-permute-start | bytes 2949128 | tf_op jit(solution)/shard_map/ppermute | solution.py:42
  344.1 55.1 %collective-permute-start.44 = (bf16[384,1280]{1,0:T(8,128)(2,1)}, bf16[384,1280]{1,0:T(8,128)(2,1)}, u32[]{:S(2)}, u32[]{:S(2)}) collective-permute-start(bf16[384,1280]{1,0:T(8,128)(2,1)} %add_convert_fusion.6), channel_id=1, source_target_pairs={{0,2},{1,3},{2,0},{3,1},{4,6},{5,7},{6,4},{7,5},{8,10},{9,11},{10,... | collective-permute-start | bytes 2949128 | tf_op jit(solution)/shard_map/ppermute | solution.py:42
  377.3 32.2 %collective-permute-start.40 = (bf16[384,320]{1,0:T(8,128)(2,1)}, bf16[384,320]{1,0:T(8,128)(2,1)}, u32[]{:S(2)}, u32[]{:S(2)}) collective-permute-start(bf16[384,320]{1,0:T(8,128)(2,1)} %get-tuple-element.293), channel_id=1, source_target_pairs={{0,1},{1,0},{2,3},{3,2},{4,5},{5,4},{6,7},{7,6},{8,9},{9,8},{10,11... | collective-permute-start | bytes 737288 | tf_op jit(solution)/shard_map/ppermute | solution.py:42
  377.4 32.2 %collective-permute-start.41 = (bf16[384,320]{1,0:T(8,128)(2,1)}, bf16[384,320]{1,0:T(8,128)(2,1)}, u32[]{:S(2)}, u32[]{:S(2)}) collective-permute-start(bf16[384,320]{1,0:T(8,128)(2,1)} %get-tuple-element.292), channel_id=1, source_target_pairs={{0,2},{1,3},{2,0},{3,1},{4,6},{5,7},{6,4},{7,5},{8,10},{9,11},{10,... | collective-permute-start | bytes 737288 | tf_op jit(solution)/shard_map/ppermute | solution.py:42
  378.9 30.7 %collective-permute-start.42 = (bf16[384,320]{1,0:T(8,128)(2,1)}, bf16[384,320]{1,0:T(8,128)(2,1)}, u32[]{:S(2)}, u32[]{:S(2)}) collective-permute-start(bf16[384,320]{1,0:T(8,128)(2,1)} %get-tuple-element.291), channel_id=1, source_target_pairs={{0,3},{1,2},{2,1},{3,0},{4,7},{5,6},{6,5},{7,4},{8,11},{9,10},{10,... | collective-permute-start | bytes 737288 | tf_op jit(solution)/shard_map/ppermute | solution.py:42
  399.1 217.3 %reduce-scatter.5.cloned.1.call-start = ((), (), s32[]{:S(2)}) async-start(), calls=%async_computation.5 | async-start | bytes 3686400 | tf_op jit(solution)/shard_map/reduce_scatter | solution.py:562
  425.8 41.0 %collective-permute-start.45 = (bf16[384,320]{1,0:T(8,128)(2,1)S(1)}, bf16[384,320]{1,0:T(8,128)(2,1)}, u32[]{:S(2)}, u32[]{:S(2)}) collective-permute-start(bf16[384,320]{1,0:T(8,128)(2,1)S(1)} %copy-done.63), channel_id=1, source_target_pairs={{0,1},{1,0},{2,3},{3,2},{4,5},{5,4},{6,7},{7,6},{8,9},{9,8},{10,11... | collective-permute-start | bytes 737288 | tf_op jit(solution)/shard_map/ppermute | solution.py:42
  426.0 40.8 %collective-permute-start.46 = (bf16[384,320]{1,0:T(8,128)(2,1)S(1)}, bf16[384,320]{1,0:T(8,128)(2,1)}, u32[]{:S(2)}, u32[]{:S(2)}) collective-permute-start(bf16[384,320]{1,0:T(8,128)(2,1)S(1)} %copy-done.62), channel_id=1, source_target_pairs={{0,2},{1,3},{2,0},{3,1},{4,6},{5,7},{6,4},{7,5},{8,10},{9,11},{10,... | collective-permute-start | bytes 737288 | tf_op jit(solution)/shard_map/ppermute | solution.py:42
  427.4 39.4 %collective-permute-start.47 = (bf16[384,320]{1,0:T(8,128)(2,1)S(1)}, bf16[384,320]{1,0:T(8,128)(2,1)}, u32[]{:S(2)}, u32[]{:S(2)}) collective-permute-start(bf16[384,320]{1,0:T(8,128)(2,1)S(1)} %get-tuple-element.286), channel_id=1, source_target_pairs={{0,3},{1,2},{2,1},{3,0},{4,7},{5,6},{6,5},{7,4},{8,11},{9,10},{10,... | collective-permute-start | bytes 737288 | tf_op jit(solution)/shard_map/ppermute | solution.py:42
  427.7 37.7 %collective-permute-start.48 = (bf16[1280,384]{1,0:T(8,128)(2,1)}, bf16[1280,384]{1,0:T(8,128)(2,1)S(1)}, u32[]{:S(2)}, u32[]{:S(2)}) collective-permute-start(bf16[1280,384]{1,0:T(8,128)(2,1)} %get-tuple-element.187), channel_id=1, source_target_pairs={{0,1},{1,0},{2,3},{3,2},{4,5},{5,4},{6,7},{7,6},{8,9},{9,8},{10,11... | collective-permute-start | bytes 2949128 | tf_op jit(solution)/shard_map/ppermute | solution.py:42
  430.7 34.7 %collective-permute-start.50 = (bf16[1280,384]{1,0:T(8,128)(2,1)S(1)}, bf16[1280,384]{1,0:T(8,128)(2,1)S(1)}, u32[]{:S(2)}, u32[]{:S(2)}) collective-permute-start(bf16[1280,384]{1,0:T(8,128)(2,1)S(1)} %add_convert_fusion.5), channel_id=1, source_target_pairs={{0,2},{1,3},{2,0},{3,1},{4,6},{5,7},{6,4},{7,5},{8,10},{9,11},{10,... | collective-permute-start | bytes 2949128 | tf_op jit(solution)/shard_map/ppermute | solution.py:42
  534.6 32.0 %collective-permute-start.54 = (bf16[384,1280]{1,0:T(8,128)(2,1)}, bf16[384,1280]{1,0:T(8,128)(2,1)}, u32[]{:S(2)}, u32[]{:S(2)}) collective-permute-start(bf16[384,1280]{1,0:T(8,128)(2,1)} %get-tuple-element.204), channel_id=1, source_target_pairs={{0,1},{1,0},{2,3},{3,2},{4,5},{5,4},{6,7},{7,6},{8,9},{9,8},{10,11... | collective-permute-start | bytes 2949128 | tf_op jit(solution)/shard_map/ppermute | solution.py:42
  537.5 24.8 %collective-permute-start.53 = (bf16[384,1280]{1,0:T(8,128)(2,1)}, bf16[384,1280]{1,0:T(8,128)(2,1)S(1)}, u32[]{:S(2)}, u32[]{:S(2)}) collective-permute-start(bf16[384,1280]{1,0:T(8,128)(2,1)} %add_convert_fusion.3), channel_id=1, source_target_pairs={{0,2},{1,3},{2,0},{3,1},{4,6},{5,7},{6,4},{7,5},{8,10},{9,11},{10,... | collective-permute-start | bytes 2949128 | tf_op jit(solution)/shard_map/ppermute | solution.py:42
  542.7 39.8 %collective-permute-start.56 = (bf16[384,1280]{1,0:T(8,128)(2,1)S(1)}, bf16[384,1280]{1,0:T(8,128)(2,1)S(1)}, u32[]{:S(2)}, u32[]{:S(2)}) collective-permute-start(bf16[384,1280]{1,0:T(8,128)(2,1)S(1)} %add_convert_fusion.2), channel_id=1, source_target_pairs={{0,2},{1,3},{2,0},{3,1},{4,6},{5,7},{6,4},{7,5},{8,10},{9,11},{10,... | collective-permute-start | bytes 2949128 | tf_op jit(solution)/shard_map/ppermute | solution.py:42
  597.9 19.1 %collective-permute-start.69 = (bf16[160,1280]{1,0:T(8,128)(2,1)}, bf16[160,1280]{1,0:T(8,128)(2,1)}, u32[]{:S(2)}, u32[]{:S(2)}) collective-permute-start(bf16[160,1280]{1,0:T(8,128)(2,1)} %get-tuple-element.221.refs_0_), channel_id=1, source_target_pairs={{0,2},{1,3},{2,0},{3,1},{4,6},{5,7},{6,4},{7,5},{8,10},{9,11},{10,... | collective-permute-start | bytes 1228808 | tf_op jit(solution)/shard_map/ppermute | solution.py:42
  598.3 19.1 %collective-permute-start.66 = (bf16[160,1280]{1,0:T(8,128)(2,1)S(1)}, bf16[160,1280]{1,0:T(8,128)(2,1)}, u32[]{:S(2)}, u32[]{:S(2)}) collective-permute-start(bf16[160,1280]{1,0:T(8,128)(2,1)S(1)} %get-tuple-element.216.refs_0_), channel_id=1, source_target_pairs={{0,2},{1,3},{2,0},{3,1},{4,6},{5,7},{6,4},{7,5},{8,10},{9,11},{10,... | collective-permute-start | bytes 1228808 | tf_op jit(solution)/shard_map/ppermute | solution.py:42
  616.9 13.4 %collective-permute-start.65 = (bf16[160,1280]{1,0:T(8,128)(2,1)S(1)}, bf16[160,1280]{1,0:T(8,128)(2,1)S(1)}, u32[]{:S(2)}, u32[]{:S(2)}) collective-permute-start(bf16[160,1280]{1,0:T(8,128)(2,1)S(1)} %get-tuple-element.216.refs_0_), channel_id=1, source_target_pairs={{0,1},{1,0},{2,3},{3,2},{4,5},{5,4},{6,7},{7,6},{8,9},{9,8},{10,11... | collective-permute-start | bytes 1228808 | tf_op jit(solution)/shard_map/ppermute | solution.py:42
  617.4 14.4 %collective-permute-start.67 = (bf16[160,1280]{1,0:T(8,128)(2,1)}, bf16[160,1280]{1,0:T(8,128)(2,1)}, u32[]{:S(2)}, u32[]{:S(2)}) collective-permute-start(bf16[160,1280]{1,0:T(8,128)(2,1)} %collective-permute-done.66.refs_2_), channel_id=1, source_target_pairs={{0,1},{1,0},{2,3},{3,2},{4,5},{5,4},{6,7},{7,6},{8,9},{9,8},{10,11... | collective-permute-start | bytes 1228808 | tf_op jit(solution)/shard_map/ppermute | solution.py:42
  620.2 22.3 %collective-permute-start.62 = (bf16[160,1280]{1,0:T(8,128)(2,1)}, bf16[160,1280]{1,0:T(8,128)(2,1)S(1)}, u32[]{:S(2)}, u32[]{:S(2)}) collective-permute-start(bf16[160,1280]{1,0:T(8,128)(2,1)} %reduce-scatter.5.cloned.1.call-done.refs_0_), channel_id=1, source_target_pairs={{0,1},{1,0},{2,3},{3,2},{4,5},{5,4},{6,7},{7,6},{8,9},{9,8},{10,11... | collective-permute-start | bytes 1228808 | tf_op jit(solution)/shard_map/ppermute | solution.py:42
  628.5 14.0 %collective-permute-start.64 = (bf16[160,1280]{1,0:T(8,128)(2,1)}, bf16[160,1280]{1,0:T(8,128)(2,1)S(1)}, u32[]{:S(2)}, u32[]{:S(2)}) collective-permute-start(bf16[160,1280]{1,0:T(8,128)(2,1)} %collective-permute-done.63.refs_2_), channel_id=1, source_target_pairs={{0,1},{1,0},{2,3},{3,2},{4,5},{5,4},{6,7},{7,6},{8,9},{9,8},{10,11... | collective-permute-start | bytes 1228808 | tf_op jit(solution)/shard_map/ppermute | solution.py:42
  (159 other events, 1292.0 us)
Sparse Core Ops, SparseCore 0:
  10.8 64.3 all-gather.2
  77.3 100.5 all-gather.4
  399.2 119.9 reduce-scatter.2
  540.0 74.8 reduce-scatter.4
